TPU v7x, 32 devices: a whole 2x2x4 slice. The times are simulated.
32 devices in a mesh: shard: 8 (over z, x), rep: 4 (over y, core).
Axes of the slice: x: 2, y: 2, z: 4, core: 2. Of those that a mesh axis runs over, the one named last changes fastest.
Arguments:
- hidden_in: bfloat16 [16384, 2048], P(('shard', 'rep')), may hold values from -6 to 6
- doc_ids: int32 [32, 512], P(('shard', 'rep')), may hold values from 0 to 3, never falling along the last dimension, each value on 1 to 256 neighbouring positions
- expert_ids: int32 [16384, 8], P(('shard', 'rep')), may hold values from 0 to 63, as said below
- slot_rows: int32 [32, 2, 128], P(('shard', 'rep')), may hold values from 0 to 512, as said below
- out_grad: bfloat16 [16384, 2048], P(('shard', 'rep')), may hold values from -6 to 6
- attn_gain: bfloat16 [2048], P('shard'), may hold values from 0.5 to 1.5
- w_query: bfloat16 [2048, 2048], P('shard'), may hold values from -0.125 to 0.125
- w_key: bfloat16 [2048, 2048], P('shard'), may hold values from -0.125 to 0.125
- w_value: bfloat16 [2048, 2048], P('shard'), may hold values from -0.125 to 0.125
- query_gain: bfloat16 [2048], P('shard'), may hold values from 0.5 to 1.5
- key_gain: bfloat16 [2048], P('shard'), may hold values from 0.5 to 1.5
- w_output: bfloat16 [2048, 2048], P('shard'), may hold values from -0.75 to 0.75
- ffn_gain: bfloat16 [2048], P('shard'), may hold values from 0.5 to 1.5
- w_router: bfloat16 [2048, 64], P('shard'), may hold values from -0.0625 to 0.0625
- w_gate: bfloat16 [2, 2048, 1024], P(None, 'shard'), may hold values from -0.125 to 0.125
- w_up: bfloat16 [2, 2048, 1024], P(None, 'shard'), may hold values from -0.125 to 0.125
- w_down: bfloat16 [2, 1024, 2048], P(None, 'shard'), may hold values from -24 to 24
Outputs:
- hidden_out: bfloat16 [16384, 2048], P(('shard', 'rep'))
- input_grad: float32 [16384, 2048], P(('shard', 'rep'))
- attn_gain_grad: float32 [2048], P('shard')
- w_query_grad: float32 [2048, 2048], P('shard')
- w_key_grad: float32 [2048, 2048], P('shard')
- w_value_grad: float32 [2048, 2048], P('shard')
- query_gain_grad: float32 [2048], P('shard')
- key_gain_grad: float32 [2048], P('shard')
- w_output_grad: float32 [2048, 2048], P('shard')
- ffn_gain_grad: float32 [2048], P('shard')
- w_router_grad: float32 [2048, 64], P('shard')
- w_gate_grad: float32 [2, 2048, 1024], P(None, 'shard')
- w_up_grad: float32 [2, 2048, 1024], P(None, 'shard')
- w_down_grad: float32 [2, 1024, 2048], P(None, 'shard')
Inputs may be any that keep to these rules, and one draw needn't show every extreme that they name: `expert_ids`: each row names 8 different experts. `slot_rows`: for each sequence and each expert e below 2: the entries, without repeats, are the places in the sequence of exactly the tokens whose row of expert_ids names e, in any order, followed by the filler 512; 64 or more are live, and in each sequence some expert fills all 128 slots. `doc_ids`: document numbers never fall along a sequence; a document has at most 256 tokens.
All inputs are finite; a program needn't handle non-finite values.
Results may differ from a plain program's by a relative error of at most 0.02.
Values may be sent and summed in bfloat16 or wider, within the bound.
No kernel may reach another device: no remote copies, remote signals or barrier semaphores. Data moves between devices by JAX's collectives and lax.ppermute only.
A program may use at most 320 MiB of HBM per device.

v0:
```python
import jax
import jax.numpy as jnp
from jax import lax
from jax.sharding import PartitionSpec as P

HEADS = 16


EPSILON = 1e-05
THETA = 10000.0


def rms_scale(values):
    return lax.rsqrt(jnp.mean(values * values, -1, keepdims=True) + EPSILON)


def norm_back(values, scale, gain, upstream):
    gain_grad = jnp.sum(upstream * values * scale, 0)
    weighted = upstream * gain
    inner_mean = jnp.mean(weighted * values, -1, keepdims=True)
    return (scale * weighted - values * scale * scale * scale * inner_mean, gain_grad)


def doc_places(docs):
    places = jnp.arange(docs.shape[0], dtype=jnp.int32)
    earlier = jnp.concatenate([docs[:1], docs[:-1]], 0)
    starts = lax.cummax(jnp.where(docs != earlier, places, jnp.zeros_like(places)), axis=0)
    return (places - starts).astype(jnp.float32)


def rope_tables(positions, head_dim):
    half = head_dim // 2
    inverse_rates = THETA ** (-jnp.arange(half, dtype=jnp.float32) * 2.0 / head_dim)
    angles = positions[:, None] * inverse_rates[None, :]
    cosine = jnp.concatenate([jnp.cos(angles), jnp.cos(angles)], -1)[:, None, :]
    sine = jnp.concatenate([jnp.sin(angles), jnp.sin(angles)], -1)[:, None, :]
    return (cosine, sine)


def rotate(values, cosine, sine):
    half = values.shape[-1] // 2
    turned = jnp.concatenate([-values[..., half:], values[..., :half]], -1)
    return values * cosine + turned * sine


def rotate_back(upstream, cosine, sine):
    half = upstream.shape[-1] // 2
    moved = upstream * sine
    return upstream * cosine + jnp.concatenate([moved[..., half:], -moved[..., :half]], -1)


def local(
    hidden_in,
    doc_ids,
    expert_ids,
    slot_rows,
    out_grad,
    attn_gain,
    w_query,
    w_key,
    w_value,
    query_gain,
    key_gain,
    w_output,
    ffn_gain,
    w_router,
    w_gate,
    w_up,
    w_down,
):
    length, width = hidden_in.shape
    head_dim = width // HEADS
    routed = w_router.shape[1]
    experts = w_gate.shape[0]
    block = min(length, 512)
    count = length // block
    factor = head_dim ** (-0.5)
    gathered = (
        lax.all_gather(attn_gain, "shard", axis=0, tiled=True),
        lax.all_gather(w_query, "shard", axis=0, tiled=True),
        lax.all_gather(w_key, "shard", axis=0, tiled=True),
        lax.all_gather(w_value, "shard", axis=0, tiled=True),
        lax.all_gather(query_gain, "shard", axis=0, tiled=True),
        lax.all_gather(key_gain, "shard", axis=0, tiled=True),
        lax.all_gather(w_output, "shard", axis=0, tiled=True),
        lax.all_gather(ffn_gain, "shard", axis=0, tiled=True),
        lax.all_gather(w_router, "shard", axis=0, tiled=True),
    )
    query_w, key_w, value_w, output_w, router_w = (
        gathered[1],
        gathered[2],
        gathered[3],
        gathered[6],
        gathered[8],
    )
    gain_one = gathered[0].astype(jnp.float32)
    gain_query = gathered[4].astype(jnp.float32)
    gain_key = gathered[5].astype(jnp.float32)
    gain_two = gathered[7].astype(jnp.float32)
    hidden = hidden_in.astype(jnp.float32)
    scale_one = rms_scale(hidden)
    normed = (hidden * scale_one * gain_one).astype(jnp.bfloat16)
    query_raw = jnp.dot(normed, query_w, preferred_element_type=jnp.float32)
    key_raw = jnp.dot(normed, key_w, preferred_element_type=jnp.float32)
    values = (
        jnp.dot(normed, value_w, preferred_element_type=jnp.float32)
        .astype(jnp.bfloat16)
        .reshape(length, HEADS, head_dim)
    )
    docs = doc_ids[0]
    cosine, sine = rope_tables(doc_places(docs), head_dim)
    query_scale = rms_scale(query_raw)
    key_scale = rms_scale(key_raw)
    queries = rotate(
        (query_raw * query_scale * gain_query).reshape(length, HEADS, head_dim), cosine, sine
    ).astype(jnp.bfloat16)
    keys = rotate(
        (key_raw * key_scale * gain_key).reshape(length, HEADS, head_dim), cosine, sine
    ).astype(jnp.bfloat16)
    places = jnp.arange(length)
    allowed = (docs[:, None] == docs[None, :]) & (places[None, :] <= places[:, None])

    def attend_block(index):
        scores = (
            jnp.einsum("ihd,jhd->hij", queries, keys, preferred_element_type=jnp.float32) * factor
        )
        scores = jnp.where(allowed[None], scores, -jnp.inf)
        highest = jnp.max(scores, -1, keepdims=True)
        weights = jnp.exp(scores - highest)
        total = jnp.sum(weights, -1, keepdims=True)
        probs = (weights / total).astype(jnp.bfloat16)
        mixed_part = jnp.einsum("hij,jhd->ihd", probs, values, preferred_element_type=jnp.float32)
        return (mixed_part.astype(jnp.bfloat16), highest + jnp.log(total))

    mixed, log_total = lax.map(attend_block, jnp.arange(count))
    mixed = mixed.reshape(length, width)
    residual = hidden + jnp.dot(mixed, output_w, preferred_element_type=jnp.float32)
    scale_two = rms_scale(residual)
    inner = (residual * scale_two * gain_two).astype(jnp.bfloat16)
    logits = jnp.dot(inner, router_w, preferred_element_type=jnp.float32)
    onehot = (expert_ids[:, :, None] == jnp.arange(routed, dtype=jnp.int32)[None, None, :]).astype(
        jnp.float32
    )
    probs_all = jax.nn.softmax(logits, axis=-1)
    gates = jnp.sum(onehot * probs_all[:, None, :], -1)
    window = jnp.sum(gates[:, :, None] * onehot[:, :, :experts], 1)
    slots = slot_rows[0]
    expert_column = jnp.arange(experts)[:, None]
    inner_pad = jnp.concatenate([inner, jnp.zeros((1, width), jnp.bfloat16)], 0)
    window_pad = jnp.concatenate([window, jnp.zeros((1, experts), jnp.float32)], 0)
    slot_inputs = inner_pad[slots]
    slot_gates = window_pad[slots, expert_column]
    gate_full, up_full, down_full = (
        lax.all_gather(w_gate, "shard", axis=1, tiled=True),
        lax.all_gather(w_up, "shard", axis=1, tiled=True),
        lax.all_gather(w_down, "shard", axis=1, tiled=True),
    )
    gate_part = jnp.einsum(
        "ecd,edf->ecf", slot_inputs, gate_full, preferred_element_type=jnp.float32
    )
    up_part = jnp.einsum("ecd,edf->ecf", slot_inputs, up_full, preferred_element_type=jnp.float32)
    sigma = jax.nn.sigmoid(gate_part)
    swished = gate_part * sigma
    activated = (swished * up_part).astype(jnp.bfloat16)
    returned = jnp.einsum("ecf,efd->ecd", activated, down_full, preferred_element_type=jnp.float32)
    experts_sum = (
        jnp.zeros((length + 1, width), jnp.float32).at[slots].add(slot_gates[:, :, None] * returned)
    )
    output = (residual + experts_sum[:length]).astype(jnp.bfloat16)
    upstream = out_grad.astype(jnp.float32)
    upstream_pad = jnp.concatenate([upstream, jnp.zeros((1, width), jnp.float32)], 0)
    slot_upstream = upstream_pad[slots]
    returned_grad = (slot_gates[:, :, None] * slot_upstream).astype(jnp.bfloat16)
    slot_gate_grad = jnp.sum(returned * slot_upstream, -1)
    gate_back, up_back, down_back = (
        lax.all_gather(w_gate, "shard", axis=1, tiled=True),
        lax.all_gather(w_up, "shard", axis=1, tiled=True),
        lax.all_gather(w_down, "shard", axis=1, tiled=True),
    )
    down_w_grad = jnp.einsum(
        "ecf,ecd->efd", activated, returned_grad, preferred_element_type=jnp.float32
    )
    act_grad = jnp.einsum(
        "ecd,efd->ecf", returned_grad, down_back, preferred_element_type=jnp.float32
    )
    gate_grad = (act_grad * up_part * sigma * (1.0 + gate_part * (1.0 - sigma))).astype(
        jnp.bfloat16
    )
    up_grad = (act_grad * swished).astype(jnp.bfloat16)
    gate_w_grad = jnp.einsum(
        "ecd,ecf->edf", slot_inputs, gate_grad, preferred_element_type=jnp.float32
    )
    up_w_grad = jnp.einsum("ecd,ecf->edf", slot_inputs, up_grad, preferred_element_type=jnp.float32)
    expert_owned = (
        lax.psum_scatter(
            gate_w_grad.astype(jnp.bfloat16), "shard", scatter_dimension=1, tiled=True
        ).astype(jnp.float32),
        lax.psum_scatter(
            up_w_grad.astype(jnp.bfloat16), "shard", scatter_dimension=1, tiled=True
        ).astype(jnp.float32),
        lax.psum_scatter(
            down_w_grad.astype(jnp.bfloat16), "shard", scatter_dimension=1, tiled=True
        ).astype(jnp.float32),
    )
    slot_input_grad = jnp.einsum(
        "ecf,edf->ecd", gate_grad, gate_back, preferred_element_type=jnp.float32
    )
    slot_input_grad = slot_input_grad + jnp.einsum(
        "ecf,edf->ecd", up_grad, up_back, preferred_element_type=jnp.float32
    )
    inner_grad = jnp.zeros((length + 1, width), jnp.float32).at[slots].add(slot_input_grad)[:length]
    window_grad = (
        jnp.zeros((length + 1, experts), jnp.float32)
        .at[slots, expert_column]
        .add(slot_gate_grad)[:length]
    )
    gates_grad = jnp.sum(window_grad[:, None, :] * onehot[:, :, :experts], -1)
    chosen_grad = jnp.sum(gates_grad[:, :, None] * onehot, 1)
    logits_grad = (
        probs_all * (chosen_grad - jnp.sum(probs_all * chosen_grad, -1, keepdims=True))
    ).astype(jnp.bfloat16)
    regathered = (
        lax.all_gather(w_query, "shard", axis=0, tiled=True),
        lax.all_gather(w_key, "shard", axis=0, tiled=True),
        lax.all_gather(w_value, "shard", axis=0, tiled=True),
        lax.all_gather(w_output, "shard", axis=0, tiled=True),
        lax.all_gather(w_router, "shard", axis=0, tiled=True),
    )
    query_b, key_b, value_b, output_b, router_b = regathered
    router_grad = jnp.einsum("td,tr->dr", inner, logits_grad, preferred_element_type=jnp.float32)
    inner_grad = inner_grad + jnp.einsum(
        "tr,dr->td", logits_grad, router_b, preferred_element_type=jnp.float32
    )
    residual_part, gain_two_grad = norm_back(residual, scale_two, gain_two, inner_grad)
    residual_grad = upstream + residual_part
    branch_grad = residual_grad.astype(jnp.bfloat16)
    output_w_grad = jnp.einsum("ti,td->id", mixed, branch_grad, preferred_element_type=jnp.float32)
    mixed_grad = jnp.einsum(
        "td,id->ti", branch_grad, output_b, preferred_element_type=jnp.float32
    ).astype(jnp.bfloat16)
    mixed_grad = mixed_grad.reshape(length, HEADS, head_dim)

    def attend_back(carry, index):
        key_sum, value_sum = carry
        scores = (
            jnp.einsum("ihd,jhd->hij", queries, keys, preferred_element_type=jnp.float32) * factor
        )
        scores = jnp.where(allowed[None], scores, -jnp.inf)
        probs = jnp.exp(scores - log_total[index])
        value_sum = value_sum + jnp.einsum(
            "hij,ihd->jhd",
            probs.astype(jnp.bfloat16),
            mixed_grad,
            preferred_element_type=jnp.float32,
        )
        prob_grad = jnp.einsum(
            "ihd,jhd->hij", mixed_grad, values, preferred_element_type=jnp.float32
        )
        score_grad = (probs * (prob_grad - jnp.sum(probs * prob_grad, -1, keepdims=True))).astype(
            jnp.bfloat16
        )
        key_sum = (
            key_sum
            + jnp.einsum("hij,ihd->jhd", score_grad, queries, preferred_element_type=jnp.float32)
            * factor
        )
        query_part_grad = (
            jnp.einsum("hij,jhd->ihd", score_grad, keys, preferred_element_type=jnp.float32)
            * factor
        )
        return ((key_sum, value_sum), query_part_grad)

    empty = jnp.zeros((length, HEADS, head_dim), jnp.float32)
    sums, query_grad = lax.scan(attend_back, (empty, empty), jnp.arange(count))
    key_grad, value_grad = sums
    query_grad = rotate_back(query_grad.reshape(length, HEADS, head_dim), cosine, sine).reshape(
        length, width
    )
    key_grad = rotate_back(key_grad, cosine, sine).reshape(length, width)
    value_grad = value_grad.reshape(length, width).astype(jnp.bfloat16)
    query_raw_grad, gain_query_grad = norm_back(query_raw, query_scale, gain_query, query_grad)
    key_raw_grad, gain_key_grad = norm_back(key_raw, key_scale, gain_key, key_grad)
    query_raw_grad = query_raw_grad.astype(jnp.bfloat16)
    key_raw_grad = key_raw_grad.astype(jnp.bfloat16)
    query_w_grad = jnp.einsum(
        "td,te->de", normed, query_raw_grad, preferred_element_type=jnp.float32
    )
    key_w_grad = jnp.einsum("td,te->de", normed, key_raw_grad, preferred_element_type=jnp.float32)
    value_w_grad = jnp.einsum("td,te->de", normed, value_grad, preferred_element_type=jnp.float32)
    normed_grad = jnp.einsum(
        "te,de->td", query_raw_grad, query_b, preferred_element_type=jnp.float32
    )
    normed_grad = normed_grad + jnp.einsum(
        "te,de->td", key_raw_grad, key_b, preferred_element_type=jnp.float32
    )
    normed_grad = normed_grad + jnp.einsum(
        "te,de->td", value_grad, value_b, preferred_element_type=jnp.float32
    )
    hidden_part, gain_one_grad = norm_back(hidden, scale_one, gain_one, normed_grad)
    input_grad = residual_grad + hidden_part
    attn_owned = (
        lax.psum_scatter(
            gain_one_grad.astype(jnp.bfloat16), "shard", scatter_dimension=0, tiled=True
        ).astype(jnp.float32),
        lax.psum_scatter(
            query_w_grad.astype(jnp.bfloat16), "shard", scatter_dimension=0, tiled=True
        ).astype(jnp.float32),
        lax.psum_scatter(
            key_w_grad.astype(jnp.bfloat16), "shard", scatter_dimension=0, tiled=True
        ).astype(jnp.float32),
        lax.psum_scatter(
            value_w_grad.astype(jnp.bfloat16), "shard", scatter_dimension=0, tiled=True
        ).astype(jnp.float32),
        lax.psum_scatter(
            gain_query_grad.astype(jnp.bfloat16), "shard", scatter_dimension=0, tiled=True
        ).astype(jnp.float32),
        lax.psum_scatter(
            gain_key_grad.astype(jnp.bfloat16), "shard", scatter_dimension=0, tiled=True
        ).astype(jnp.float32),
        lax.psum_scatter(
            output_w_grad.astype(jnp.bfloat16), "shard", scatter_dimension=0, tiled=True
        ).astype(jnp.float32),
        lax.psum_scatter(
            gain_two_grad.astype(jnp.bfloat16), "shard", scatter_dimension=0, tiled=True
        ).astype(jnp.float32),
        lax.psum_scatter(
            router_grad.astype(jnp.bfloat16), "shard", scatter_dimension=0, tiled=True
        ).astype(jnp.float32),
    )
    owned = attn_owned + expert_owned
    owned = (
        lax.psum(owned[0].astype(jnp.bfloat16), "rep").astype(jnp.float32),
        lax.psum(owned[1].astype(jnp.bfloat16), "rep").astype(jnp.float32),
        lax.psum(owned[2].astype(jnp.bfloat16), "rep").astype(jnp.float32),
        lax.psum(owned[3].astype(jnp.bfloat16), "rep").astype(jnp.float32),
        lax.psum(owned[4].astype(jnp.bfloat16), "rep").astype(jnp.float32),
        lax.psum(owned[5].astype(jnp.bfloat16), "rep").astype(jnp.float32),
        lax.psum(owned[6].astype(jnp.bfloat16), "rep").astype(jnp.float32),
        lax.psum(owned[7].astype(jnp.bfloat16), "rep").astype(jnp.float32),
        lax.psum(owned[8].astype(jnp.bfloat16), "rep").astype(jnp.float32),
        lax.psum(owned[9].astype(jnp.bfloat16), "rep").astype(jnp.float32),
        lax.psum(owned[10].astype(jnp.bfloat16), "rep").astype(jnp.float32),
        lax.psum(owned[11].astype(jnp.bfloat16), "rep").astype(jnp.float32),
    )
    return (
        output,
        input_grad,
        owned[0],
        owned[1],
        owned[2],
        owned[3],
        owned[4],
        owned[5],
        owned[6],
        owned[7],
        owned[8],
        owned[9],
        owned[10],
        owned[11],
    )


def solution(mesh):
    return jax.shard_map(
        local,
        mesh=mesh,
        in_specs=(
            P(("shard", "rep"), None),
            P(("shard", "rep"), None),
            P(("shard", "rep"), None),
            P(("shard", "rep"), None, None),
            P(("shard", "rep"), None),
            P("shard"),
            P("shard", None),
            P("shard", None),
            P("shard", None),
            P("shard"),
            P("shard"),
            P("shard", None),
            P("shard"),
            P("shard", None),
            P(None, "shard", None),
            P(None, "shard", None),
            P(None, "shard", None),
        ),
        out_specs=(
            P(("shard", "rep"), None),
            P(("shard", "rep"), None),
            P("shard"),
            P("shard", None),
            P("shard", None),
            P("shard", None),
            P("shard"),
            P("shard"),
            P("shard", None),
            P("shard"),
            P("shard", None),
            P(None, "shard", None),
            P(None, "shard", None),
            P(None, "shard", None),
        ),
        check_vma=False,
    )
```

profile of v0, /device:TPU:0, one launch (start us, length us, event | category | flops | bytes accessed | tf_op | source)
XLA Modules:
  0.0 2191.9 jit_solution(15768521721953528877)
XLA Ops:
  16.7 23.2 %all-gather.3 = bf16[8,1,256]{2,1,0:T(2,128)(2,1)S(1)} all-gather(bf16[1,1,256]{2,1,0:T(2,128)(2,1)S(1)} %reshape.303), channel_id=1, replica_groups=mesh['shard'=8,'rep'=4] {'shard'}, dimensions={0}, use_global_device_ids=true | all-gather | bytes 4608 | tf_op jit(solution)/shard_map/all_gather | solution.py:86
  39.9 17.2 all-gather.2
  57.1 18.7 all-gather.1
  75.8 17.2 all-gather
  93.0 32.6 %all_gather.52 = bf16[2048,64]{0,1:T(8,128)(2,1)S(1)} all-gather(bf16[256,64]{0,1:T(8,128)(2,1)S(1)} %copy-done.52), channel_id=1, replica_groups=mesh['shard'=8,'rep'=4] {'shard'}, dimensions={0}, use_global_device_ids=true | all-gather | bytes 294912 | tf_op jit(solution)/shard_map/all_gather | solution.py:87
  159.1 107.8 %all-gather.16.cloned.1.call-done = bf16[2048,2048]{1,0:T(8,128)(2,1)} async-done(((bf16[256,2048]{1,0:T(8,128)(2,1)}), bf16[2048,2048]{1,0:T(8,128)(2,1)}) %all-gather.16.cloned.1.call-update) | async-done | bytes 8388624 | tf_op jit(solution)/shard_map/all_gather | solution.py:81
  310.1 81.7 %all-gather.12.cloned.1.call-done = bf16[2048,2048]{1,0:T(8,128)(2,1)} async-done(((bf16[256,2048]{1,0:T(8,128)(2,1)}), bf16[2048,2048]{1,0:T(8,128)(2,1)}) %all-gather.12.cloned.1.call-update) | async-done | bytes 8388624 | tf_op jit(solution)/shard_map/all_gather | solution.py:82
  410.6 105.8 %all-gather.18.cloned.1.call-done = bf16[2048,2048]{1,0:T(8,128)(2,1)} async-done(((bf16[256,2048]{1,0:T(8,128)(2,1)}), bf16[2048,2048]{1,0:T(8,128)(2,1)}) %all-gather.18.cloned.1.call-update) | async-done | bytes 8388624 | tf_op jit(solution)/shard_map/all_gather | solution.py:85
  533.3 107.9 %all-gather.20.cloned.1.call-done = bf16[2,2048,1024]{2,1,0:T(8,128)(2,1)} async-done(((bf16[2,256,1024]{2,1,0:T(8,128)(2,1)}), bf16[2,2048,1024]{2,1,0:T(8,128)(2,1)}) %all-gather.20.cloned.1.call-update) | async-done | bytes 8388624 | tf_op jit(solution)/shard_map/all_gather | solution.py:154
  646.7 119.1 %all-gather.22.cloned.1.call-done = bf16[2,2048,1024]{2,1,0:T(8,128)(2,1)} async-done(((bf16[2,256,1024]{2,1,0:T(8,128)(2,1)}), bf16[2,2048,1024]{2,1,0:T(8,128)(2,1)}) %all-gather.22.cloned.1.call-update) | async-done | bytes 8388624 | tf_op jit(solution)/shard_map/all_gather | solution.py:155
  772.0 118.7 %all-gather.24.cloned.1.call-done = bf16[2,1024,2048]{2,1,0:T(8,128)(2,1)} async-done(((bf16[2,128,2048]{2,1,0:T(8,128)(2,1)}), bf16[2,1024,2048]{2,1,0:T(8,128)(2,1)}) %all-gather.24.cloned.1.call-update) | async-done | bytes 8388624 | tf_op jit(solution)/shard_map/all_gather | solution.py:156
  897.0 12.2 scatter_fusion
  1024.3 13.6 multiply_reduce_fusion
  1037.8 12.1 multiply_convert_fusion
  1131.7 84.8 %reduce-scatter.15.cloned.1.call-done = bf16[256,2048]{1,0:T(8,128)(2,1)} async-done(((bf16[2048,2048]{1,0:T(8,128)(2,1)}), bf16[256,2048]{1,0:T(8,128)(2,1)}) %reduce-scatter.15.cloned.1.call-update) | async-done | bytes 1048592 | tf_op jit(solution)/shard_map/reduce_scatter | solution.py:320
  1216.5 150.1 %reduce-scatter.21.cloned.1.call-done = bf16[2,256,1024]{2,1,0:T(8,128)(2,1)} async-done(((bf16[2,2048,1024]{2,1,0:T(8,128)(2,1)}), bf16[2,256,1024]{2,1,0:T(8,128)(2,1)}) %reduce-scatter.21.cloned.1.call-update) | async-done | bytes 1048592 | tf_op jit(solution)/shard_map/reduce_scatter | solution.py:198
  1366.6 150.2 %reduce-scatter.19.cloned.1.call-done = bf16[2,256,1024]{2,1,0:T(8,128)(2,1)} async-done(((bf16[2,2048,1024]{2,1,0:T(8,128)(2,1)}), bf16[2,256,1024]{2,1,0:T(8,128)(2,1)}) %reduce-scatter.19.cloned.1.call-update) | async-done | bytes 1048592 | tf_op jit(solution)/shard_map/reduce_scatter | solution.py:195
  1516.8 150.1 %reduce-scatter.13.cloned.1.call-done = bf16[256,2048]{1,0:T(8,128)(2,1)} async-done(((bf16[2048,2048]{1,0:T(8,128)(2,1)}), bf16[256,2048]{1,0:T(8,128)(2,1)}) %reduce-scatter.13.cloned.1.call-update) | async-done | bytes 1048592 | tf_op jit(solution)/shard_map/reduce_scatter | solution.py:311
  1666.9 150.2 %reduce-scatter.11.cloned.1.call-done = bf16[256,2048]{1,0:T(8,128)(2,1)} async-done(((bf16[2048,2048]{1,0:T(8,128)(2,1)}), bf16[256,2048]{1,0:T(8,128)(2,1)}) %reduce-scatter.11.cloned.1.call-update) | async-done | bytes 1048592 | tf_op jit(solution)/shard_map/reduce_scatter | solution.py:308
  1817.2 150.1 %reduce-scatter.9.cloned.1.call-done = bf16[256,2048]{1,0:T(8,128)(2,1)} async-done(((bf16[2048,2048]{1,0:T(8,128)(2,1)}), bf16[256,2048]{1,0:T(8,128)(2,1)}) %reduce-scatter.9.cloned.1.call-update) | async-done | bytes 1048592 | tf_op jit(solution)/shard_map/reduce_scatter | solution.py:305
  1978.1 11.7 fusion.16
  1989.8 35.7 %all-reduce.7 = (bf16[2048]{0:T(1024)(128)(2,1)S(1)}, bf16[2048]{0:T(1024)(128)(2,1)S(1)}, bf16[2048]{0:T(1024)(128)(2,1)S(1)}, bf16[2048]{0:T(1024)(128)(2,1)S(1)}) all-reduce(bf16[2048]{0:T(1024)(128)(2,1)S(1)} %get-tuple-element.71, ...), channel_id=2, replica_groups=mesh['shard'=8,'rep'=4] {'shard'}, use_global_device_ids=true, to_apply=%region_25.26.clone | all-reduce | flops 8192 | bytes 32768
  2032.8 11.7 all-reduce.8
  2047.4 123.9 %all-reduce.12.cloned.1.call-done = (bf16[256,2048]{1,0:T(8,128)(2,1)}, bf16[256,2048]{1,0:T(8,128)(2,1)}, bf16[256,2048]{1,0:T(8,128)(2,1)}, bf16[256,2048]{1,0...) async-done(((bf16[256,2048]{1,0:T(8,128)(2,1)}, bf16[256,2048]{1,0:T(8,128)(2,1)}, ...) | async-done | bytes 7340048 | tf_op jit(solution)/shard_map/psum | solution.py:333
  (294 shorter events, 369.7 us)
Async XLA Ops:
  7.2 134.9 %all-gather.14.cloned.1.call-start = ((), (), s32[]{:S(2)}) async-start(), calls=%async_computation.9 | async-start | bytes 9437184 | tf_op jit(solution)/shard_map/all_gather | solution.py:80
  8.0 85.0 %copy-start.52 = (bf16[256,64]{0,1:T(8,128)(2,1)S(1)}, bf16[256,64]{0,1:T(8,128)(2,1)}, u32[]{:S(2)}) copy-start(bf16[256,64]{0,1:T(8,128)(2,1)} %param.30) | copy-start | bytes 98308
  8.0 259.0 %all-gather.16.cloned.1.call-start = ((), (), s32[]{:S(2)}) async-start(), calls=%async_computation.10 | async-start | bytes 9437184 | tf_op jit(solution)/shard_map/all_gather | solution.py:81
  8.7 117.0 %copy-start.46 = (s32[512,8]{0,1:T(8,128)S(1)}, s32[512,8]{0,1:T(8,128)}, u32[]{:S(2)}) copy-start(s32[512,8]{0,1:T(8,128)} %param.19) | copy-start | bytes 49156
  8.7 383.0 %all-gather.12.cloned.1.call-start = ((), (), s32[]{:S(2)}) async-start(), calls=%async_computation.8 | async-start | bytes 9437184 | tf_op jit(solution)/shard_map/all_gather | solution.py:82
  9.5 118.6 %copy-start.20 = (bf16[512,2048]{1,0:T(8,128)(2,1)S(1)}, bf16[512,2048]{1,0:T(8,128)(2,1)}, u32[]{:S(2)}) copy-start(bf16[512,2048]{1,0:T(8,128)(2,1)} %param.21) | copy-start | bytes 6291460
  9.5 506.9 %all-gather.18.cloned.1.call-start = ((), (), s32[]{:S(2)}) async-start(), calls=%async_computation.11 | async-start | bytes 9437184 | tf_op jit(solution)/shard_map/all_gather | solution.py:85
  10.1 631.1 %all-gather.20.cloned.1.call-start = ((), (), s32[]{:S(2)}) async-start(), calls=%async_computation.12 | async-start | bytes 9437184 | tf_op jit(solution)/shard_map/all_gather | solution.py:154
  10.7 755.2 %all-gather.22.cloned.1.call-start = ((), (), s32[]{:S(2)}) async-start(), calls=%async_computation.13 | async-start | bytes 9437184 | tf_op jit(solution)/shard_map/all_gather | solution.py:155
  11.2 879.5 %all-gather.24.cloned.1.call-start = ((), (), s32[]{:S(2)}) async-start(), calls=%async_computation.14 | async-start | bytes 9437184 | tf_op jit(solution)/shard_map/all_gather | solution.py:156
  12.0 1119.7 %reduce-scatter.23.cloned.1.call-start = ((), (), s32[]{:S(2)}) async-start(), calls=%async_computation.22 | async-start | bytes 9437184 | tf_op jit(solution)/shard_map/reduce_scatter | solution.py:201
  16.1 375.7 %copy-start.58 = (f32[512]{0:T(512)}, f32[512]{0:T(512)S(1)}, u32[]{:S(2)}) copy-start(f32[512]{0:T(512)S(1)} %add_rsqrt_fusion.3) | copy-start | bytes 6148
  57.0 217.1 %copy-start.49 = (f32[8,1,256]{2,1,0:T(1,128)}, f32[8,1,256]{2,1,0:T(1,128)S(1)}, u32[]{:S(2)}) copy-start(f32[8,1,256]{2,1,0:T(1,128)S(1)} %convert_element_type.251) | copy-start | bytes 24580
  75.8 73.7 %copy-start.47 = (f32[8,1,256]{2,1,0:T(1,128)}, f32[8,1,256]{2,1,0:T(1,128)S(1)}, u32[]{:S(2)}) copy-start(f32[8,1,256]{2,1,0:T(1,128)S(1)} %convert_element_type.250) | copy-start | bytes 24580
  125.6 404.5 %copy-start.28 = (bf16[2048,64]{0,1:T(8,128)(2,1)}, bf16[2048,64]{0,1:T(8,128)(2,1)S(1)}, u32[]{:S(2)}) copy-start(bf16[2048,64]{0,1:T(8,128)(2,1)S(1)} %all_gather.52) | copy-start | bytes 786436
  646.7 244.0 %copy-start.13 = (f32[256,2048]{1,0:T(8,128)S(1)}, f32[256,2048]{1,0:T(8,128)}, u32[]{:S(2)}) copy-start(f32[256,2048]{1,0:T(8,128)} %gather_fusion.2) | copy-start | bytes 6291460
  920.5 296.0 %reduce-scatter.15.cloned.1.call-start = ((), (), s32[]{:S(2)}) async-start(), calls=%async_computation.18 | async-start | bytes 9437184 | tf_op jit(solution)/shard_map/reduce_scatter | solution.py:320
  979.3 387.3 %reduce-scatter.21.cloned.1.call-start = ((), (), s32[]{:S(2)}) async-start(), calls=%async_computation.21 | async-start | bytes 9437184 | tf_op jit(solution)/shard_map/reduce_scatter | solution.py:198
  986.0 530.8 %reduce-scatter.19.cloned.1.call-start = ((), (), s32[]{:S(2)}) async-start(), calls=%async_computation.20 | async-start | bytes 9437184 | tf_op jit(solution)/shard_map/reduce_scatter | solution.py:195
  992.7 674.3 %reduce-scatter.13.cloned.1.call-start = ((), (), s32[]{:S(2)}) async-start(), calls=%async_computation.17 | async-start | bytes 9437184 | tf_op jit(solution)/shard_map/reduce_scatter | solution.py:311
  1024.0 793.1 %reduce-scatter.11.cloned.1.call-start = ((), (), s32[]{:S(2)}) async-start(), calls=%async_computation.16 | async-start | bytes 9437184 | tf_op jit(solution)/shard_map/reduce_scatter | solution.py:308
  1096.4 870.8 %reduce-scatter.9.cloned.1.call-start = ((), (), s32[]{:S(2)}) async-start(), calls=%async_computation.15 | async-start | bytes 9437184 | tf_op jit(solution)/shard_map/reduce_scatter | solution.py:305
  1117.7 915.0 %reduce-scatter.17.cloned.1.call-start = ((), (), s32[]{:S(2)}) async-start(), calls=%async_computation.19 | async-start | bytes 294912 | tf_op jit(solution)/shard_map/reduce_scatter | solution.py:326
  1120.8 1050.4 %all-reduce.12.cloned.1.call-start = ((), (), s32[]{:S(2)}) async-start(), calls=%async_computation.23 | async-start | bytes 14680064 | tf_op jit(solution)/shard_map/psum | solution.py:333
  (63 other events, 331.6 us)
Sparse Core Ops, SparseCore 0:
  10.2 131.8 all-gather.13
  144.2 122.6 all-gather.15
  269.1 122.6 all-gather.11
  393.7 122.6 all-gather.17
  518.5 122.6 all-gather.19
  643.2 122.6 all-gather.21
  768.0 122.6 all-gather.23
  920.6 145.6 reduce-scatter.22
  1069.9 146.5 reduce-scatter.14
  1220.0 146.5 reduce-scatter.20
  1370.2 146.5 reduce-scatter.18
  1520.3 146.5 reduce-scatter.12
  1670.6 146.5 reduce-scatter.10
  1820.7 146.5 reduce-scatter.8
  1971.0 61.5 reduce-scatter.16
  2035.4 135.8 all-reduce.11
where the time goes:
time: 2200 us; the launch traced here: 2190 us
  waiting for transfers between devices  1610 us (73%)
  matrix products  223 us (10%)
  blocking collectives  156 us (7%)
  other arithmetic  119 us (5%)
  local copies, waits for them, and re-layouts  65.3 us (3%)
    reduce_scatter x1, waiting for transfers between devices, local(): lax.psum_scatter(key_w_grad.astype(jnp.bfloat16), 'shard', scatter_dimens...  150 us
    reduce_scatter x1, waiting for transfers between devices, local(): lax.psum_scatter(gate_w_grad.astype(jnp.bfloat16), 'shard', scatter_dimen...  150 us
    reduce_scatter x1, waiting for transfers between devices, local(): lax.psum_scatter(query_w_grad.astype(jnp.bfloat16), 'shard', scatter_dime...  150 us
    reduce_scatter x1, waiting for transfers between devices, local(): lax.psum_scatter(value_w_grad.astype(jnp.bfloat16), 'shard', scatter_dime...  150 us
    reduce_scatter x1, waiting for transfers between devices, local(): lax.psum_scatter(up_w_grad.astype(jnp.bfloat16), 'shard', scatter_dimensi...  150 us
    psum x1, waiting for transfers between devices, local(): lax.psum(owned[1].astype(jnp.bfloat16), 'rep').astype(jnp.float32)  124 us
    all_gather x1, waiting for transfers between devices, local(): lax.all_gather(w_up, 'shard', axis=1, tiled=True)  119 us
    all_gather x1, waiting for transfers between devices, local(): lax.all_gather(w_down, 'shard', axis=1, tiled=True)  119 us
  transfers between devices with their start and end apart: 16, of which 14 were waited for; matrix products, arithmetic and copies ran while one was open for 15% of the time, Pallas kernels for 0%

commit v1 on v0

v1 whole, which is shorter than its diff:
```python
import functools

import jax
import jax.numpy as jnp
from jax import lax
from jax.experimental import pallas as pl
from jax.experimental.pallas import tpu as pltpu
from jax.sharding import PartitionSpec as P

HEADS = 16
EPSILON = 1e-05
THETA = 10000.0
REACH = 2
ROWS = 128
F32 = jnp.float32
BF16 = jnp.bfloat16


def rms_scale(values):
    return lax.rsqrt(jnp.mean(values * values, -1, keepdims=True) + EPSILON)


def norm_back(values, scale, gain, upstream):
    gain_grad = jnp.sum(upstream * values * scale, 0)
    weighted = upstream * gain
    inner_mean = jnp.mean(weighted * values, -1, keepdims=True)
    return (scale * weighted - values * scale * scale * scale * inner_mean, gain_grad)


def dot(a, b, dims=((1,), (0,))):
    return lax.dot_general(a, b, (dims, ((), ())), preferred_element_type=F32)


def swap(x, mask):
    return lax.ppermute(x, "rep", [(i, i ^ mask) for i in range(4)])


def flip(x, mask):
    return jnp.stack([x[j ^ mask] for j in range(4)])


def rep_sum(x):
    x = x + flip(swap(x, 1), 1)
    return x + flip(swap(x, 2), 2)


def rep_gather(x):
    one, two = swap(x, 1), swap(x, 2)
    return [x, one, two, swap(two, 1)]


def in_order(pieces, rep):
    low = rep % 2 == 1
    high = rep // 2 == 1
    a, b, c, d = pieces
    a, b = jnp.where(low, b, a), jnp.where(low, a, b)
    c, d = jnp.where(low, d, c), jnp.where(low, c, d)
    return (
        jnp.where(high, c, a),
        jnp.where(high, d, b),
        jnp.where(high, a, c),
        jnp.where(high, b, d),
    )


def mask_bias(bias, doc_col, doc_row):
    length = doc_col.shape[0]
    rows = lax.broadcasted_iota(jnp.int32, (length, length), 0)
    cols = lax.broadcasted_iota(jnp.int32, (length, length), 1)
    allowed = (doc_col[...] == doc_row[0]) & (cols <= rows)
    bias[...] = jnp.where(allowed, 0.0, -jnp.inf).astype(F32)


def turn(values, cosine, sine):
    half = values.shape[-1] // 2
    lanes = lax.broadcasted_iota(jnp.int32, values.shape, 1)
    turned = jnp.where(lanes < half, -1.0, 1.0) * pltpu.roll(values, half, 1)
    return values * cosine + turned * sine


def turn_back(values, cosine, sine):
    half = values.shape[-1] // 2
    lanes = lax.broadcasted_iota(jnp.int32, values.shape, 1)
    moved = pltpu.roll(values * sine, half, 1)
    return values * cosine + jnp.where(lanes < half, 1.0, -1.0) * moved


def spans(length):
    return [
        (i * ROWS, (i + 1) * ROWS, max(0, (i - REACH) * ROWS)) for i in range(length // ROWS)
    ]


def attend_kernel(
    factor,
    q_ref,
    k_ref,
    v_ref,
    q_scale,
    k_scale,
    q_gain,
    k_gain,
    cosine,
    sine,
    doc_col,
    doc_row,
    mixed_ref,
    queries_ref,
    keys_ref,
    values_ref,
    bias,
):
    @pl.when(pl.program_id(1) == 0)
    def _():
        mask_bias(bias, doc_col, doc_row)

    cos, sin = cosine[...], sine[...]
    queries_ref[...] = turn(q_ref[...] * q_scale[...] * q_gain[...], cos, sin).astype(BF16)
    keys_ref[...] = turn(k_ref[...] * k_scale[...] * k_gain[...], cos, sin).astype(BF16)
    values_ref[...] = v_ref[...].astype(BF16)
    for start, end, low in spans(q_ref.shape[0]):
        scores = dot(queries_ref[start:end], keys_ref[low:end], ((1,), (1,))) * factor
        scores = scores + bias[start:end, low:end]
        weights = jnp.exp(scores - jnp.max(scores, -1, keepdims=True))
        probs = (weights * (1.0 / jnp.sum(weights, -1, keepdims=True))).astype(BF16)
        mixed_ref[start:end] = dot(probs, values_ref[low:end]).astype(BF16)


def attend_back_kernel(
    factor,
    queries,
    keys,
    values,
    grads,
    cosine,
    sine,
    doc_col,
    doc_row,
    dq_ref,
    dk_ref,
    dv_ref,
    bias,
    dk_sum,
    dv_sum,
):
    @pl.when(pl.program_id(1) == 0)
    def _():
        mask_bias(bias, doc_col, doc_row)

    cos, sin = cosine[...], sine[...]
    dk_sum[...] = jnp.zeros_like(dk_sum)
    dv_sum[...] = jnp.zeros_like(dv_sum)
    for start, end, low in spans(queries.shape[0]):
        q, g = queries[start:end], grads[start:end]
        k, v = keys[low:end], values[low:end]
        scores = dot(q, k, ((1,), (1,))) * factor + bias[start:end, low:end]
        weights = jnp.exp(scores - jnp.max(scores, -1, keepdims=True))
        probs = weights * (1.0 / jnp.sum(weights, -1, keepdims=True))
        dv_sum[low:end] += dot(probs.astype(BF16), g, ((0,), (0,)))
        prob_grad = dot(g, v, ((1,), (1,)))
        score_grad = probs * (prob_grad - jnp.sum(probs * prob_grad, -1, keepdims=True))
        score_grad = score_grad.astype(BF16)
        dq_ref[start:end] = turn_back(dot(score_grad, k) * factor, cos[start:end], sin[start:end])
        dk_sum[low:end] += dot(score_grad, q, ((0,), (0,)))
    dk_ref[...] = turn_back(dk_sum[...] * factor, cos, sin)
    dv_ref[...] = dv_sum[...].astype(BF16)


def cost(flops, moved, exps=0):
    return pl.CostEstimate(flops=flops, bytes_accessed=moved, transcendentals=exps)


def attend(qkv, q_scale, k_scale, q_gain, k_gain, cosine, sine, doc_col, doc_row, heads, dim):
    tokens = qkv.shape[0]
    length = doc_row.shape[-1]
    block = lambda off: pl.BlockSpec((length, dim), lambda j, h: (j, off + h))
    per_row = pl.BlockSpec((length, 1), lambda j, h: (j, 0))
    table = pl.BlockSpec((length, dim), lambda j, h: (j, 0))
    gain = pl.BlockSpec((1, dim), lambda j, h: (0, h))
    row = pl.BlockSpec((1, 1, length), lambda j, h: (j, 0, 0))
    out = jax.ShapeDtypeStruct((tokens, heads * dim), BF16)
    return pl.pallas_call(
        functools.partial(attend_kernel, dim ** (-0.5)),
        grid=(tokens // length, heads),
        in_specs=[block(0), block(heads), block(2 * heads), per_row, per_row, gain, gain]
        + [table, table, per_row, row],
        out_specs=[block(0)] * 4,
        out_shape=[out] * 4,
        scratch_shapes=[pltpu.VMEM((length, length), F32)],
        cost_estimate=cost(
            4 * tokens * length * heads * dim, tokens * heads * dim * 20, tokens * length * heads
        ),
        name="attend",
    )(qkv, qkv, qkv, q_scale, k_scale, q_gain, k_gain, cosine, sine, doc_col, doc_row)


def attend_back(queries, keys, values, grads, cosine, sine, doc_col, doc_row, heads, dim):
    tokens = queries.shape[0]
    length = doc_row.shape[-1]
    block = pl.BlockSpec((length, dim), lambda j, h: (j, h))
    per_row = pl.BlockSpec((length, 1), lambda j, h: (j, 0))
    table = pl.BlockSpec((length, dim), lambda j, h: (j, 0))
    row = pl.BlockSpec((1, 1, length), lambda j, h: (j, 0, 0))
    wide = jax.ShapeDtypeStruct((tokens, heads * dim), F32)
    return pl.pallas_call(
        functools.partial(attend_back_kernel, dim ** (-0.5)),
        grid=(tokens // length, heads),
        in_specs=[block] * 4 + [table, table, per_row, row],
        out_specs=[block] * 3,
        out_shape=[wide, wide, jax.ShapeDtypeStruct((tokens, heads * dim), BF16)],
        scratch_shapes=[
            pltpu.VMEM((length, length), F32),
            pltpu.VMEM((length, dim), F32),
            pltpu.VMEM((length, dim), F32),
        ],
        cost_estimate=cost(
            10 * tokens * length * heads * dim, tokens * heads * dim * 18, tokens * length * heads
        ),
        name="attend_back",
    )(queries, keys, values, grads, cosine, sine, doc_col, doc_row)


def shard_gather(x):
    return lax.all_gather(x, "shard", axis=0, tiled=True)


def shard_scatter(x):
    return lax.psum_scatter(x, "shard", scatter_dimension=0, tiled=True).astype(F32)


def split_sum(x):
    high = x.astype(BF16)
    return high, (x - high.astype(F32)).astype(BF16)


def local(
    n_shard,
    hidden_in,
    doc_ids,
    expert_ids,
    slot_rows,
    out_grad,
    attn_gain,
    w_query,
    w_key,
    w_value,
    query_gain,
    key_gain,
    w_output,
    ffn_gain,
    w_router,
    w_gate,
    w_up,
    w_down,
):
    length, width = hidden_in.shape
    dim = width // HEADS
    heads = HEADS // 4
    part = width // 4
    routed = w_router.shape[1]
    experts = w_gate.shape[0]
    hidden_units = w_gate.shape[2]
    half_units = hidden_units // 2
    cap = slot_rows.shape[2]
    rep = lax.axis_index("rep")
    shard = lax.axis_index("shard")
    core, side = rep % 2, rep // 2
    my_rows = width // n_shard
    quarter = my_rows // 4

    cut = lambda w: lax.dynamic_slice_in_dim(w, rep * part, part, 1)
    qkv_block = jnp.concatenate([cut(w_query), cut(w_key), cut(w_value)], 1)
    output_block = lax.dynamic_slice_in_dim(w_output, rep * quarter, quarter, 0)
    pick = lambda w: lax.dynamic_index_in_dim(w, core, 0, keepdims=False)
    down_rows = hidden_units // n_shard
    unit = jnp.arange(half_units)
    unit = (unit // (down_rows // 2)) * down_rows + unit % (down_rows // 2)
    choose = lambda which: (
        jnp.arange(hidden_units)[:, None] == (unit + which * (down_rows // 2))[None, :]
    ).astype(BF16)
    mine = choose(side)
    gate_up_block = jnp.concatenate(
        [dot(pick(w_gate), mine).astype(BF16), dot(pick(w_up), mine).astype(BF16)], 1
    )
    down_block = lax.dynamic_slice_in_dim(pick(w_down), side * (down_rows // 2), down_rows // 2, 0)
    w_qkv = shard_gather(qkv_block)
    gains = lax.all_gather(
        jnp.stack([attn_gain, query_gain, key_gain, ffn_gain]), "shard", axis=1, tiled=True
    ).astype(F32)
    router_w = shard_gather(w_router)
    w_out_part = shard_gather(output_block).reshape(n_shard, quarter, width)
    w_gu = shard_gather(gate_up_block)
    w_dn = shard_gather(down_block)
    gain_one, gain_two = gains[0], gains[3]
    gain_query = lax.dynamic_slice_in_dim(gains[1:2], rep * part, part, 1)
    gain_key = lax.dynamic_slice_in_dim(gains[2:3], rep * part, part, 1)
    output_w = jnp.stack(in_order(rep_gather(w_out_part), rep), 1).reshape(width, width)

    hidden_all = jnp.concatenate(rep_gather(hidden_in), 0)
    docs_all = jnp.concatenate(rep_gather(doc_ids), 0)
    slots = slot_rows[0].reshape(experts * cap)
    select = (slots[:, None] == jnp.arange(length, dtype=jnp.int32)[None, :]).astype(BF16)
    upstream = out_grad.astype(F32)

    def to_experts(x):
        own = lax.dynamic_index_in_dim(x, core, 0, keepdims=False)
        other = lax.dynamic_index_in_dim(x, 1 - core, 0, keepdims=False)
        pair = jnp.stack([own, swap(other, 1)])
        return jnp.concatenate([pair, swap(pair, 2)], 0)

    def from_experts(x, send):
        pair = x[:2] + swap(x[2:].astype(send), 2).astype(F32)
        other = swap(pair[1].astype(send), 1).astype(F32)
        first = jnp.where(core == 0, pair[0], other)
        return jnp.stack([first, jnp.where(core == 0, other, pair[0])])

    def add_slots(x):
        high, low = split_sum(x.reshape(experts * cap, width))
        return dot(select, high, ((0,), (0,))) + dot(select, low, ((0,), (0,)))

    slot_upstream = to_experts(dot(select, out_grad).astype(BF16).reshape(experts, cap, width))

    normed_scale = rms_scale(hidden_all.astype(F32))
    normed = (hidden_all.astype(F32) * normed_scale * gain_one).astype(BF16)
    before = docs_all[:, None, :] < docs_all[:, :, None]
    starts = jnp.sum(before.astype(jnp.int32), -1)
    places = (jnp.arange(length, dtype=jnp.int32)[None, :] - starts).astype(F32).reshape(-1)
    rates = THETA ** (-jnp.arange(dim // 2, dtype=F32) * 2.0 / dim)
    angles = places[:, None] * jnp.concatenate([rates, rates])[None, :]
    cosine, sine = jnp.cos(angles), jnp.sin(angles)
    doc_col = docs_all.reshape(-1, 1)
    doc_row = docs_all.reshape(4, 1, length)

    qkv = dot(normed, w_qkv)
    query_raw, key_raw = qkv[:, :part], qkv[:, part : 2 * part]
    squares = jnp.stack([jnp.sum(query_raw * query_raw, -1), jnp.sum(key_raw * key_raw, -1)], -1)
    squares = rep_sum(squares.reshape(4, length, 2)).reshape(-1, 2)
    scales = lax.rsqrt(squares / width + EPSILON)
    query_scale, key_scale = scales[:, :1], scales[:, 1:]
    mixed_heads, queries, keys, values = attend(
        qkv,
        query_scale,
        key_scale,
        gain_query,
        gain_key,
        cosine,
        sine,
        doc_col,
        doc_row,
        heads,
        dim,
    )
    blocks = mixed_heads.reshape(4, length, part)
    from_side = swap(blocks[2:], 2)
    mixed = jnp.concatenate(
        in_order([blocks[0], swap(blocks[1], 1), from_side[0], swap(from_side[1], 1)], rep), 1
    )
    hidden = hidden_in.astype(F32)
    residual = hidden + dot(mixed, output_w)
    scale_two = rms_scale(residual)
    inner = (residual * scale_two * gain_two).astype(BF16)
    logits = dot(inner, router_w)
    probs_all = jax.nn.softmax(logits, axis=-1)
    named = jnp.sum(
        (expert_ids[:, :, None] == jnp.arange(experts, dtype=jnp.int32)).astype(F32), 1
    )
    window = probs_all[:, :experts] * named
    select_wide = select.reshape(experts, cap, length).astype(F32)
    slot_gates = to_experts(jnp.sum(select_wide * window.T[:, None, :], -1))
    slot_inputs = to_experts(dot(select, inner).astype(BF16).reshape(experts, cap, width))
    slot_inputs = slot_inputs.reshape(4 * cap, width)

    gate_up = dot(slot_inputs, w_gu)
    gate_part, up_part = gate_up[:, :half_units], gate_up[:, half_units:]
    sigma = jax.nn.sigmoid(gate_part)
    swished = gate_part * sigma
    activated = (swished * up_part).astype(BF16)
    returned = dot(activated, w_dn).reshape(4, cap, width)
    slot_gate_grad = from_experts(jnp.sum(returned * slot_upstream.astype(F32), -1), F32)
    returned_grad = (slot_gates[:, :, None] * slot_upstream.astype(F32)).astype(BF16)
    returned_grad = returned_grad.reshape(4 * cap, width)
    act_grad = dot(returned_grad, w_dn, ((1,), (1,)))
    gate_grad = act_grad * up_part * sigma * (1.0 + gate_part * (1.0 - sigma))
    gate_up_grad = jnp.concatenate([gate_grad.astype(BF16), (act_grad * swished).astype(BF16)], 1)
    slot_input_grad = dot(gate_up_grad, w_gu, ((1,), (1,))).reshape(4, cap, width)
    slot_input_grad = from_experts(slot_input_grad, BF16)
    down_owned = shard_scatter(dot(activated, returned_grad, ((0,), (0,))).astype(BF16))
    gate_up_owned = shard_scatter(dot(slot_inputs, gate_up_grad, ((0,), (0,))).astype(BF16))
    own_gates = jnp.sum(select_wide * window.T[:, None, :], -1)
    returned = from_experts(returned, BF16)
    output = (residual + add_slots(own_gates[:, :, None] * returned)).astype(BF16)

    window_grad = jnp.sum(select_wide * slot_gate_grad[:, :, None], 1).T
    chosen_grad = jnp.concatenate(
        [window_grad * named, jnp.zeros((length, routed - experts), F32)], 1
    )
    logits_grad = (
        probs_all * (chosen_grad - jnp.sum(probs_all * chosen_grad, -1, keepdims=True))
    ).astype(BF16)
    router_grad = dot(logits_grad, inner, ((0,), (0,)))
    inner_grad = add_slots(slot_input_grad) + dot(logits_grad, router_w, ((1,), (1,)))
    residual_part, gain_two_grad = norm_back(residual, scale_two, gain_two, inner_grad)
    residual_grad = upstream + residual_part
    branch_grad = residual_grad.astype(BF16)
    mixed_grad = dot(branch_grad, output_w, ((1,), (1,))).astype(BF16)
    piece = lambda j: lax.dynamic_slice_in_dim(mixed_grad, (rep ^ j) * part, part, 1)
    from_side = swap(jnp.stack([piece(2), piece(3)]), 2)
    grads = jnp.concatenate([piece(0), swap(piece(1), 1), from_side[0], swap(from_side[1], 1)], 0)
    out_w_grad = dot(mixed, branch_grad, ((0,), (0,))).astype(BF16)
    out_w_grad = out_w_grad.reshape(n_shard, 2, 2, quarter, width)
    at = lambda x, i, axis: lax.dynamic_index_in_dim(x, i, axis, keepdims=False)
    out_w_grad = at(out_w_grad, core, 2).astype(F32) + swap(at(out_w_grad, 1 - core, 2), 1)
    out_w_grad = out_w_grad.astype(BF16)
    out_w_grad = at(out_w_grad, side, 1).astype(F32) + swap(at(out_w_grad, 1 - side, 1), 2)
    out_owned = shard_scatter(out_w_grad.astype(BF16).reshape(n_shard * quarter, width))

    query_grad, key_grad, value_grad = attend_back(
        queries, keys, values, grads, cosine, sine, doc_col, doc_row, heads, dim
    )
    weighted_q, weighted_k = query_grad * gain_query, key_grad * gain_key
    means = jnp.stack(
        [jnp.sum(weighted_q * query_raw, -1), jnp.sum(weighted_k * key_raw, -1)], -1
    )
    means = rep_sum(means.reshape(4, length, 2)).reshape(-1, 2) / width
    gain_query_grad = jnp.sum(query_grad * query_raw * query_scale, 0)
    gain_key_grad = jnp.sum(key_grad * key_raw * key_scale, 0)
    query_raw_grad = query_scale * weighted_q - query_raw * query_scale**3 * means[:, :1]
    key_raw_grad = key_scale * weighted_k - key_raw * key_scale**3 * means[:, 1:]
    qkv_grad = jnp.concatenate(
        [query_raw_grad.astype(BF16), key_raw_grad.astype(BF16), value_grad], 1
    )
    qkv_owned = shard_scatter(dot(normed, qkv_grad, ((0,), (0,))).astype(BF16))
    normed_grad = dot(qkv_grad, w_qkv, ((1,), (1,)))
    gain_one_grad = jnp.sum(normed_grad * hidden_all.astype(F32) * normed_scale, 0)
    normed_grad = normed_grad.reshape(4, length, width)
    from_core = swap(normed_grad[1::2].astype(BF16), 1).astype(F32)
    pair_two = (normed_grad[2] + from_core[1]).astype(BF16)
    normed_grad = normed_grad[0] + from_core[0] + swap(pair_two, 2).astype(F32)
    weighted = normed_grad * gain_one
    scale_one = normed_scale[:length]
    inner_mean = jnp.mean(weighted * hidden, -1, keepdims=True)
    hidden_part = scale_one * weighted - hidden * scale_one * scale_one * scale_one * inner_mean
    input_grad = residual_grad + hidden_part

    place = lambda g: lax.dynamic_update_slice_in_dim(
        jnp.zeros((1, width), F32), g[None], rep * part, 1
    )
    small = jnp.concatenate(
        [
            router_grad,
            gain_one_grad[None],
            place(gain_query_grad),
            place(gain_key_grad),
            gain_two_grad[None],
            jnp.zeros((4, width), F32),
        ],
        0,
    )
    small = lax.psum(small, ("shard", "rep"))
    small = lax.dynamic_slice_in_dim(small, shard * my_rows, my_rows, 1)
    qkv_pieces = in_order(rep_gather(qkv_owned.astype(BF16)), rep)
    spread = lambda i: jnp.concatenate(
        [p[:, i * part : (i + 1) * part] for p in qkv_pieces], 1
    ).astype(F32)
    out_full = jnp.concatenate(in_order(rep_gather(out_owned.astype(BF16)), rep), 0).astype(F32)
    gu_pieces = in_order(rep_gather(gate_up_owned.astype(BF16)), rep)
    dn_pieces = in_order(rep_gather(down_owned.astype(BF16)), rep)
    one, two = choose(0), choose(1)
    join = lambda i: jnp.stack(
        [
            dot(gu_pieces[e][:, i * half_units : (i + 1) * half_units], one, ((1,), (1,)))
            + dot(gu_pieces[2 + e][:, i * half_units : (i + 1) * half_units], two, ((1,), (1,)))
            for e in range(experts)
        ]
    )
    down_full = jnp.stack(
        [jnp.concatenate([dn_pieces[e], dn_pieces[2 + e]], 0) for e in range(experts)]
    ).astype(F32)
    return (
        output,
        input_grad,
        small[routed],
        spread(0),
        spread(1),
        spread(2),
        small[routed + 1],
        small[routed + 2],
        out_full,
        small[routed + 3],
        small[:routed].T,
        join(0),
        join(1),
        down_full,
    )


def solution(mesh):
    tokens = P(("shard", "rep"), None)
    rows = P("shard", None)
    middle = P(None, "shard", None)
    return jax.shard_map(
        functools.partial(local, mesh.shape["shard"]),
        mesh=mesh,
        in_specs=(
            tokens,
            tokens,
            tokens,
            P(("shard", "rep"), None, None),
            tokens,
            P("shard"),
            rows,
            rows,
            rows,
            P("shard"),
            P("shard"),
            rows,
            P("shard"),
            rows,
            middle,
            middle,
            middle,
        ),
        out_specs=(
            tokens,
            tokens,
            P("shard"),
            rows,
            rows,
            rows,
            P("shard"),
            P("shard"),
            rows,
            P("shard"),
            rows,
            middle,
            middle,
            middle,
        ),
        check_vma=False,
    )
```

time: 2200 us -> 983 us (0.45)
  waiting for transfers between devices: 1610 us -> 513 us
  blocking collectives: 156 us -> 59.2 us
  matrix products: 223 us -> 129 us
  Pallas kernels: 0 us -> 73.2 us
  starting transfers between devices: 1.47 us -> 24.9 us
    reduce_scatter x8 -> x4, waiting for transfers between devices: 836 us -> 222 us  [shard_scatter(): lax.psum_scatter(x, 'shard', scatter_dimension=0, tiled=True).astype(F32)]
    all_gather x7 -> x4, waiting for transfers between devices: 646 us -> 61.3 us  [shard_gather(): return lax.all_gather(x, 'shard', axis=0, tiled=True)]
    ppermute x0 -> x47, waiting for transfers between devices: none -> 230 us  [swap(): return lax.ppermute(x, 'rep', [(i, i ^ mask) for i in range(4)])]
    psum x1, waiting for transfers between devices: 124 us -> 0.01 us  [local(): small = lax.psum(small, ('shard', 'rep'))]
    dot_general x30 -> x31, matrix products: 223 us -> 129 us  [dot(): return lax.dot_general(a, b, (dims, ((), ())), preferred_element_type=F32)]
    pallas_call x0 -> x2, Pallas kernels: none -> 73.2 us  [the longest x1 38 us: attend_back(): pl.pallas_call(functools.partial(attend_back_kernel, dim ** (-0.5)), grid...]
    all_gather x5 -> x2, blocking collectives: 109 us -> 59.2 us  [the longest x1 31.8 us: shard_gather(): return lax.all_gather(x, 'shard', axis=0, tiled=True)]
    unnamed x1 -> x0, blocking collectives: 35.7 us -> none
  transfers between devices with their start and end apart: 16 -> 56, of which waited for: 14 -> 24; matrix products, arithmetic and copies ran while one was open for 15% -> 25% of each run, Pallas kernels for 0% -> 7%
where the time goes in v1:
time: 983 us; the launch traced here: 978 us
  waiting for transfers between devices  513 us (52%)
  matrix products  129 us (13%)
  other arithmetic  111 us (11%)
  Pallas kernels  73.2 us (7%)
  blocking collectives  59.2 us (6%)
  local copies, waits for them, and re-layouts  52.3 us (5%)
  starting transfers between devices  24.9 us (3%)
  between operations  15.6 us (2%)
    ppermute x47, waiting for transfers between devices, swap(): return lax.ppermute(x, 'rep', [(i, i ^ mask) for i in range(4)])  230 us
    reduce_scatter x4, waiting for transfers between devices, shard_scatter(): lax.psum_scatter(x, 'shard', scatter_dimension=0, tiled=True).astype(F32)  222 us
    dot_general x31, matrix products, dot(): return lax.dot_general(a, b, (dims, ((), ())), preferred_element_type=F32)  129 us
    all_gather x4, waiting for transfers between devices, shard_gather(): return lax.all_gather(x, 'shard', axis=0, tiled=True)  61.3 us
    pallas_call x1, Pallas kernels, attend_back(): pl.pallas_call(functools.partial(attend_back_kernel, dim ** (-0.5)), grid...  38 us
    pallas_call x1, Pallas kernels, attend(): pl.pallas_call(functools.partial(attend_kernel, dim ** (-0.5)), grid=(tok...  35.2 us
    all_gather x1, blocking collectives, shard_gather(): return lax.all_gather(x, 'shard', axis=0, tiled=True)  31.8 us
    all_gather x1, blocking collectives, local(): lax.all_gather(jnp.stack([attn_gain, query_gain, key_gain, ffn_gain]), 's...  27.4 us
  transfers between devices with their start and end apart: 56, of which 24 were waited for; matrix products, arithmetic and copies ran while one was open for 25% of the time, Pallas kernels for 7%

profile of v1, /device:TPU:0, one launch (start us, length us, event | category | flops | bytes accessed | tf_op | source)
XLA Modules:
  0.0 978.3 jit_solution(10564259447714399593)
XLA Ops:
  19.5 41.6 %collective-permute-done.1 = bf16[512,2048]{1,0:T(8,128)(2,1)} collective-permute-done((bf16[512,2048]{1,0:T(8,128)(2,1)S(1)}, bf16[512,2048]{1,0:T(8,128)(2,1)}, u32[]{:S(2)}, u32[]{:S(2)}) %collective-permute-start.1) | collective-permute-done | bytes 2097184 | tf_op jit(solution)/shard_map/ppermute | solution.py:35
  65.3 27.4 %all_gather.18 = bf16[4,2048]{1,0:T(4,128)(2,1)S(1)} all-gather(bf16[4,256]{1,0:T(4,128)(2,1)S(1)} %pad_maximum_fusion.29), channel_id=1, replica_groups=mesh['shard'=8,'rep'=4] {'shard'}, dimensions={1}, use_global_device_ids=true | all-gather | bytes 18432 | tf_op jit(solution)/shard_map/all_gather | solution.py:287
  101.5 61.2 %all-gather.6.cloned.1.call-done = bf16[2048,1536]{1,0:T(8,128)(2,1)} async-done(((bf16[256,1536]{1,0:T(8,128)(2,1)}), bf16[2048,1536]{1,0:T(8,128)(2,1)}) %all-gather.6.cloned.1.call-update) | async-done | bytes 6291472 | tf_op jit(solution)/shard_map/all_gather | solution.py:224
  162.8 22.5 %fusion.22.q_ref.k_ref.v_ref = f32[2048,1536]{1,0:T(8,128)} fusion(bf16[2048,1536]{1,0:T(8,128)(2,1)} %all-gather.6.cloned.1.call-done, f32[2048]{0:T(1024)S(1)} %bitcast.282, f32[2048]{0:T(1024)S(1)} %add_rsqrt_fusion, bf16[512,2048]{1,0:T(8,128)(2,1)} %collective-permute-done.2, bf16[512,2048]{1,0:T(8,128)(2,1)} %collective-permute-done.1, ...), kind=kOutput, calls=%fused_computation.60 | convolution fusion | flops 12931039232 | bytes 27279360 | tf_op jit(solution)/shard_map/dot_general | solution.py:31
  207.6 35.2 %attend.1 = (bf16[2048,512]{1,0:T(8,128)(2,1)}, bf16[2048,512]{1,0:T(8,128)(2,1)}, bf16[2048,512]{1,0:T(8,128)(2,1)}, bf16[2048,512]{1,0:T(8,128)(2,1)}) custom-call(f32[2048,1536]{1,0:T(8,128)} %fusion.22.q_ref.k_ref.v_ref, f32[2048,1536]{1,0:T(8,128)} %fusion.22.q_ref.k_ref.v_ref, f32[2048,1536]{1,0:T(8,128)} %fusion.22.q_ref.k_ref.v_ref, ...), custom_call_target="tpu_custom_call" | custom-call | flops 2147483648 | bytes 20971520 | tf_op jit(solution)/shard_map/attend/pallas_call | solution.py:182
  252.1 18.4 %collective-permute-done.8 = bf16[2,512,512]{2,1,0:T(8,128)(2,1)S(1)} collective-permute-done((bf16[2,512,512]{2,1,0:T(8,128)(2,1)}, bf16[2,512,512]{2,1,0:T(8,128)(2,1)S(1)}, u32[]{:S(2)}, u32[]{:S(2)}) %collective-permute-start.8) | collective-permute-done | bytes 1048608 | tf_op jit(solution)/shard_map/ppermute | solution.py:35
  285.8 31.8 %all_gather.21 = bf16[2048,64]{0,1:T(8,128)(2,1)S(1)} all-gather(bf16[256,64]{0,1:T(8,128)(2,1)S(1)} %copy-done.51), channel_id=1, replica_groups=mesh['shard'=8,'rep'=4] {'shard'}, dimensions={0}, use_global_device_ids=true | all-gather | bytes 294912 | tf_op jit(solution)/shard_map/all_gather | solution.py:224
  321.9 8.2 collective-permute-done.15
  363.0 23.4 %collective-permute-done.22 = bf16[2,128,2048]{2,1,0:T(8,128)(2,1)S(1)} collective-permute-done((bf16[2,128,2048]{2,1,0:T(8,128)(2,1)S(1)}, bf16[2,128,2048]{2,1,0:T(8,128)(2,1)S(1)}, u32[]{:S(2)}, u32[]{:S(2)}) %collective-permute-start.22) | collective-permute-done | bytes 1048608 | tf_op jit(solution)/shard_map/ppermute | solution.py:35
  405.3 24.6 %collective-permute-done.27 = bf16[2,512,512]{2,1,0:T(8,128)(2,1)S(1)} collective-permute-done((bf16[2,512,512]{2,1,0:T(8,128)(2,1)S(1)}, bf16[2,512,512]{2,1,0:T(8,128)(2,1)S(1)}, u32[]{:S(2)}, u32[]{:S(2)}) %collective-permute-start.27) | collective-permute-done | bytes 1048608 | tf_op jit(solution)/shard_map/ppermute | solution.py:35
  437.5 38.0 %attend_back.1 = (f32[2048,512]{1,0:T(8,128)}, f32[2048,512]{1,0:T(8,128)}, bf16[2048,512]{1,0:T(8,128)(2,1)}) custom-call(bf16[2048,512]{1,0:T(8,128)(2,1)} %get-tuple-element.22.queries, bf16[2048,512]{1,0:T(8,128)(2,1)} %get-tuple-element.23.keys, bf16[2048,512]{1,0:T(8,128)(2,1)} %get-tuple-element.24.values, ...), custom_call_target="tpu_custom_call" | custom-call | flops 5368709120 | bytes 18874368 | tf_op jit(solution)/shard_map/attend_back/pallas_call | solution.py:205
  475.6 7.0 multiply_reduce_fusion.1
  491.7 8.4 subtract_convert_fusion.1
  500.1 25.2 %fusion.4 = (f32[2048]{0:T(1024)S(1)}, bf16[2048,2048]{1,0:T(8,128)(2,1)}, f32[2048,2048]{1,0:T(8,128)}) fusion(f32[2048]{0:T(1024)S(1)} %copy-done.61, bf16[512,2048]{1,0:T(8,128)(2,1)} %collective-permute-done.2, bf16[512,2048]{1,0:T(8,128)(2,1)} %collective-permute-done.1, bf16[512,2048]{1,0:T(8,128)(2,1)} %collective-permute-done, ...), kind=kOutput, calls=%fused_computation.7 | convolution fusion | flops 12954105856 | bytes 46153728 | tf_op jit(solution)/shard_map/dot_general | solution.py:31
  534.4 7.1 convolution_convert_fusion
  546.0 7.5 collective-permute-done.36
  563.1 47.9 %collective-permute-done.37 = bf16[8,64,2048]{2,1,0:T(8,128)(2,1)} collective-permute-done((bf16[8,64,2048]{2,1,0:T(8,128)(2,1)}, bf16[8,64,2048]{2,1,0:T(8,128)(2,1)}, u32[]{:S(2)}, u32[]{:S(2)}) %collective-permute-start.37) | collective-permute-done | bytes 2097184 | tf_op jit(solution)/shard_map/ppermute | solution.py:35
  615.5 19.8 %convolution_convert_fusion.1 = bf16[2048,1536]{1,0:T(8,128)(2,1)} fusion(bf16[2048,512]{1,0:T(8,128)(2,1)} %get-tuple-element.27, bf16[2048,512]{1,0:T(8,128)(2,1)} %get-tuple-element.51, bf16[2048,512]{1,0:T(8,128)(2,1)} %get-tuple-element.50, f32[2048]{0:T(1024)S(1)} %bitcast.283, f32[2048]{0:T(1024)S(1)} %copy-done.61, ...), kind=kOutput, calls=%fused_computation.13 | convolution fusion | flops 12953059328 | bytes 20987904 | tf_op jit(solution)/shard_map/dot_general | solution.py:31
  639.6 22.4 %collective-permute-done.16 = bf16[2,128,2048]{2,1,0:T(8,128)(2,1)S(1)} collective-permute-done((bf16[2,128,2048]{2,1,0:T(8,128)(2,1)S(1)}, bf16[2,128,2048]{2,1,0:T(8,128)(2,1)S(1)}, u32[]{:S(2)}, u32[]{:S(2)}) %collective-permute-start.16) | collective-permute-done | bytes 1048608 | tf_op jit(solution)/shard_map/ppermute | solution.py:35
  687.8 57.2 %reduce-scatter.9.cloned.1.call-done = bf16[256,1024]{1,0:T(8,128)(2,1)} async-done(((bf16[2048,1024]{1,0:T(8,128)(2,1)}), bf16[256,1024]{1,0:T(8,128)(2,1)}) %reduce-scatter.9.cloned.1.call-update) | async-done | bytes 524304 | tf_op jit(solution)/shard_map/reduce_scatter | solution.py:228
  772.0 45.2 %reduce-scatter.7.cloned.1.call-done = bf16[64,2048]{1,0:T(8,128)(2,1)} async-done(((bf16[512,2048]{1,0:T(8,128)(2,1)}), bf16[64,2048]{1,0:T(8,128)(2,1)}) %reduce-scatter.7.cloned.1.call-update) | async-done | bytes 262160 | tf_op jit(solution)/shard_map/reduce_scatter | solution.py:228
  818.6 119.3 %reduce-scatter.5.cloned.1.call-done = bf16[256,1536]{1,0:T(8,128)(2,1)} async-done(((bf16[2048,1536]{1,0:T(8,128)(2,1)}), bf16[256,1536]{1,0:T(8,128)(2,1)}) %reduce-scatter.5.cloned.1.call-update) | async-done | bytes 786448 | tf_op jit(solution)/shard_map/reduce_scatter | solution.py:228
  945.2 11.4 %collective-permute-done.33 = bf16[256,1536]{1,0:T(8,128)(2,1)S(1)} collective-permute-done((bf16[256,1536]{1,0:T(8,128)(2,1)}, bf16[256,1536]{1,0:T(8,128)(2,1)S(1)}, u32[]{:S(2)}, u32[]{:S(2)}) %collective-permute-start.33) | collective-permute-done | bytes 786464 | tf_op jit(solution)/shard_map/ppermute | solution.py:35
  956.6 6.8 fusion.12
  (427 shorter events, 245.0 us)
Async XLA Ops:
  7.2 88.5 %all-gather.8.cloned.1.call-start = ((), (), s32[]{:S(2)}) async-start(), calls=%async_computation.5 | async-start | bytes 2359296 | tf_op jit(solution)/shard_map/all_gather | solution.py:224
  9.2 153.6 %all-gather.6.cloned.1.call-start = ((), (), s32[]{:S(2)}) async-start(), calls=%async_computation.4 | async-start | bytes 7077888 | tf_op jit(solution)/shard_map/all_gather | solution.py:224
  12.2 320.6 %all-gather.10.cloned.1.call-start = ((), (), s32[]{:S(2)}) async-start(), calls=%async_computation.6 | async-start | bytes 4718592 | tf_op jit(solution)/shard_map/all_gather | solution.py:224
  12.3 48.8 %collective-permute-start.1 = (bf16[512,2048]{1,0:T(8,128)(2,1)S(1)}, bf16[512,2048]{1,0:T(8,128)(2,1)}, u32[]{:S(2)}, u32[]{:S(2)}) collective-permute-start(bf16[512,2048]{1,0:T(8,128)(2,1)S(1)} %copy-done.7), channel_id=1, source_target_pairs={{0,2},{1,3},{2,0},{3,1},{4,6},{5,7},{6,4},{7,5},{8,10},{9,11},{10,... | collective-permute-start | bytes 6291464 | tf_op jit(solution)/shard_map/ppermute | solution.py:35
  15.3 78.2 %collective-permute-start.5 = (s32[1,512]{1,0:T(1,128)S(1)}, s32[1,512]{1,0:T(1,128)S(1)}, u32[]{:S(2)}, u32[]{:S(2)}) collective-permute-start(s32[1,512]{1,0:T(1,128)S(1)} %copy-done.64), channel_id=1, source_target_pairs={{0,1},{1,0},{2,3},{3,2},{4,5},{5,4},{6,7},{7,6},{8,9},{9,8},{10,11... | collective-permute-start | bytes 6152 | tf_op jit(solution)/shard_map/ppermute | solution.py:35
  15.3 78.1 %collective-permute-start.6 = (s32[1,512]{1,0:T(1,128)S(1)}, s32[1,512]{1,0:T(1,128)S(1)}, u32[]{:S(2)}, u32[]{:S(2)}) collective-permute-start(s32[1,512]{1,0:T(1,128)S(1)} %copy-done.64), channel_id=1, source_target_pairs={{0,2},{1,3},{2,0},{3,1},{4,6},{5,7},{6,4},{7,5},{8,10},{9,11},{10,... | collective-permute-start | bytes 6152 | tf_op jit(solution)/shard_map/ppermute | solution.py:35
  15.5 81.7 %collective-permute-start = (bf16[512,2048]{1,0:T(8,128)(2,1)S(1)}, bf16[512,2048]{1,0:T(8,128)(2,1)}, u32[]{:S(2)}, u32[]{:S(2)}) collective-permute-start(bf16[512,2048]{1,0:T(8,128)(2,1)S(1)} %copy-done.7), channel_id=1, source_target_pairs={{0,1},{1,0},{2,3},{3,2},{4,5},{5,4},{6,7},{7,6},{8,9},{9,8},{10,11... | collective-permute-start | bytes 6291464 | tf_op jit(solution)/shard_map/ppermute | solution.py:35
  19.4 260.4 %collective-permute-start.20 = (bf16[128,2048]{1,0:T(8,128)(2,1)}, bf16[128,2048]{1,0:T(8,128)(2,1)}, u32[]{:S(2)}, u32[]{:S(2)}) collective-permute-start(bf16[128,2048]{1,0:T(8,128)(2,1)} %get-tuple-element.93), channel_id=1, source_target_pairs={{0,1},{1,0},{2,3},{3,2},{4,5},{5,4},{6,7},{7,6},{8,9},{9,8},{10,11... | collective-permute-start | bytes 1572872 | tf_op jit(solution)/shard_map/ppermute | solution.py:35
  61.1 36.1 %collective-permute-start.2 = (bf16[512,2048]{1,0:T(8,128)(2,1)}, bf16[512,2048]{1,0:T(8,128)(2,1)}, u32[]{:S(2)}, u32[]{:S(2)}) collective-permute-start(bf16[512,2048]{1,0:T(8,128)(2,1)} %collective-permute-done.1), channel_id=1, source_target_pairs={{0,1},{1,0},{2,3},{3,2},{4,5},{5,4},{6,7},{7,6},{8,9},{9,8},{10,11... | collective-permute-start | bytes 6291464 | tf_op jit(solution)/shard_map/ppermute | solution.py:35
  65.2 274.5 %all-gather.12.cloned.1.call-start = ((), (), s32[]{:S(2)}) async-start(), calls=%async_computation.12 | async-start | bytes 2359296 | tf_op jit(solution)/shard_map/all_gather | solution.py:224
  95.7 101.8 %collective-permute-start.11 = (bf16[8,64,2048]{2,1,0:T(8,128)(2,1)}, bf16[8,64,2048]{2,1,0:T(8,128)(2,1)}, u32[]{:S(2)}, u32[]{:S(2)}) collective-permute-start(bf16[8,64,2048]{2,1,0:T(8,128)(2,1)} %bitcast.262), channel_id=1, source_target_pairs={{0,2},{1,3},{2,0},{3,1},{4,6},{5,7},{6,4},{7,5},{8,10},{9,11},{10,... | collective-permute-start | bytes 6291464 | tf_op jit(solution)/shard_map/ppermute | solution.py:35
  197.1 50.9 %collective-permute-start.13 = (bf16[8,64,2048]{2,1,0:T(8,128)(2,1)}, bf16[8,64,2048]{2,1,0:T(8,128)(2,1)}, u32[]{:S(2)}, u32[]{:S(2)}) collective-permute-start(bf16[8,64,2048]{2,1,0:T(8,128)(2,1)} %bitcast.263), channel_id=1, source_target_pairs={{0,1},{1,0},{2,3},{3,2},{4,5},{5,4},{6,7},{7,6},{8,9},{9,8},{10,11... | collective-permute-start | bytes 6291464 | tf_op jit(solution)/shard_map/ppermute | solution.py:35
  197.5 50.4 %collective-permute-start.12 = (bf16[8,64,2048]{2,1,0:T(8,128)(2,1)}, bf16[8,64,2048]{2,1,0:T(8,128)(2,1)}, u32[]{:S(2)}, u32[]{:S(2)}) collective-permute-start(bf16[8,64,2048]{2,1,0:T(8,128)(2,1)} %collective-permute-done.11), channel_id=1, source_target_pairs={{0,1},{1,0},{2,3},{3,2},{4,5},{5,4},{6,7},{7,6},{8,9},{9,8},{10,11... | collective-permute-start | bytes 6291464 | tf_op jit(solution)/shard_map/ppermute | solution.py:35
  247.8 424.2 %reduce-scatter.11.cloned.1.call-start = ((), (), s32[]{:S(2)}) async-start(), calls=%async_computation.11 | async-start | bytes 2359296 | tf_op jit(solution)/shard_map/reduce_scatter | solution.py:228
  281.9 35.8 %collective-permute-start.21 = (bf16[2,128,2048]{2,1,0:T(8,128)(2,1)}, bf16[2,128,2048]{2,1,0:T(8,128)(2,1)}, u32[]{:S(2)}, u32[]{:S(2)}) collective-permute-start(bf16[2,128,2048]{2,1,0:T(8,128)(2,1)} %pad_maximum_fusion.14), channel_id=1, source_target_pairs={{0,2},{1,3},{2,0},{3,1},{4,6},{5,7},{6,4},{7,5},{8,10},{9,11},{10,... | collective-permute-start | bytes 3145736 | tf_op jit(solution)/shard_map/ppermute | solution.py:35
  284.3 45.8 %collective-permute-start.15 = (bf16[2,128,2048]{2,1,0:T(8,128)(2,1)}, bf16[2,128,2048]{2,1,0:T(8,128)(2,1)}, u32[]{:S(2)}, u32[]{:S(2)}) collective-permute-start(bf16[2,128,2048]{2,1,0:T(8,128)(2,1)} %pad_maximum_fusion.13), channel_id=1, source_target_pairs={{0,2},{1,3},{2,0},{3,1},{4,6},{5,7},{6,4},{7,5},{8,10},{9,11},{10,... | collective-permute-start | bytes 3145736 | tf_op jit(solution)/shard_map/ppermute | solution.py:35
  434.7 248.1 %all-reduce.3.cloned.1.call-start = ((), (), s32[]{:S(2)}) async-start(), calls=%async_computation.7 | async-start | bytes 1179648 | tf_op jit(solution)/shard_map/psum | solution.py:459
  526.9 218.0 %reduce-scatter.9.cloned.1.call-start = ((), (), s32[]{:S(2)}) async-start(), calls=%async_computation.10 | async-start | bytes 4718592 | tf_op jit(solution)/shard_map/reduce_scatter | solution.py:228
  533.2 283.9 %reduce-scatter.7.cloned.1.call-start = ((), (), s32[]{:S(2)}) async-start(), calls=%async_computation.9 | async-start | bytes 2359296 | tf_op jit(solution)/shard_map/reduce_scatter | solution.py:228
  562.5 48.5 %collective-permute-start.37 = (bf16[8,64,2048]{2,1,0:T(8,128)(2,1)}, bf16[8,64,2048]{2,1,0:T(8,128)(2,1)}, u32[]{:S(2)}, u32[]{:S(2)}) collective-permute-start(bf16[8,64,2048]{2,1,0:T(8,128)(2,1)} %dynamic-slice_bitcast_fusion.1), channel_id=1, source_target_pairs={{0,2},{1,3},{2,0},{3,1},{4,6},{5,7},{6,4},{7,5},{8,10},{9,11},{10,... | collective-permute-start | bytes 6291464 | tf_op jit(solution)/shard_map/ppermute | solution.py:35
  615.5 322.4 %reduce-scatter.5.cloned.1.call-start = ((), (), s32[]{:S(2)}) async-start(), calls=%async_computation.8 | async-start | bytes 7077888 | tf_op jit(solution)/shard_map/reduce_scatter | solution.py:228
  668.6 80.4 %collective-permute-start.31 = (bf16[2,512,2048]{2,1,0:T(8,128)(2,1)}, bf16[2,512,2048]{2,1,0:T(8,128)(2,1)}, u32[]{:S(2)}, u32[]{:S(2)}) collective-permute-start(bf16[2,512,2048]{2,1,0:T(8,128)(2,1)} %slice.326), channel_id=1, source_target_pairs={{0,1},{1,0},{2,3},{3,2},{4,5},{5,4},{6,7},{7,6},{8,9},{9,8},{10,11... | collective-permute-start | bytes 12582920 | tf_op jit(solution)/shard_map/ppermute | solution.py:35
  762.5 176.9 %collective-permute-start.32 = (bf16[512,2048]{1,0:T(8,128)(2,1)}, bf16[512,2048]{1,0:T(8,128)(2,1)}, u32[]{:S(2)}, u32[]{:S(2)}) collective-permute-start(bf16[512,2048]{1,0:T(8,128)(2,1)} %fusion.15), channel_id=1, source_target_pairs={{0,2},{1,3},{2,0},{3,1},{4,6},{5,7},{6,4},{7,5},{8,10},{9,11},{10,... | collective-permute-start | bytes 6291464 | tf_op jit(solution)/shard_map/ppermute | solution.py:35
  817.2 127.5 %collective-permute-start.38 = (bf16[64,2048]{1,0:T(8,128)(2,1)}, bf16[64,2048]{1,0:T(8,128)(2,1)S(1)}, u32[]{:S(2)}, u32[]{:S(2)}) collective-permute-start(bf16[64,2048]{1,0:T(8,128)(2,1)} %reduce-scatter.7.cloned.1.call-done), channel_id=1, source_target_pairs={{0,2},{1,3},{2,0},{3,1},{4,6},{5,7},{6,4},{7,5},{8,10},{9,11},{10,... | collective-permute-start | bytes 786440 | tf_op jit(solution)/shard_map/ppermute | solution.py:35
  (107 other events, 1647.5 us)
Sparse Core Ops, SparseCore 0:
  10.7 51.8 all-gather.7
  65.3 97.3 all-gather.5
  164.9 71.0 all-gather.9
  248.0 47.4 all-gather.11
  434.9 65.8 reduce-scatter.10
  527.0 125.6 all-reduce.2
  656.4 88.5 reduce-scatter.8
  749.0 68.0 reduce-scatter.6
  820.7 117.1 reduce-scatter.4

commit v2 on v1

--- a/solution.py
+++ b/solution.py
@@ -218,6 +218,112 @@
         ),
         name="attend_back",
     )(queries, keys, values, grads, cosine, sine, doc_col, doc_row)
+
+
+def tie(*arrays):
+    return lax.optimization_barrier(arrays)
+
+
+def ring_of(n):
+    return list(range(0, n, 2)) + list(range(n - 1, 0, -2))
+
+
+def ring_step(x, n, back=False):
+    ring = ring_of(n)
+    pairs = [(ring[i], ring[(i + 1) % n]) for i in range(n)]
+    return lax.ppermute(x, "shard", [(b, a) for a, b in pairs] if back else pairs)
+
+
+def ring_ids(n, shard):
+    ring = ring_of(n)
+    places = jnp.asarray([ring.index(i) for i in range(n)], jnp.int32)
+    return jnp.asarray(ring, jnp.int32)[(places[shard] + jnp.arange(n, dtype=jnp.int32)) % n]
+
+
+def ring_gather(block, n, due):
+    half = block.shape[0] // 2
+    pieces = [(block, 0, 0)]
+    ahead = behind = block
+    for k in range(1, n // 2):
+        behind, ahead = tie(ring_step(behind, n), ring_step(ahead, n, True))
+        if k == n // 2 - 1:
+            behind, ahead, *due = tie(behind, ahead, *due)
+        pieces += [(behind, n - k, 0), (ahead, k, 0)]
+    pieces.append((ring_step(behind[:half], n), n // 2, 0))
+    pieces.append((ring_step(ahead[half:], n, True), n // 2, half))
+    return pieces, due
+
+
+def place_kernel(n, cut, starts, *refs):
+    ins, outs, bufs = refs[:n], refs[n : n + 2], refs[n + 2 : 2 * n + 2]
+    sem_in, sem_out = refs[-2], refs[-1]
+    loads = [pltpu.make_async_copy(ins[i], bufs[i], sem_in.at[i]) for i in range(n)]
+    for load in loads:
+        load.start()
+    stores = []
+    for i in range(n):
+        loads[i].wait()
+        at = pl.multiple_of(starts[i], 16)
+        rows, cols = bufs[i].shape
+        for o, first, size in ((0, 0, cut), (1, cut, cols - cut)):
+            stores.append(
+                pltpu.make_async_copy(
+                    bufs[i].at[:, pl.ds(first, size)],
+                    outs[o].at[pl.ds(at, rows)],
+                    sem_out.at[2 * i + o],
+                )
+            )
+            stores[-1].start()
+    for store in stores:
+        store.wait()
+
+
+def place_rows(pieces, starts, rows, cut):
+    cols = pieces[0].shape[1]
+    n = len(pieces)
+    anywhere = pl.BlockSpec(memory_space=pl.ANY)
+    return pl.pallas_call(
+        functools.partial(place_kernel, n, cut),
+        grid_spec=pltpu.PrefetchScalarGridSpec(
+            num_scalar_prefetch=1,
+            grid=(),
+            in_specs=[anywhere] * n,
+            out_specs=[anywhere] * 2,
+            scratch_shapes=[pltpu.VMEM(x.shape, x.dtype) for x in pieces]
+            + [pltpu.SemaphoreType.DMA((n,)), pltpu.SemaphoreType.DMA((2 * n,))],
+        ),
+        out_shape=[
+            jax.ShapeDtypeStruct((rows, size), pieces[0].dtype) for size in (cut, cols - cut)
+        ],
+        cost_estimate=cost(0, 4 * rows * cols),
+        name="place_rows",
+    )(starts, *pieces)
+
+
+def ring_scatter(parts, n, shard, due):
+    rows = parts[0].shape[0] // n
+    half = rows // 2
+    ids = ring_ids(n, shard)
+    chunk = lambda k, first=0, size=rows: jnp.concatenate(
+        [lax.dynamic_slice_in_dim(x, ids[k % n] * rows + first, size, 0) for x in parts], 1
+    )
+    done = []
+    ahead = ring_step(chunk(n // 2, 0, half), n)
+    behind = ring_step(chunk(n // 2, half, half), n, True)
+    for k in range(n // 2 - 1, -1, -1):
+        at = n // 2 - 1 - k
+        ahead, behind, *got = tie(ahead, behind, *(due[at](*done) if at < len(due) else ()))
+        done = got or done
+        if k == 0:
+            break
+        a, b = chunk(k), chunk(n - k)
+        if at == 0:
+            a = jnp.concatenate([a[:half].astype(F32) + ahead, a[half:]], 0)
+            b = jnp.concatenate([b[:half], b[half:].astype(F32) + behind], 0)
+        else:
+            a, b = a.astype(F32) + ahead, b.astype(F32) + behind
+        ahead, behind = ring_step(a.astype(BF16), n), ring_step(b.astype(BF16), n, True)
+    return chunk(0).astype(F32) + ahead + behind, done
 
 
 def shard_gather(x):
@@ -283,45 +389,13 @@
         [dot(pick(w_gate), mine).astype(BF16), dot(pick(w_up), mine).astype(BF16)], 1
     )
     down_block = lax.dynamic_slice_in_dim(pick(w_down), side * (down_rows // 2), down_rows // 2, 0)
-    w_qkv = shard_gather(qkv_block)
-    gains = lax.all_gather(
-        jnp.stack([attn_gain, query_gain, key_gain, ffn_gain]), "shard", axis=1, tiled=True
-    ).astype(F32)
-    router_w = shard_gather(w_router)
-    w_out_part = shard_gather(output_block).reshape(n_shard, quarter, width)
-    w_gu = shard_gather(gate_up_block)
-    w_dn = shard_gather(down_block)
-    gain_one, gain_two = gains[0], gains[3]
-    gain_query = lax.dynamic_slice_in_dim(gains[1:2], rep * part, part, 1)
-    gain_key = lax.dynamic_slice_in_dim(gains[2:3], rep * part, part, 1)
-    output_w = jnp.stack(in_order(rep_gather(w_out_part), rep), 1).reshape(width, width)
-
-    hidden_all = jnp.concatenate(rep_gather(hidden_in), 0)
+    small_block = jnp.concatenate(
+        [w_router, jnp.stack([attn_gain, query_gain, key_gain, ffn_gain], 1)]
+        + [jnp.zeros((my_rows, 128 - 4 - routed), BF16)],
+        1,
+    )
+
     docs_all = jnp.concatenate(rep_gather(doc_ids), 0)
-    slots = slot_rows[0].reshape(experts * cap)
-    select = (slots[:, None] == jnp.arange(length, dtype=jnp.int32)[None, :]).astype(BF16)
-    upstream = out_grad.astype(F32)
-
-    def to_experts(x):
-        own = lax.dynamic_index_in_dim(x, core, 0, keepdims=False)
-        other = lax.dynamic_index_in_dim(x, 1 - core, 0, keepdims=False)
-        pair = jnp.stack([own, swap(other, 1)])
-        return jnp.concatenate([pair, swap(pair, 2)], 0)
-
-    def from_experts(x, send):
-        pair = x[:2] + swap(x[2:].astype(send), 2).astype(F32)
-        other = swap(pair[1].astype(send), 1).astype(F32)
-        first = jnp.where(core == 0, pair[0], other)
-        return jnp.stack([first, jnp.where(core == 0, other, pair[0])])
-
-    def add_slots(x):
-        high, low = split_sum(x.reshape(experts * cap, width))
-        return dot(select, high, ((0,), (0,))) + dot(select, low, ((0,), (0,)))
-
-    slot_upstream = to_experts(dot(select, out_grad).astype(BF16).reshape(experts, cap, width))
-
-    normed_scale = rms_scale(hidden_all.astype(F32))
-    normed = (hidden_all.astype(F32) * normed_scale * gain_one).astype(BF16)
     before = docs_all[:, None, :] < docs_all[:, :, None]
     starts = jnp.sum(before.astype(jnp.int32), -1)
     places = (jnp.arange(length, dtype=jnp.int32)[None, :] - starts).astype(F32).reshape(-1)
@@ -330,13 +404,71 @@
     cosine, sine = jnp.cos(angles), jnp.sin(angles)
     doc_col = docs_all.reshape(-1, 1)
     doc_row = docs_all.reshape(4, 1, length)
-
+    slots = slot_rows[0].reshape(experts * cap)
+    select = (slots[:, None] == jnp.arange(length, dtype=jnp.int32)[None, :]).astype(BF16)
+    own_upstream = dot(select, out_grad).astype(BF16)
+
+    pieces, (hidden_side, cosine, sine, own_upstream) = ring_gather(
+        jnp.concatenate([qkv_block, small_block], 1),
+        n_shard,
+        (swap(hidden_in, 2), cosine, sine, own_upstream),
+    )
+    piece, k, first = pieces[-3]
+    piece, output_block, gate_up_block, down_block = tie(
+        piece, output_block, gate_up_block, down_block
+    )
+    pieces[-3] = (piece, k, first)
+    hidden_all = jnp.concatenate(
+        [hidden_in, swap(hidden_in, 1), hidden_side, swap(hidden_side, 1)], 0
+    )
+    normed_scale = rms_scale(hidden_all.astype(F32))
+    piece, k, first = pieces[-1]
+    piece, normed_scale = tie(piece, normed_scale)
+    pieces[-1] = (piece, k, first)
+    ids = ring_ids(n_shard, shard)
+    starts = jnp.stack([ids[k] * my_rows + first for _, k, first in pieces])
+    w_qkv, small_w = place_rows([piece for piece, _, _ in pieces], starts, width, 3 * part)
+    router_w = small_w[:, :routed]
+    gains = small_w[:, routed : routed + 4].T.astype(F32)
+    w_out_part = shard_gather(output_block).reshape(n_shard, quarter, width)
+    w_gu = shard_gather(gate_up_block)
+    w_dn = shard_gather(down_block)
+    gain_one, gain_two = gains[0], gains[3]
+    gain_query = lax.dynamic_slice_in_dim(gains[1:2], rep * part, part, 1)
+    gain_key = lax.dynamic_slice_in_dim(gains[2:3], rep * part, part, 1)
+
+    upstream = out_grad.astype(F32)
+
+    def to_experts(x):
+        own = lax.dynamic_index_in_dim(x, core, 0, keepdims=False)
+        other = lax.dynamic_index_in_dim(x, 1 - core, 0, keepdims=False)
+        pair = jnp.stack([own, swap(other, 1)])
+        return jnp.concatenate([pair, swap(pair, 2)], 0)
+
+    def send_side(x, send):
+        return swap(x[2:].astype(send), 2)
+
+    def from_experts(x, there, send):
+        pair = x[:2] + there.astype(F32)
+        other = swap(pair[1].astype(send), 1).astype(F32)
+        first = jnp.where(core == 0, pair[0], other)
+        return jnp.stack([first, jnp.where(core == 0, other, pair[0])])
+
+    def add_slots(x):
+        high, low = split_sum(x.reshape(experts * cap, width))
+        return dot(select, high, ((0,), (0,))) + dot(select, low, ((0,), (0,)))
+
+    slot_upstream = to_experts(own_upstream.reshape(experts, cap, width))
+    normed = (hidden_all.astype(F32) * normed_scale * gain_one).astype(BF16)
+    w_qkv, slot_upstream = tie(w_qkv, slot_upstream)
     qkv = dot(normed, w_qkv)
     query_raw, key_raw = qkv[:, :part], qkv[:, part : 2 * part]
     squares = jnp.stack([jnp.sum(query_raw * query_raw, -1), jnp.sum(key_raw * key_raw, -1)], -1)
     squares = rep_sum(squares.reshape(4, length, 2)).reshape(-1, 2)
     scales = lax.rsqrt(squares / width + EPSILON)
     query_scale, key_scale = scales[:, :1], scales[:, 1:]
+    scales, w_out_part = tie(scales, w_out_part)
+    out_pieces = in_order(rep_gather(w_out_part), rep)
     mixed_heads, queries, keys, values = attend(
         qkv,
         query_scale,
@@ -352,6 +484,8 @@
     )
     blocks = mixed_heads.reshape(4, length, part)
     from_side = swap(blocks[2:], 2)
+    from_side, w_gu, *out_pieces = tie(from_side, w_gu, *out_pieces)
+    output_w = jnp.stack(out_pieces, 1).reshape(width, width)
     mixed = jnp.concatenate(
         in_order([blocks[0], swap(blocks[1], 1), from_side[0], swap(from_side[1], 1)], rep), 1
     )
@@ -376,19 +510,22 @@
     swished = gate_part * sigma
     activated = (swished * up_part).astype(BF16)
     returned = dot(activated, w_dn).reshape(4, cap, width)
-    slot_gate_grad = from_experts(jnp.sum(returned * slot_upstream.astype(F32), -1), F32)
+    slot_gate_grad = jnp.sum(returned * slot_upstream.astype(F32), -1)
+    slot_gate_grad = from_experts(slot_gate_grad, send_side(slot_gate_grad, F32), F32)
     returned_grad = (slot_gates[:, :, None] * slot_upstream.astype(F32)).astype(BF16)
     returned_grad = returned_grad.reshape(4 * cap, width)
     act_grad = dot(returned_grad, w_dn, ((1,), (1,)))
     gate_grad = act_grad * up_part * sigma * (1.0 + gate_part * (1.0 - sigma))
     gate_up_grad = jnp.concatenate([gate_grad.astype(BF16), (act_grad * swished).astype(BF16)], 1)
     slot_input_grad = dot(gate_up_grad, w_gu, ((1,), (1,))).reshape(4, cap, width)
-    slot_input_grad = from_experts(slot_input_grad, BF16)
-    down_owned = shard_scatter(dot(activated, returned_grad, ((0,), (0,))).astype(BF16))
-    gate_up_owned = shard_scatter(dot(slot_inputs, gate_up_grad, ((0,), (0,))).astype(BF16))
-    own_gates = jnp.sum(select_wide * window.T[:, None, :], -1)
-    returned = from_experts(returned, BF16)
-    output = (residual + add_slots(own_gates[:, :, None] * returned)).astype(BF16)
+    down_w_grad = dot(activated, returned_grad, ((0,), (0,))).astype(BF16)
+    gate_up_w_grad = dot(slot_inputs, gate_up_grad, ((0,), (0,))).astype(BF16)
+    there, down_w_grad, gate_up_w_grad = tie(
+        send_side(slot_input_grad, BF16), down_w_grad, gate_up_w_grad
+    )
+    slot_input_grad = from_experts(slot_input_grad, there, BF16)
+    gate_up_owned = shard_scatter(gate_up_w_grad)
+    down_owned = shard_scatter(down_w_grad)
 
     window_grad = jnp.sum(select_wide * slot_gate_grad[:, :, None], 1).T
     chosen_grad = jnp.concatenate(
@@ -397,7 +534,7 @@
     logits_grad = (
         probs_all * (chosen_grad - jnp.sum(probs_all * chosen_grad, -1, keepdims=True))
     ).astype(BF16)
-    router_grad = dot(logits_grad, inner, ((0,), (0,)))
+    router_grad = dot(inner, logits_grad, ((0,), (0,)))
     inner_grad = add_slots(slot_input_grad) + dot(logits_grad, router_w, ((1,), (1,)))
     residual_part, gain_two_grad = norm_back(residual, scale_two, gain_two, inner_grad)
     residual_grad = upstream + residual_part
@@ -405,23 +542,30 @@
     mixed_grad = dot(branch_grad, output_w, ((1,), (1,))).astype(BF16)
     piece = lambda j: lax.dynamic_slice_in_dim(mixed_grad, (rep ^ j) * part, part, 1)
     from_side = swap(jnp.stack([piece(2), piece(3)]), 2)
-    grads = jnp.concatenate([piece(0), swap(piece(1), 1), from_side[0], swap(from_side[1], 1)], 0)
+    from_core, branch_grad = tie(swap(piece(1), 1), branch_grad)
     out_w_grad = dot(mixed, branch_grad, ((0,), (0,))).astype(BF16)
     out_w_grad = out_w_grad.reshape(n_shard, 2, 2, quarter, width)
     at = lambda x, i, axis: lax.dynamic_index_in_dim(x, i, axis, keepdims=False)
     out_w_grad = at(out_w_grad, core, 2).astype(F32) + swap(at(out_w_grad, 1 - core, 2), 1)
     out_w_grad = out_w_grad.astype(BF16)
-    out_w_grad = at(out_w_grad, side, 1).astype(F32) + swap(at(out_w_grad, 1 - side, 1), 2)
-    out_owned = shard_scatter(out_w_grad.astype(BF16).reshape(n_shard * quarter, width))
+    from_side, out_w_grad, returned = tie(from_side, out_w_grad, returned)
+    grads = jnp.concatenate([piece(0), from_core, from_side[0], swap(from_side[1], 1)], 0)
+    returned_there = send_side(returned, BF16)
 
     query_grad, key_grad, value_grad = attend_back(
         queries, keys, values, grads, cosine, sine, doc_col, doc_row, heads, dim
     )
+    value_grad, returned_there = tie(value_grad, returned_there)
+    own_gates = jnp.sum(select_wide * window.T[:, None, :], -1)
+    returned = from_experts(returned, returned_there, BF16)
+    output = (residual + add_slots(own_gates[:, :, None] * returned)).astype(BF16)
     weighted_q, weighted_k = query_grad * gain_query, key_grad * gain_key
     means = jnp.stack(
         [jnp.sum(weighted_q * query_raw, -1), jnp.sum(weighted_k * key_raw, -1)], -1
     )
     means = rep_sum(means.reshape(4, length, 2)).reshape(-1, 2) / width
+    means, out_w_grad, gate_up_owned = tie(means, out_w_grad, gate_up_owned)
+    out_there = swap(at(out_w_grad, 1 - side, 1), 2)
     gain_query_grad = jnp.sum(query_grad * query_raw * query_scale, 0)
     gain_key_grad = jnp.sum(key_grad * key_raw * key_scale, 0)
     query_raw_grad = query_scale * weighted_q - query_raw * query_scale**3 * means[:, :1]
@@ -429,39 +573,56 @@
     qkv_grad = jnp.concatenate(
         [query_raw_grad.astype(BF16), key_raw_grad.astype(BF16), value_grad], 1
     )
-    qkv_owned = shard_scatter(dot(normed, qkv_grad, ((0,), (0,))).astype(BF16))
-    normed_grad = dot(qkv_grad, w_qkv, ((1,), (1,)))
-    gain_one_grad = jnp.sum(normed_grad * hidden_all.astype(F32) * normed_scale, 0)
-    normed_grad = normed_grad.reshape(4, length, width)
-    from_core = swap(normed_grad[1::2].astype(BF16), 1).astype(F32)
-    pair_two = (normed_grad[2] + from_core[1]).astype(BF16)
-    normed_grad = normed_grad[0] + from_core[0] + swap(pair_two, 2).astype(F32)
+    qkv_w_grad = dot(normed, qkv_grad, ((0,), (0,))).astype(BF16)
+    qkv_grad, qkv_w_grad = tie(qkv_grad, qkv_w_grad)
+    place = lambda g: lax.dynamic_update_slice_in_dim(
+        jnp.zeros((width,), F32), g, rep * part, 0
+    )
+    small = jnp.stack([gain_two_grad, place(gain_query_grad), place(gain_key_grad)], 1)
+    small = jnp.concatenate(
+        [router_grad, small, jnp.zeros((width, 128 - 3 - routed), F32)], 1
+    ).astype(BF16)
+    slot_grads = qkv_grad.reshape(4, length, 3 * part)
+    back = lambda j: dot(slot_grads[j], w_qkv, ((1,), (1,)))
+    due = (
+        lambda: (back(1), back(3), out_there),
+        lambda one, three, there: (
+            back(2),
+            swap(jnp.stack([one, three]).astype(BF16), 1),
+            (at(out_w_grad, side, 1).astype(F32) + there).astype(BF16),
+        ),
+        lambda two, from_core, total: (
+            back(0) + from_core[0].astype(F32),
+            (two + from_core[1].astype(F32)).astype(BF16),
+            total,
+            down_owned,
+        ),
+        lambda zero, two, total, down: (
+            zero,
+            swap(two, 2),
+            shard_scatter(total.reshape(n_shard * quarter, width)),
+            down,
+        ),
+    )
+    qkv_owned, (normed_grad, from_side, out_owned, down_owned) = ring_scatter(
+        [qkv_w_grad, small], n_shard, shard, due
+    )
+    normed_grad = normed_grad + from_side.astype(F32)
     weighted = normed_grad * gain_one
     scale_one = normed_scale[:length]
     inner_mean = jnp.mean(weighted * hidden, -1, keepdims=True)
     hidden_part = scale_one * weighted - hidden * scale_one * scale_one * scale_one * inner_mean
     input_grad = residual_grad + hidden_part
 
-    place = lambda g: lax.dynamic_update_slice_in_dim(
-        jnp.zeros((1, width), F32), g[None], rep * part, 1
-    )
-    small = jnp.concatenate(
-        [
-            router_grad,
-            gain_one_grad[None],
-            place(gain_query_grad),
-            place(gain_key_grad),
-            gain_two_grad[None],
-            jnp.zeros((4, width), F32),
-        ],
-        0,
-    )
-    small = lax.psum(small, ("shard", "rep"))
-    small = lax.dynamic_slice_in_dim(small, shard * my_rows, my_rows, 1)
     qkv_pieces = in_order(rep_gather(qkv_owned.astype(BF16)), rep)
     spread = lambda i: jnp.concatenate(
         [p[:, i * part : (i + 1) * part] for p in qkv_pieces], 1
     ).astype(F32)
+    grads_qkv = [spread(i) for i in range(3)]
+    small = sum(p[:, 3 * part :].astype(F32) for p in qkv_pieces)
+    gain_one_grad = sum(
+        jnp.sum(w.astype(F32) * g, 1) for w, g in zip((w_query, w_key, w_value), grads_qkv)
+    ) / attn_gain.astype(F32)
     out_full = jnp.concatenate(in_order(rep_gather(out_owned.astype(BF16)), rep), 0).astype(F32)
     gu_pieces = in_order(rep_gather(gate_up_owned.astype(BF16)), rep)
     dn_pieces = in_order(rep_gather(down_owned.astype(BF16)), rep)
@@ -479,15 +640,13 @@
     return (
         output,
         input_grad,
-        small[routed],
-        spread(0),
-        spread(1),
-        spread(2),
-        small[routed + 1],
-        small[routed + 2],
+        gain_one_grad,
+        *grads_qkv,
+        small[:, routed + 1],
+        small[:, routed + 2],
         out_full,
-        small[routed + 3],
-        small[:routed].T,
+        small[:, routed],
+        small[:, :routed],
         join(0),
         join(1),
         down_full,

time: 983 us -> 795 us (0.81)
  waiting for transfers between devices: 513 us -> 334 us
  blocking collectives: 59.2 us -> 0 us
  local copies, waits for them, and re-layouts: 52.3 us -> 76.9 us
  starting transfers between devices: 24.9 us -> 35.6 us
    reduce_scatter x4 -> x3, waiting for transfers between devices: 222 us -> 23.8 us  [shard_scatter(): lax.psum_scatter(x, 'shard', scatter_dimension=0, tiled=True).astype(F32)]
    ppermute x0 -> x16, waiting for transfers between devices: none -> 84.1 us  [ring_step(): lax.ppermute(x, 'shard', [(b, a) for a, b in pairs] if back else pairs)]
    all_gather x4 -> x3, waiting for transfers between devices: 61.3 us -> 0.04 us  [shard_gather(): return lax.all_gather(x, 'shard', axis=0, tiled=True)]
    all_gather x2 -> x0, blocking collectives: 59.2 us -> none  [the longest x1 31.8 us: shard_gather(): return lax.all_gather(x, 'shard', axis=0, tiled=True)]
    ppermute x0 -> x16, starting transfers between devices: none -> 16.7 us  [ring_step(): lax.ppermute(x, 'shard', [(b, a) for a, b in pairs] if back else pairs)]
    dynamic_slice x0 -> x16, local copies, waits for them, and re-layouts: none -> 11.2 us  [the longest x13 5.87 us: ring_scatter(): lax.dynamic_slice_in_dim(x, ids[k % n] * rows + first, size, 0)]
    unnamed x153 -> x209, local copies, waits for them, and re-layouts: 16.5 us -> 24.4 us
    dot_general x31 -> x34, matrix products: 129 us -> 123 us  [dot(): return lax.dot_general(a, b, (dims, ((), ())), preferred_element_type=F32)]
  transfers between devices with their start and end apart: 56 -> 69, of which waited for: 24 -> 36; matrix products, arithmetic and copies ran while one was open for 25% -> 35% of each run, Pallas kernels for 7% -> 10%
where the time goes in v2:
time: 795 us; the launch traced here: 789 us
  waiting for transfers between devices  334 us (42%)
  matrix products  123 us (15%)
  other arithmetic  117 us (15%)
  Pallas kernels  80.1 us (10%)
  local copies, waits for them, and re-layouts  76.9 us (10%)
  starting transfers between devices  35.6 us (4%)
  between operations  21.5 us (3%)
    ppermute x47, waiting for transfers between devices, swap(): return lax.ppermute(x, 'rep', [(i, i ^ mask) for i in range(4)])  226 us
    dot_general x34, matrix products, dot(): return lax.dot_general(a, b, (dims, ((), ())), preferred_element_type=F32)  123 us
    ppermute x16, waiting for transfers between devices, ring_step(): lax.ppermute(x, 'shard', [(b, a) for a, b in pairs] if back else pairs)  84.1 us
    pallas_call x1, Pallas kernels, attend_back(): pl.pallas_call(functools.partial(attend_back_kernel, dim ** (-0.5)), grid...  38.6 us
    pallas_call x1, Pallas kernels, attend(): pl.pallas_call(functools.partial(attend_kernel, dim ** (-0.5)), grid=(tok...  35 us
    unnamed x209, local copies, waits for them, and re-layouts  24.4 us
    reduce_scatter x3, waiting for transfers between devices, shard_scatter(): lax.psum_scatter(x, 'shard', scatter_dimension=0, tiled=True).astype(F32)  23.8 us
    ppermute x47, starting transfers between devices, swap(): return lax.ppermute(x, 'rep', [(i, i ^ mask) for i in range(4)])  18.6 us
  transfers between devices with their start and end apart: 69, of which 36 were waited for; matrix products, arithmetic and copies ran while one was open for 35% of the time, Pallas kernels for 10%

profile of v2, /device:TPU:0, one launch (start us, length us, event | category | flops | bytes accessed | tf_op | source)
XLA Modules:
  0.0 788.9 jit_solution(7660343657245804311)
XLA Ops:
  25.4 14.3 %collective-permute-done.2.refs_2_ = bf16[256,1664]{1,0:T(8,128)(2,1)} collective-permute-done((bf16[256,1664]{1,0:T(8,128)(2,1)}, bf16[256,1664]{1,0:T(8,128)(2,1)}, u32[]{:S(2)}, u32[]{:S(2)}) %collective-permute-start.2) | collective-permute-done | bytes 852000 | tf_op jit(solution)/shard_map/ppermute | solution.py:234
  47.7 13.3 %collective-permute-done.3.refs_3_ = bf16[256,1664]{1,0:T(8,128)(2,1)S(1)} collective-permute-done((bf16[256,1664]{1,0:T(8,128)(2,1)}, bf16[256,1664]{1,0:T(8,128)(2,1)S(1)}, u32[]{:S(2)}, u32[]{:S(2)}) %collective-permute-start.3) | collective-permute-done | bytes 852000 | tf_op jit(solution)/shard_map/ppermute | solution.py:234
  70.4 10.9 %collective-permute-done.5.refs_5_ = bf16[256,1664]{1,0:T(8,128)(2,1)S(1)} collective-permute-done((bf16[256,1664]{1,0:T(8,128)(2,1)}, bf16[256,1664]{1,0:T(8,128)(2,1)S(1)}, u32[]{:S(2)}, u32[]{:S(2)}) %collective-permute-start.5) | collective-permute-done | bytes 852000 | tf_op jit(solution)/shard_map/ppermute | solution.py:234
  99.9 11.7 %collective-permute-done.15 = bf16[2,128,2048]{2,1,0:T(8,128)(2,1)} collective-permute-done((bf16[2,128,2048]{2,1,0:T(8,128)(2,1)}, bf16[2,128,2048]{2,1,0:T(8,128)(2,1)}, u32[]{:S(2)}, u32[]{:S(2)}) %collective-permute-start.15) | collective-permute-done | bytes 1048608 | tf_op jit(solution)/shard_map/ppermute | solution.py:35
  127.4 22.7 %fusion.15.q_ref.k_ref.v_ref = f32[2048,1536]{1,0:T(8,128)} fusion(bf16[2048,1536]{1,0:T(8,128)(2,1)} %get-tuple-element.102, f32[2048]{0:T(1024)S(1)} %bitcast.281, f32[2048]{0:T(1024)S(1)} %add_rsqrt_fusion, bf16[512,2048]{1,0:T(8,128)(2,1)} %collective-permute-done.11, bf16[512,2048]{1,0:T(8,128)(2,1)} %collective-permute-done.7, ...), kind=kOutput, calls=%fused_computation.56 | convolution fusion | flops 12931039232 | bytes 27279360 | tf_op jit(solution)/shard_map/dot_general | solution.py:31
  162.7 46.7 %collective-permute-done.19 = bf16[8,64,2048]{2,1,0:T(8,128)(2,1)S(1)} collective-permute-done((bf16[8,64,2048]{2,1,0:T(8,128)(2,1)}, bf16[8,64,2048]{2,1,0:T(8,128)(2,1)S(1)}, u32[]{:S(2)}, u32[]{:S(2)}) %collective-permute-start.19) | collective-permute-done | bytes 2097184 | tf_op jit(solution)/shard_map/ppermute | solution.py:35
  215.1 35.0 %attend.1 = (bf16[2048,512]{1,0:T(8,128)(2,1)}, bf16[2048,512]{1,0:T(8,128)(2,1)}, bf16[2048,512]{1,0:T(8,128)(2,1)}, bf16[2048,512]{1,0:T(8,128)(2,1)}) custom-call(f32[2048,1536]{1,0:T(8,128)} %fusion.15.q_ref.k_ref.v_ref, f32[2048,1536]{1,0:T(8,128)} %fusion.15.q_ref.k_ref.v_ref, f32[2048,1536]{1,0:T(8,128)} %fusion.15.q_ref.k_ref.v_ref, ...), custom_call_target="tpu_custom_call" | custom-call | flops 2147483648 | bytes 20971520 | tf_op jit(solution)/shard_map/attend/pallas_call | solution.py:182
  260.6 17.5 %collective-permute-done.18 = bf16[2,512,512]{2,1,0:T(8,128)(2,1)S(1)} collective-permute-done((bf16[2,512,512]{2,1,0:T(8,128)(2,1)}, bf16[2,512,512]{2,1,0:T(8,128)(2,1)S(1)}, u32[]{:S(2)}, u32[]{:S(2)}) %collective-permute-start.18) | collective-permute-done | bytes 1048608 | tf_op jit(solution)/shard_map/ppermute | solution.py:35
  285.0 7.8 multiply_reduce_fusion.6
  300.8 24.6 %collective-permute-done.27 = bf16[2,128,2048]{2,1,0:T(8,128)(2,1)} collective-permute-done((bf16[2,128,2048]{2,1,0:T(8,128)(2,1)}, bf16[2,128,2048]{2,1,0:T(8,128)(2,1)}, u32[]{:S(2)}, u32[]{:S(2)}) %collective-permute-start.27) | collective-permute-done | bytes 1048608 | tf_op jit(solution)/shard_map/ppermute | solution.py:35
  364.4 13.8 %collective-permute-done.28 = bf16[2,128,2048]{2,1,0:T(8,128)(2,1)} collective-permute-done((bf16[2,128,2048]{2,1,0:T(8,128)(2,1)}, bf16[2,128,2048]{2,1,0:T(8,128)(2,1)}, u32[]{:S(2)}, u32[]{:S(2)}) %collective-permute-start.28) | collective-permute-done | bytes 1048608 | tf_op jit(solution)/shard_map/ppermute | solution.py:35
  401.6 7.2 convolution_convert_fusion
  424.7 14.7 %collective-permute-done.32 = bf16[2,512,512]{2,1,0:T(8,128)(2,1)S(1)} collective-permute-done((bf16[2,512,512]{2,1,0:T(8,128)(2,1)S(1)}, bf16[2,512,512]{2,1,0:T(8,128)(2,1)S(1)}, u32[]{:S(2)}, u32[]{:S(2)}) %collective-permute-start.32) | collective-permute-done | bytes 1048608 | tf_op jit(solution)/shard_map/ppermute | solution.py:35
  448.5 38.6 %attend_back.1 = (f32[2048,512]{1,0:T(8,128)}, f32[2048,512]{1,0:T(8,128)}, bf16[2048,512]{1,0:T(8,128)(2,1)}) custom-call(bf16[2048,512]{1,0:T(8,128)(2,1)} %get-tuple-element.120.queries, bf16[2048,512]{1,0:T(8,128)(2,1)} %get-tuple-element.121.keys, bf16[2048,512]{1,0:T(8,128)(2,1)} %get-tuple-element.122.values, ...), custom_call_target="tpu_custom_call" | custom-call | flops 5368709120 | bytes 18874368 | tf_op jit(solution)/shard_map/attend_back/pallas_call | solution.py:205
  487.1 7.1 multiply_reduce_fusion.3
  508.9 7.4 subtract_convert_fusion.1
  520.7 19.7 %convolution_convert_fusion.1 = bf16[2048,1536]{1,0:T(8,128)(2,1)} fusion(f32[2048]{0:T(1024)S(1)} %bitcast.282, f32[2048]{0:T(1024)S(1)} %copy-done.83, bf16[2048,512]{1,0:T(8,128)(2,1)} %get-tuple-element.132, bf16[2048,512]{1,0:T(8,128)(2,1)} %copy-done.16, bf16[2048,512]{1,0:T(8,128)(2,1)S(1)} %get-tuple-element.259, ...), kind=kOutput, calls=%fused_computation.11 | convolution fusion | flops 12953059328 | bytes 20987904 | tf_op jit(solution)/shard_map/dot_general | solution.py:31
  557.3 34.1 %collective-permute-done.42 = bf16[8,64,2048]{2,1,0:T(8,128)(2,1)S(1)} collective-permute-done((bf16[8,64,2048]{2,1,0:T(8,128)(2,1)S(1)}, bf16[8,64,2048]{2,1,0:T(8,128)(2,1)S(1)}, u32[]{:S(2)}, u32[]{:S(2)}) %collective-permute-start.42) | collective-permute-done | bytes 2097184 | tf_op jit(solution)/shard_map/ppermute | solution.py:35
  611.5 7.9 %collective-permute-done.43 = bf16[256,1664]{1,0:T(8,128)(2,1)} collective-permute-done((bf16[256,1664]{1,0:T(8,128)(2,1)}, bf16[256,1664]{1,0:T(8,128)(2,1)}, u32[]{:S(2)}, u32[]{:S(2)}) %collective-permute-start.43) | collective-permute-done | bytes 852000 | tf_op jit(solution)/shard_map/ppermute | solution.py:234
  629.0 7.9 %convert_add_fusion.3 = f32[512,2048]{1,0:T(8,128)} fusion(bf16[2,512,2048]{2,1,0:T(8,128)(2,1)S(1)} %collective-permute-done.45, bf16[2048,1536]{1,0:T(8,128)(2,1)} %get-tuple-element.102, bf16[2048,1536]{1,0:T(8,128)(2,1)S(1)} %copy-done.18), kind=kOutput, calls=%fused_computation.30 | convolution fusion | flops 3223322624 | bytes 14155776 | tf_op jit(solution)/shard_map/dot_general | solution.py:31
  665.5 25.2 %collective-permute-done.49 = bf16[256,1664]{1,0:T(8,128)(2,1)S(1)} collective-permute-done((bf16[256,1664]{1,0:T(8,128)(2,1)S(1)}, bf16[256,1664]{1,0:T(8,128)(2,1)S(1)}, u32[]{:S(2)}, u32[]{:S(2)}) %collective-permute-start.49) | collective-permute-done | bytes 852000 | tf_op jit(solution)/shard_map/ppermute | solution.py:234
  692.5 7.3 collective-permute-done.50
  699.8 23.8 %reduce-scatter.8.cloned.1.call-done = bf16[64,2048]{1,0:T(8,128)(2,1)} async-done(((bf16[512,2048]{1,0:T(8,128)(2,1)}), bf16[64,2048]{1,0:T(8,128)(2,1)}) %reduce-scatter.8.cloned.1.call-update) | async-done | bytes 262160 | tf_op jit(solution)/shard_map/reduce_scatter | solution.py:334
  747.0 19.4 %collective-permute-done.51 = bf16[256,1664]{1,0:T(8,128)(2,1)S(1)} collective-permute-done((bf16[256,1664]{1,0:T(8,128)(2,1)S(1)}, bf16[256,1664]{1,0:T(8,128)(2,1)S(1)}, u32[]{:S(2)}, u32[]{:S(2)}) %collective-permute-start.51) | collective-permute-done | bytes 852000 | tf_op jit(solution)/shard_map/ppermute | solution.py:35
  (548 shorter events, 329.0 us)
Async XLA Ops:
  7.2 154.9 %all-gather.6.cloned.1.call-start = ((), (), s32[]{:S(2)}) async-start(), calls=%async_computation.4 | async-start | bytes 2359296 | tf_op jit(solution)/shard_map/all_gather | solution.py:330
  7.2 39.3 %collective-permute-start.8 = (s32[1,512]{1,0:T(1,128)}, s32[1,512]{1,0:T(1,128)S(1)}, u32[]{:S(2)}, u32[]{:S(2)}) collective-permute-start(s32[1,512]{1,0:T(1,128)} %param.22), channel_id=1, source_target_pairs={{0,1},{1,0},{2,3},{3,2},{4,5},{5,4},{6,7},{7,6},{8,9},{9,8},{10,11... | collective-permute-start | bytes 6152 | tf_op jit(solution)/shard_map/ppermute | solution.py:35
  7.8 38.6 %collective-permute-start.9 = (s32[1,512]{1,0:T(1,128)}, s32[1,512]{1,0:T(1,128)S(1)}, u32[]{:S(2)}, u32[]{:S(2)}) collective-permute-start(s32[1,512]{1,0:T(1,128)} %param.22), channel_id=1, source_target_pairs={{0,2},{1,3},{2,0},{3,1},{4,6},{5,7},{6,4},{7,5},{8,10},{9,11},{10,... | collective-permute-start | bytes 6152 | tf_op jit(solution)/shard_map/ppermute | solution.py:35
  20.4 61.5 %collective-permute-start.7 = (bf16[512,2048]{1,0:T(8,128)(2,1)}, bf16[512,2048]{1,0:T(8,128)(2,1)}, u32[]{:S(2)}, u32[]{:S(2)}) collective-permute-start(bf16[512,2048]{1,0:T(8,128)(2,1)} %param.21), channel_id=1, source_target_pairs={{0,2},{1,3},{2,0},{3,1},{4,6},{5,7},{6,4},{7,5},{8,10},{9,11},{10,... | collective-permute-start | bytes 6291464 | tf_op jit(solution)/shard_map/ppermute | solution.py:35
  81.9 196.2 %all-gather.4.cloned.1.call-start = ((), (), s32[]{:S(2)}) async-start(), calls=%async_computation.3 | async-start | bytes 4718592 | tf_op jit(solution)/shard_map/all_gather | solution.py:330
  82.3 32.2 %collective-permute-start = (bf16[512,2048]{1,0:T(8,128)(2,1)}, bf16[512,2048]{1,0:T(8,128)(2,1)S(1)}, u32[]{:S(2)}, u32[]{:S(2)}) collective-permute-start(bf16[512,2048]{1,0:T(8,128)(2,1)} %param.21), channel_id=1, source_target_pairs={{0,1},{1,0},{2,3},{3,2},{4,5},{5,4},{6,7},{7,6},{8,9},{9,8},{10,11... | collective-permute-start | bytes 6291464 | tf_op jit(solution)/shard_map/ppermute | solution.py:35
  82.8 31.7 %collective-permute-start.11 = (bf16[512,2048]{1,0:T(8,128)(2,1)}, bf16[512,2048]{1,0:T(8,128)(2,1)}, u32[]{:S(2)}, u32[]{:S(2)}) collective-permute-start(bf16[512,2048]{1,0:T(8,128)(2,1)} %collective-permute-done.7), channel_id=1, source_target_pairs={{0,1},{1,0},{2,3},{3,2},{4,5},{5,4},{6,7},{7,6},{8,9},{9,8},{10,11... | collective-permute-start | bytes 6291464 | tf_op jit(solution)/shard_map/ppermute | solution.py:35
  99.8 231.1 %all-gather.8.cloned.1.call-start = ((), (), s32[]{:S(2)}) async-start(), calls=%async_computation.5 | async-start | bytes 2359296 | tf_op jit(solution)/shard_map/all_gather | solution.py:330
  162.1 47.2 %collective-permute-start.19 = (bf16[8,64,2048]{2,1,0:T(8,128)(2,1)}, bf16[8,64,2048]{2,1,0:T(8,128)(2,1)S(1)}, u32[]{:S(2)}, u32[]{:S(2)}) collective-permute-start(bf16[8,64,2048]{2,1,0:T(8,128)(2,1)} %bitcast.255), channel_id=1, source_target_pairs={{0,2},{1,3},{2,0},{3,1},{4,6},{5,7},{6,4},{7,5},{8,10},{9,11},{10,... | collective-permute-start | bytes 6291464 | tf_op jit(solution)/shard_map/ppermute | solution.py:35
  162.7 92.3 %collective-permute-start.21 = (bf16[8,64,2048]{2,1,0:T(8,128)(2,1)}, bf16[8,64,2048]{2,1,0:T(8,128)(2,1)}, u32[]{:S(2)}, u32[]{:S(2)}) collective-permute-start(bf16[8,64,2048]{2,1,0:T(8,128)(2,1)} %bitcast.256), channel_id=1, source_target_pairs={{0,1},{1,0},{2,3},{3,2},{4,5},{5,4},{6,7},{7,6},{8,9},{9,8},{10,11... | collective-permute-start | bytes 6291464 | tf_op jit(solution)/shard_map/ppermute | solution.py:35
  209.4 45.6 %collective-permute-start.20 = (bf16[8,64,2048]{2,1,0:T(8,128)(2,1)S(1)}, bf16[8,64,2048]{2,1,0:T(8,128)(2,1)}, u32[]{:S(2)}, u32[]{:S(2)}) collective-permute-start(bf16[8,64,2048]{2,1,0:T(8,128)(2,1)S(1)} %collective-permute-done.19), channel_id=1, source_target_pairs={{0,1},{1,0},{2,3},{3,2},{4,5},{5,4},{6,7},{7,6},{8,9},{9,8},{10,11... | collective-permute-start | bytes 6291464 | tf_op jit(solution)/shard_map/ppermute | solution.py:35
  252.9 255.2 %reduce-scatter.4.cloned.1.call-start = ((), (), s32[]{:S(2)}) async-start(), calls=%async_computation.6 | async-start | bytes 4718592 | tf_op jit(solution)/shard_map/reduce_scatter | solution.py:334
  381.9 255.1 %reduce-scatter.6.cloned.1.call-start = ((), (), s32[]{:S(2)}) async-start(), calls=%async_computation.7 | async-start | bytes 2359296 | tf_op jit(solution)/shard_map/reduce_scatter | solution.py:334
  442.7 280.9 %reduce-scatter.8.cloned.1.call-start = ((), (), s32[]{:S(2)}) async-start(), calls=%async_computation.8 | async-start | bytes 2359296 | tf_op jit(solution)/shard_map/reduce_scatter | solution.py:334
  445.5 56.6 %collective-permute-start.36 = (bf16[2,128,2048]{2,1,0:T(8,128)(2,1)}, bf16[2,128,2048]{2,1,0:T(8,128)(2,1)}, u32[]{:S(2)}, u32[]{:S(2)}) collective-permute-start(bf16[2,128,2048]{2,1,0:T(8,128)(2,1)} %slice.643), channel_id=1, source_target_pairs={{0,2},{1,3},{2,0},{3,1},{4,6},{5,7},{6,4},{7,5},{8,10},{9,11},{10,... | collective-permute-start | bytes 3145736 | tf_op jit(solution)/shard_map/ppermute | solution.py:35
  543.7 47.7 %collective-permute-start.42 = (bf16[8,64,2048]{2,1,0:T(8,128)(2,1)S(1)}, bf16[8,64,2048]{2,1,0:T(8,128)(2,1)S(1)}, u32[]{:S(2)}, u32[]{:S(2)}) collective-permute-start(bf16[8,64,2048]{2,1,0:T(8,128)(2,1)S(1)} %dynamic-slice_bitcast_fusion), channel_id=1, source_target_pairs={{0,2},{1,3},{2,0},{3,1},{4,6},{5,7},{6,4},{7,5},{8,10},{9,11},{10,... | collective-permute-start | bytes 6291464 | tf_op jit(solution)/shard_map/ppermute | solution.py:35
  591.8 29.7 %collective-permute-start.45 = (bf16[2,512,2048]{2,1,0:T(8,128)(2,1)S(1)}, bf16[2,512,2048]{2,1,0:T(8,128)(2,1)S(1)}, u32[]{:S(2)}, u32[]{:S(2)}) collective-permute-start(bf16[2,512,2048]{2,1,0:T(8,128)(2,1)S(1)} %pad_maximum_fusion.3), channel_id=1, source_target_pairs={{0,1},{1,0},{2,3},{3,2},{4,5},{5,4},{6,7},{7,6},{8,9},{9,8},{10,11... | collective-permute-start | bytes 12582920 | tf_op jit(solution)/shard_map/ppermute | solution.py:35
  594.7 55.2 %collective-permute-start.59 = (bf16[256,1024]{1,0:T(8,128)(2,1)}, bf16[256,1024]{1,0:T(8,128)(2,1)}, u32[]{:S(2)}, u32[]{:S(2)}) collective-permute-start(bf16[256,1024]{1,0:T(8,128)(2,1)} %reduce-scatter.4.cloned.1.call-done), channel_id=1, source_target_pairs={{0,1},{1,0},{2,3},{3,2},{4,5},{5,4},{6,7},{7,6},{8,9},{9,8},{10,11... | collective-permute-start | bytes 1572872 | tf_op jit(solution)/shard_map/ppermute | solution.py:35
  609.4 40.5 %collective-permute-start.58 = (bf16[256,1024]{1,0:T(8,128)(2,1)}, bf16[256,1024]{1,0:T(8,128)(2,1)}, u32[]{:S(2)}, u32[]{:S(2)}) collective-permute-start(bf16[256,1024]{1,0:T(8,128)(2,1)} %collective-permute-done.57), channel_id=1, source_target_pairs={{0,1},{1,0},{2,3},{3,2},{4,5},{5,4},{6,7},{7,6},{8,9},{9,8},{10,11... | collective-permute-start | bytes 1572872 | tf_op jit(solution)/shard_map/ppermute | solution.py:35
  654.5 45.3 %collective-permute-start.50 = (bf16[512,2048]{1,0:T(8,128)(2,1)S(1)}, bf16[512,2048]{1,0:T(8,128)(2,1)S(1)}, u32[]{:S(2)}, u32[]{:S(2)}) collective-permute-start(bf16[512,2048]{1,0:T(8,128)(2,1)S(1)} %copy-done.33), channel_id=1, source_target_pairs={{0,2},{1,3},{2,0},{3,1},{4,6},{5,7},{6,4},{7,5},{8,10},{9,11},{10,... | collective-permute-start | bytes 6291464 | tf_op jit(solution)/shard_map/ppermute | solution.py:35
  656.9 33.8 %collective-permute-start.49 = (bf16[256,1664]{1,0:T(8,128)(2,1)S(1)}, bf16[256,1664]{1,0:T(8,128)(2,1)S(1)}, u32[]{:S(2)}, u32[]{:S(2)}) collective-permute-start(bf16[256,1664]{1,0:T(8,128)(2,1)S(1)} %add_convert_fusion.2), channel_id=1, source_target_pairs={{8,0},{16,8},{24,16},{28,24},{20,28},{12,20},{4,12},{0,4},{9,1},{1... | collective-permute-start | bytes 2555912 | tf_op jit(solution)/shard_map/ppermute | solution.py:234
  660.0 30.7 %collective-permute-start.48 = (bf16[256,1664]{1,0:T(8,128)(2,1)S(1)}, bf16[256,1664]{1,0:T(8,128)(2,1)S(1)}, u32[]{:S(2)}, u32[]{:S(2)}) collective-permute-start(bf16[256,1664]{1,0:T(8,128)(2,1)S(1)} %add_convert_fusion.3), channel_id=1, source_target_pairs={{0,8},{8,16},{16,24},{24,28},{28,20},{20,12},{12,4},{4,0},{1,9},{9... | collective-permute-start | bytes 2555912 | tf_op jit(solution)/shard_map/ppermute | solution.py:234
  723.5 44.4 %collective-permute-start.56 = (bf16[64,2048]{1,0:T(8,128)(2,1)}, bf16[64,2048]{1,0:T(8,128)(2,1)S(1)}, u32[]{:S(2)}, u32[]{:S(2)}) collective-permute-start(bf16[64,2048]{1,0:T(8,128)(2,1)} %reduce-scatter.8.cloned.1.call-done), channel_id=1, source_target_pairs={{0,1},{1,0},{2,3},{3,2},{4,5},{5,4},{6,7},{7,6},{8,9},{9,8},{10,11... | collective-permute-start | bytes 786440 | tf_op jit(solution)/shard_map/ppermute | solution.py:35
  727.9 41.6 %collective-permute-start.53 = (bf16[256,1664]{1,0:T(8,128)(2,1)S(1)}, bf16[256,1664]{1,0:T(8,128)(2,1)S(1)}, u32[]{:S(2)}, u32[]{:S(2)}) collective-permute-start(bf16[256,1664]{1,0:T(8,128)(2,1)S(1)} %add_convert_fusion.1), channel_id=1, source_target_pairs={{0,1},{1,0},{2,3},{3,2},{4,5},{5,4},{6,7},{7,6},{8,9},{9,8},{10,11... | collective-permute-start | bytes 2555912 | tf_op jit(solution)/shard_map/ppermute | solution.py:35
  (146 other events, 2406.4 us)
Sparse Core Ops, SparseCore 0:
  82.1 50.0 all-gather.5
  134.2 71.3 all-gather.3
  253.0 49.9 all-gather.7
  382.0 88.3 reduce-scatter.3
  474.4 68.0 reduce-scatter.5
  645.6 77.8 reduce-scatter.7

commit v3 on v2

--- a/solution.py
+++ b/solution.py
@@ -2,6 +2,7 @@
 
 import jax
 import jax.numpy as jnp
+import numpy as np
 from jax import lax
 from jax.experimental import pallas as pl
 from jax.experimental.pallas import tpu as pltpu
@@ -234,10 +235,13 @@
     return lax.ppermute(x, "shard", [(b, a) for a, b in pairs] if back else pairs)
 
 
-def ring_ids(n, shard):
+def ring_ids(n):
     ring = ring_of(n)
-    places = jnp.asarray([ring.index(i) for i in range(n)], jnp.int32)
-    return jnp.asarray(ring, jnp.int32)[(places[shard] + jnp.arange(n, dtype=jnp.int32)) % n]
+    return np.array([[ring[(ring.index(s) + i) % n] for i in range(n)] for s in range(n)], np.int32)
+
+
+def of_shard(table, shard):
+    return lax.dynamic_index_in_dim(jnp.asarray(table), shard, 0, keepdims=False)
 
 
 def ring_gather(block, n, due):
@@ -303,9 +307,9 @@
 def ring_scatter(parts, n, shard, due):
     rows = parts[0].shape[0] // n
     half = rows // 2
-    ids = ring_ids(n, shard)
+    starts = of_shard(ring_ids(n) * rows, shard)
     chunk = lambda k, first=0, size=rows: jnp.concatenate(
-        [lax.dynamic_slice_in_dim(x, ids[k % n] * rows + first, size, 0) for x in parts], 1
+        [lax.dynamic_slice_in_dim(x, starts[k % n] + first, size, 0) for x in parts], 1
     )
     done = []
     ahead = ring_step(chunk(n // 2, 0, half), n)
@@ -406,18 +410,21 @@
     doc_row = docs_all.reshape(4, 1, length)
     slots = slot_rows[0].reshape(experts * cap)
     select = (slots[:, None] == jnp.arange(length, dtype=jnp.int32)[None, :]).astype(BF16)
-    own_upstream = dot(select, out_grad).astype(BF16)
-
-    pieces, (hidden_side, cosine, sine, own_upstream) = ring_gather(
+
+    def to_experts(x):
+        own = lax.dynamic_index_in_dim(x, core, 0, keepdims=False)
+        other = lax.dynamic_index_in_dim(x, 1 - core, 0, keepdims=False)
+        pair = jnp.stack([own, swap(other, 1)])
+        return jnp.concatenate([pair, swap(pair, 2)], 0)
+
+    slot_upstream = to_experts(dot(select, out_grad).astype(BF16).reshape(experts, cap, width))
+
+    pieces, arrays = ring_gather(
         jnp.concatenate([qkv_block, small_block], 1),
         n_shard,
-        (swap(hidden_in, 2), cosine, sine, own_upstream),
-    )
-    piece, k, first = pieces[-3]
-    piece, output_block, gate_up_block, down_block = tie(
-        piece, output_block, gate_up_block, down_block
-    )
-    pieces[-3] = (piece, k, first)
+        (swap(hidden_in, 2), cosine, sine, slot_upstream, output_block, gate_up_block, down_block),
+    )
+    hidden_side, cosine, sine, slot_upstream, output_block, gate_up_block, down_block = arrays
     hidden_all = jnp.concatenate(
         [hidden_in, swap(hidden_in, 1), hidden_side, swap(hidden_side, 1)], 0
     )
@@ -425,8 +432,9 @@
     piece, k, first = pieces[-1]
     piece, normed_scale = tie(piece, normed_scale)
     pieces[-1] = (piece, k, first)
-    ids = ring_ids(n_shard, shard)
-    starts = jnp.stack([ids[k] * my_rows + first for _, k, first in pieces])
+    ids = ring_ids(n_shard)
+    starts = np.stack([ids[:, k] * my_rows + first for _, k, first in pieces], 1)
+    starts = of_shard(starts, shard)
     w_qkv, small_w = place_rows([piece for piece, _, _ in pieces], starts, width, 3 * part)
     router_w = small_w[:, :routed]
     gains = small_w[:, routed : routed + 4].T.astype(F32)
@@ -439,12 +447,6 @@
 
     upstream = out_grad.astype(F32)
 
-    def to_experts(x):
-        own = lax.dynamic_index_in_dim(x, core, 0, keepdims=False)
-        other = lax.dynamic_index_in_dim(x, 1 - core, 0, keepdims=False)
-        pair = jnp.stack([own, swap(other, 1)])
-        return jnp.concatenate([pair, swap(pair, 2)], 0)
-
     def send_side(x, send):
         return swap(x[2:].astype(send), 2)
 
@@ -458,9 +460,7 @@
         high, low = split_sum(x.reshape(experts * cap, width))
         return dot(select, high, ((0,), (0,))) + dot(select, low, ((0,), (0,)))
 
-    slot_upstream = to_experts(own_upstream.reshape(experts, cap, width))
     normed = (hidden_all.astype(F32) * normed_scale * gain_one).astype(BF16)
-    w_qkv, slot_upstream = tie(w_qkv, slot_upstream)
     qkv = dot(normed, w_qkv)
     query_raw, key_raw = qkv[:, :part], qkv[:, part : 2 * part]
     squares = jnp.stack([jnp.sum(query_raw * query_raw, -1), jnp.sum(key_raw * key_raw, -1)], -1)
@@ -468,7 +468,7 @@
     scales = lax.rsqrt(squares / width + EPSILON)
     query_scale, key_scale = scales[:, :1], scales[:, 1:]
     scales, w_out_part = tie(scales, w_out_part)
-    out_pieces = in_order(rep_gather(w_out_part), rep)
+    out_core, out_side = swap(w_out_part, 1), swap(w_out_part, 2)
     mixed_heads, queries, keys, values = attend(
         qkv,
         query_scale,
@@ -482,10 +482,12 @@
         heads,
         dim,
     )
+    mixed_heads, out_core, out_side = tie(mixed_heads, out_core, out_side)
     blocks = mixed_heads.reshape(4, length, part)
     from_side = swap(blocks[2:], 2)
-    from_side, w_gu, *out_pieces = tie(from_side, w_gu, *out_pieces)
+    out_pieces = in_order([w_out_part, out_core, out_side, swap(out_side, 1)], rep)
     output_w = jnp.stack(out_pieces, 1).reshape(width, width)
+    from_side, w_gu, output_w = tie(from_side, w_gu, output_w)
     mixed = jnp.concatenate(
         in_order([blocks[0], swap(blocks[1], 1), from_side[0], swap(from_side[1], 1)], rep), 1
     )
@@ -543,19 +545,19 @@
     piece = lambda j: lax.dynamic_slice_in_dim(mixed_grad, (rep ^ j) * part, part, 1)
     from_side = swap(jnp.stack([piece(2), piece(3)]), 2)
     from_core, branch_grad = tie(swap(piece(1), 1), branch_grad)
+    at = lambda x, i, axis: lax.dynamic_index_in_dim(x, i, axis, keepdims=False)
     out_w_grad = dot(mixed, branch_grad, ((0,), (0,))).astype(BF16)
-    out_w_grad = out_w_grad.reshape(n_shard, 2, 2, quarter, width)
-    at = lambda x, i, axis: lax.dynamic_index_in_dim(x, i, axis, keepdims=False)
-    out_w_grad = at(out_w_grad, core, 2).astype(F32) + swap(at(out_w_grad, 1 - core, 2), 1)
-    out_w_grad = out_w_grad.astype(BF16)
     from_side, out_w_grad, returned = tie(from_side, out_w_grad, returned)
     grads = jnp.concatenate([piece(0), from_core, from_side[0], swap(from_side[1], 1)], 0)
     returned_there = send_side(returned, BF16)
+    out_w_grad = out_w_grad.reshape(n_shard, 2, 2, quarter, width)
+    out_there = swap(at(out_w_grad, 1 - core, 2), 1)
 
     query_grad, key_grad, value_grad = attend_back(
         queries, keys, values, grads, cosine, sine, doc_col, doc_row, heads, dim
     )
-    value_grad, returned_there = tie(value_grad, returned_there)
+    value_grad, returned_there, out_there = tie(value_grad, returned_there, out_there)
+    out_w_grad = (at(out_w_grad, core, 2).astype(F32) + out_there).astype(BF16)
     own_gates = jnp.sum(select_wide * window.T[:, None, :], -1)
     returned = from_experts(returned, returned_there, BF16)
     output = (residual + add_slots(own_gates[:, :, None] * returned)).astype(BF16)
@@ -564,7 +566,7 @@
         [jnp.sum(weighted_q * query_raw, -1), jnp.sum(weighted_k * key_raw, -1)], -1
     )
     means = rep_sum(means.reshape(4, length, 2)).reshape(-1, 2) / width
-    means, out_w_grad, gate_up_owned = tie(means, out_w_grad, gate_up_owned)
+    means, out_w_grad = tie(means, out_w_grad)
     out_there = swap(at(out_w_grad, 1 - side, 1), 2)
     gain_query_grad = jnp.sum(query_grad * query_raw * query_scale, 0)
     gain_key_grad = jnp.sum(key_grad * key_raw * key_scale, 0)
@@ -574,7 +576,11 @@
         [query_raw_grad.astype(BF16), key_raw_grad.astype(BF16), value_grad], 1
     )
     qkv_w_grad = dot(normed, qkv_grad, ((0,), (0,))).astype(BF16)
-    qkv_grad, qkv_w_grad = tie(qkv_grad, qkv_w_grad)
+    qkv_grad, qkv_w_grad, out_there, gate_up_owned = tie(
+        qkv_grad, qkv_w_grad, out_there, gate_up_owned
+    )
+    out_w_grad = (at(out_w_grad, side, 1).astype(F32) + out_there).astype(BF16)
+    out_owned = shard_scatter(out_w_grad.reshape(n_shard * quarter, width))
     place = lambda g: lax.dynamic_update_slice_in_dim(
         jnp.zeros((width,), F32), g, rep * part, 0
     )
@@ -585,26 +591,16 @@
     slot_grads = qkv_grad.reshape(4, length, 3 * part)
     back = lambda j: dot(slot_grads[j], w_qkv, ((1,), (1,)))
     due = (
-        lambda: (back(1), back(3), out_there),
-        lambda one, three, there: (
-            back(2),
-            swap(jnp.stack([one, three]).astype(BF16), 1),
-            (at(out_w_grad, side, 1).astype(F32) + there).astype(BF16),
-        ),
-        lambda two, from_core, total: (
+        lambda: (back(1), back(3)),
+        lambda one, three: (back(2), swap(jnp.stack([one, three]).astype(BF16), 1)),
+        lambda two, from_core: (
             back(0) + from_core[0].astype(F32),
-            (two + from_core[1].astype(F32)).astype(BF16),
-            total,
+            two + from_core[1].astype(F32),
             down_owned,
         ),
-        lambda zero, two, total, down: (
-            zero,
-            swap(two, 2),
-            shard_scatter(total.reshape(n_shard * quarter, width)),
-            down,
-        ),
-    )
-    qkv_owned, (normed_grad, from_side, out_owned, down_owned) = ring_scatter(
+        lambda zero, two, down: (zero, swap(two.astype(BF16), 2), down),
+    )
+    qkv_owned, (normed_grad, from_side, down_owned) = ring_scatter(
         [qkv_w_grad, small], n_shard, shard, due
     )
     normed_grad = normed_grad + from_side.astype(F32)
@@ -614,7 +610,9 @@
     hidden_part = scale_one * weighted - hidden * scale_one * scale_one * scale_one * inner_mean
     input_grad = residual_grad + hidden_part
 
-    qkv_pieces = in_order(rep_gather(qkv_owned.astype(BF16)), rep)
+    qkv_owned = qkv_owned.astype(BF16)
+    qkv_core, qkv_side, out_owned = tie(swap(qkv_owned, 1), swap(qkv_owned, 2), out_owned)
+    qkv_pieces = in_order([qkv_owned, qkv_core, qkv_side, swap(qkv_side, 1)], rep)
     spread = lambda i: jnp.concatenate(
         [p[:, i * part : (i + 1) * part] for p in qkv_pieces], 1
     ).astype(F32)

time: 795 us -> 754 us (0.948)
  waiting for transfers between devices: 334 us -> 256 us
  between operations: 21.5 us -> 33.3 us
  starting transfers between devices: 35.6 us -> 44.6 us
  local copies, waits for them, and re-layouts: 76.9 us -> 85.2 us
  matrix products: 123 us -> 131 us
    ppermute x47, waiting for transfers between devices: 226 us -> 166 us  [swap(): return lax.ppermute(x, 'rep', [(i, i ^ mask) for i in range(4)])]
    reduce_scatter x3, waiting for transfers between devices: 23.8 us -> 0.02 us  [shard_scatter(): lax.psum_scatter(x, 'shard', scatter_dimension=0, tiled=True).astype(F32)]
    dot_general x34, matrix products: 123 us -> 131 us  [dot(): return lax.dot_general(a, b, (dims, ((), ())), preferred_element_type=F32)]
    unnamed x209 -> x217, local copies, waits for them, and re-layouts: 24.4 us -> 20.9 us
  transfers between devices with their start and end apart: 69 -> 69, of which waited for: 36 -> 35; matrix products, arithmetic and copies ran while one was open for 35% -> 37% of each run, Pallas kernels for 10% -> 11%
where the time goes in v3:
time: 754 us; the launch traced here: 745 us
  waiting for transfers between devices  256 us (34%)
  matrix products  131 us (17%)
  other arithmetic  115 us (15%)
  local copies, waits for them, and re-layouts  85.2 us (11%)
  Pallas kernels  79.9 us (11%)
  starting transfers between devices  44.6 us (6%)
  between operations  33.3 us (4%)
    ppermute x47, waiting for transfers between devices, swap(): return lax.ppermute(x, 'rep', [(i, i ^ mask) for i in range(4)])  166 us
    dot_general x34, matrix products, dot(): return lax.dot_general(a, b, (dims, ((), ())), preferred_element_type=F32)  131 us
    ppermute x16, waiting for transfers between devices, ring_step(): lax.ppermute(x, 'shard', [(b, a) for a, b in pairs] if back else pairs)  88 us
    pallas_call x1, Pallas kernels, attend_back(): pl.pallas_call(functools.partial(attend_back_kernel, dim ** (-0.5)), grid...  38.5 us
    pallas_call x1, Pallas kernels, attend(): pl.pallas_call(functools.partial(attend_kernel, dim ** (-0.5)), grid=(tok...  35 us
    ppermute x47, starting transfers between devices, swap(): return lax.ppermute(x, 'rep', [(i, i ^ mask) for i in range(4)])  23.7 us
    unnamed x217, local copies, waits for them, and re-layouts  20.9 us
    ppermute x16, starting transfers between devices, ring_step(): lax.ppermute(x, 'shard', [(b, a) for a, b in pairs] if back else pairs)  20 us
  transfers between devices with their start and end apart: 69, of which 35 were waited for; matrix products, arithmetic and copies ran while one was open for 37% of the time, Pallas kernels for 11%

profile of v3, /device:TPU:0, one launch (start us, length us, event | category | flops | bytes accessed | tf_op | source)
XLA Modules:
  0.0 745.3 jit_solution(8208170592719165688)
XLA Ops:
  32.7 9.9 %collective-permute-done.2.refs_2_ = bf16[256,1664]{1,0:T(8,128)(2,1)} collective-permute-done((bf16[256,1664]{1,0:T(8,128)(2,1)}, bf16[256,1664]{1,0:T(8,128)(2,1)}, u32[]{:S(2)}, u32[]{:S(2)}) %collective-permute-start.2) | collective-permute-done | bytes 852000 | tf_op jit(solution)/shard_map/ppermute | solution.py:235
  50.5 13.2 %collective-permute-done.3.refs_3_ = bf16[256,1664]{1,0:T(8,128)(2,1)S(1)} collective-permute-done((bf16[256,1664]{1,0:T(8,128)(2,1)}, bf16[256,1664]{1,0:T(8,128)(2,1)S(1)}, u32[]{:S(2)}, u32[]{:S(2)}) %collective-permute-start.3) | collective-permute-done | bytes 852000 | tf_op jit(solution)/shard_map/ppermute | solution.py:235
  71.8 25.1 %collective-permute-done.12 = bf16[2,128,2048]{2,1,0:T(8,128)(2,1)S(1)} collective-permute-done((bf16[2,128,2048]{2,1,0:T(8,128)(2,1)S(1)}, bf16[2,128,2048]{2,1,0:T(8,128)(2,1)S(1)}, u32[]{:S(2)}, u32[]{:S(2)}) %collective-permute-start.12) | collective-permute-done | bytes 1048608 | tf_op jit(solution)/shard_map/ppermute | solution.py:36
  109.2 10.7 %collective-permute-done.14.refs_8_ = bf16[128,1664]{1,0:T(8,128)(2,1)S(1)} collective-permute-done((bf16[128,1664]{1,0:T(8,128)(2,1)S(1)}, bf16[128,1664]{1,0:T(8,128)(2,1)S(1)}, u32[]{:S(2)}, u32[]{:S(2)}) %collective-permute-start.14) | collective-permute-done | bytes 426016 | tf_op jit(solution)/shard_map/ppermute | solution.py:235
  128.5 23.5 %fusion.14.q_ref.k_ref.v_ref = f32[2048,1536]{1,0:T(8,128)} fusion(bf16[2048,1536]{1,0:T(8,128)(2,1)} %get-tuple-element.97, f32[2048]{0:T(1024)S(1)} %bitcast.282, f32[2048]{0:T(1024)S(1)} %add_rsqrt_fusion, bf16[512,2048]{1,0:T(8,128)(2,1)S(1)} %collective-permute-done.13, bf16[512,2048]{1,0:T(8,128)(2,1)} %collective-permute-done.7, ...), kind=kOutput, calls=%fused_computation.54 | convolution fusion | flops 12931039232 | bytes 27279360 | tf_op jit(solution)/shard_map/dot_general | solution.py:32
  169.9 35.0 %attend.1 = (bf16[2048,512]{1,0:T(8,128)(2,1)}, bf16[2048,512]{1,0:T(8,128)(2,1)}, bf16[2048,512]{1,0:T(8,128)(2,1)}, bf16[2048,512]{1,0:T(8,128)(2,1)}) custom-call(f32[2048,1536]{1,0:T(8,128)} %fusion.14.q_ref.k_ref.v_ref, f32[2048,1536]{1,0:T(8,128)} %fusion.14.q_ref.k_ref.v_ref, f32[2048,1536]{1,0:T(8,128)} %fusion.14.q_ref.k_ref.v_ref, ...), custom_call_target="tpu_custom_call" | custom-call | flops 2147483648 | bytes 20971520 | tf_op jit(solution)/shard_map/attend/pallas_call | solution.py:183
  222.5 17.3 %collective-permute-done.20 = bf16[2,512,512]{2,1,0:T(8,128)(2,1)S(1)} collective-permute-done((bf16[2,512,512]{2,1,0:T(8,128)(2,1)S(1)}, bf16[2,512,512]{2,1,0:T(8,128)(2,1)S(1)}, u32[]{:S(2)}, u32[]{:S(2)}) %collective-permute-start.20) | collective-permute-done | bytes 1048608 | tf_op jit(solution)/shard_map/ppermute | solution.py:36
  243.3 9.3 %multiply_reduce_fusion.6 = (f32[512]{0:T(512)S(1)}, f32[512,2048]{1,0:T(8,128)S(1)}) fusion(bf16[2048,2048]{1,0:T(8,128)(2,1)} %bitcast.242, bf16[512,512]{1,0:T(8,128)(2,1)S(1)} %get-tuple-element.275, bf16[512,512]{1,0:T(8,128)(2,1)S(1)} %get-tuple-element.274, bf16[512,512]{1,0:T(8,128)(2,1)S(1)} %get-tuple-element.273, ...), kind=kOutput, calls=%fused_computation.45 | convolution fusion | flops 4307549696 | bytes 16779264 | tf_op jit(solution)/shard_map/dot_general | solution.py:32
  260.6 24.4 %collective-permute-done.27 = bf16[2,128,2048]{2,1,0:T(8,128)(2,1)} collective-permute-done((bf16[2,128,2048]{2,1,0:T(8,128)(2,1)}, bf16[2,128,2048]{2,1,0:T(8,128)(2,1)}, u32[]{:S(2)}, u32[]{:S(2)}) %collective-permute-start.27) | collective-permute-done | bytes 1048608 | tf_op jit(solution)/shard_map/ppermute | solution.py:36
  326.6 12.5 %collective-permute-done.28 = bf16[2,128,2048]{2,1,0:T(8,128)(2,1)} collective-permute-done((bf16[2,128,2048]{2,1,0:T(8,128)(2,1)}, bf16[2,128,2048]{2,1,0:T(8,128)(2,1)}, u32[]{:S(2)}, u32[]{:S(2)}) %collective-permute-start.28) | collective-permute-done | bytes 1048608 | tf_op jit(solution)/shard_map/ppermute | solution.py:36
  364.7 7.3 convolution_convert_fusion
  372.0 16.7 %collective-permute-done.32 = bf16[2,512,512]{2,1,0:T(8,128)(2,1)S(1)} collective-permute-done((bf16[2,512,512]{2,1,0:T(8,128)(2,1)S(1)}, bf16[2,512,512]{2,1,0:T(8,128)(2,1)S(1)}, u32[]{:S(2)}, u32[]{:S(2)}) %collective-permute-start.32) | collective-permute-done | bytes 1048608 | tf_op jit(solution)/shard_map/ppermute | solution.py:36
  389.6 6.7 constant_dynamic-slice_fusion.19
  425.1 38.5 %attend_back.1 = (f32[2048,512]{1,0:T(8,128)}, f32[2048,512]{1,0:T(8,128)}, bf16[2048,512]{1,0:T(8,128)(2,1)}) custom-call(bf16[2048,512]{1,0:T(8,128)(2,1)} %get-tuple-element.115.queries, bf16[2048,512]{1,0:T(8,128)(2,1)} %get-tuple-element.116.keys, bf16[2048,512]{1,0:T(8,128)(2,1)} %get-tuple-element.117.values, ...), custom_call_target="tpu_custom_call" | custom-call | flops 5368709120 | bytes 18874368 | tf_op jit(solution)/shard_map/attend_back/pallas_call | solution.py:206
  463.6 7.1 multiply_reduce_fusion.3
  500.3 19.7 %convolution_convert_fusion.1 = bf16[2048,1536]{1,0:T(8,128)(2,1)} fusion(f32[2048]{0:T(1024)S(1)} %bitcast.283, f32[2048]{0:T(1024)S(1)} %copy-done.85, bf16[2048,512]{1,0:T(8,128)(2,1)} %get-tuple-element.127, bf16[2048,512]{1,0:T(8,128)(2,1)} %get-tuple-element.256, bf16[2048,512]{1,0:T(8,128)(2,1)S(1)} %get-tuple-element.255, ...), kind=kOutput, calls=%fused_computation.10 | convolution fusion | flops 12953059328 | bytes 20987904 | tf_op jit(solution)/shard_map/dot_general | solution.py:32
  532.1 9.6 %collective-permute-done.40 = bf16[8,64,2048]{2,1,0:T(8,128)(2,1)} collective-permute-done((bf16[8,64,2048]{2,1,0:T(8,128)(2,1)}, bf16[8,64,2048]{2,1,0:T(8,128)(2,1)}, u32[]{:S(2)}, u32[]{:S(2)}) %collective-permute-start.40) | collective-permute-done | bytes 2097184 | tf_op jit(solution)/shard_map/ppermute | solution.py:36
  547.4 7.0 fusion.33
  587.9 23.6 %collective-permute-done.44 = bf16[256,1664]{1,0:T(8,128)(2,1)S(1)} collective-permute-done((bf16[256,1664]{1,0:T(8,128)(2,1)S(1)}, bf16[256,1664]{1,0:T(8,128)(2,1)S(1)}, u32[]{:S(2)}, u32[]{:S(2)}) %collective-permute-start.44) | collective-permute-done | bytes 852000 | tf_op jit(solution)/shard_map/ppermute | solution.py:235
  617.8 8.0 %convert_add_fusion.4 = f32[512,2048]{1,0:T(8,128)} fusion(bf16[2048,1536]{1,0:T(8,128)(2,1)} %get-tuple-element.97, bf16[2,512,2048]{2,1,0:T(8,128)(2,1)S(1)} %collective-permute-done.45, bf16[2048,1536]{1,0:T(8,128)(2,1)S(1)} %bitcast.249), kind=kOutput, calls=%fused_computation.30 | convolution fusion | flops 3223322624 | bytes 14155776 | tf_op jit(solution)/shard_map/dot_general | solution.py:32
  625.9 13.5 %collective-permute-done.47 = bf16[256,1664]{1,0:T(8,128)(2,1)} collective-permute-done((bf16[256,1664]{1,0:T(8,128)(2,1)}, bf16[256,1664]{1,0:T(8,128)(2,1)}, u32[]{:S(2)}, u32[]{:S(2)}) %collective-permute-start.47) | collective-permute-done | bytes 852000 | tf_op jit(solution)/shard_map/ppermute | solution.py:235
  657.9 8.2 %collective-permute-done.49 = bf16[256,1664]{1,0:T(8,128)(2,1)S(1)} collective-permute-done((bf16[256,1664]{1,0:T(8,128)(2,1)S(1)}, bf16[256,1664]{1,0:T(8,128)(2,1)S(1)}, u32[]{:S(2)}, u32[]{:S(2)}) %collective-permute-start.49) | collective-permute-done | bytes 852000 | tf_op jit(solution)/shard_map/ppermute | solution.py:235
  670.0 16.5 %collective-permute-done.50 = bf16[512,2048]{1,0:T(8,128)(2,1)S(1)} collective-permute-done((bf16[512,2048]{1,0:T(8,128)(2,1)}, bf16[512,2048]{1,0:T(8,128)(2,1)S(1)}, u32[]{:S(2)}, u32[]{:S(2)}) %collective-permute-start.50) | collective-permute-done | bytes 2097184 | tf_op jit(solution)/shard_map/ppermute | solution.py:36
  702.2 11.3 %collective-permute-done.52 = bf16[256,1664]{1,0:T(8,128)(2,1)S(1)} collective-permute-done((bf16[256,1664]{1,0:T(8,128)(2,1)S(1)}, bf16[256,1664]{1,0:T(8,128)(2,1)S(1)}, u32[]{:S(2)}, u32[]{:S(2)}) %collective-permute-start.52) | collective-permute-done | bytes 852000 | tf_op jit(solution)/shard_map/ppermute | solution.py:36
  (554 shorter events, 337.4 us)
Async XLA Ops:
  7.2 156.8 %all-gather.4.cloned.1.call-start = ((), (), s32[]{:S(2)}) async-start(), calls=%async_computation.3 | async-start | bytes 2359296 | tf_op jit(solution)/shard_map/all_gather | solution.py:334
  26.2 72.3 %collective-permute-start.7 = (bf16[512,2048]{1,0:T(8,128)(2,1)}, bf16[512,2048]{1,0:T(8,128)(2,1)}, u32[]{:S(2)}, u32[]{:S(2)}) collective-permute-start(bf16[512,2048]{1,0:T(8,128)(2,1)} %param.19), channel_id=1, source_target_pairs={{0,2},{1,3},{2,0},{3,1},{4,6},{5,7},{6,4},{7,5},{8,10},{9,11},{10,... | collective-permute-start | bytes 6291464 | tf_op jit(solution)/shard_map/ppermute | solution.py:36
  48.1 48.8 %collective-permute-start.12 = (bf16[2,128,2048]{2,1,0:T(8,128)(2,1)S(1)}, bf16[2,128,2048]{2,1,0:T(8,128)(2,1)S(1)}, u32[]{:S(2)}, u32[]{:S(2)}) collective-permute-start(bf16[2,128,2048]{2,1,0:T(8,128)(2,1)S(1)} %pad_maximum_fusion.12), channel_id=1, source_target_pairs={{0,2},{1,3},{2,0},{3,1},{4,6},{5,7},{6,4},{7,5},{8,10},{9,11},{10,... | collective-permute-start | bytes 3145736 | tf_op jit(solution)/shard_map/ppermute | solution.py:36
  49.7 54.4 %collective-permute-start = (bf16[512,2048]{1,0:T(8,128)(2,1)}, bf16[512,2048]{1,0:T(8,128)(2,1)}, u32[]{:S(2)}, u32[]{:S(2)}) collective-permute-start(bf16[512,2048]{1,0:T(8,128)(2,1)} %param.19), channel_id=1, source_target_pairs={{0,1},{1,0},{2,3},{3,2},{4,5},{5,4},{6,7},{7,6},{8,9},{9,8},{10,11... | collective-permute-start | bytes 6291464 | tf_op jit(solution)/shard_map/ppermute | solution.py:36
  64.2 34.2 %collective-permute-start.5 = (bf16[256,1664]{1,0:T(8,128)(2,1)S(1)}, bf16[256,1664]{1,0:T(8,128)(2,1)S(1)}, u32[]{:S(2)}, u32[]{:S(2)}) collective-permute-start(bf16[256,1664]{1,0:T(8,128)(2,1)S(1)} %collective-permute-done.3.refs_3_), channel_id=1, source_target_pairs={{0,8},{8,16},{16,24},{24,28},{28,20},{20,12},{12,4},{4,0},{1,9},{9... | collective-permute-start | bytes 2555912 | tf_op jit(solution)/shard_map/ppermute | solution.py:235
  65.8 32.7 %collective-permute-start.6 = (bf16[256,1664]{1,0:T(8,128)(2,1)}, bf16[256,1664]{1,0:T(8,128)(2,1)S(1)}, u32[]{:S(2)}, u32[]{:S(2)}) collective-permute-start(bf16[256,1664]{1,0:T(8,128)(2,1)} %collective-permute-done.4.refs_4_), channel_id=1, source_target_pairs={{8,0},{16,8},{24,16},{28,24},{20,28},{12,20},{4,12},{0,4},{9,1},{1... | collective-permute-start | bytes 2555912 | tf_op jit(solution)/shard_map/ppermute | solution.py:235
  100.6 139.2 %all-gather.6.cloned.1.call-start = ((), (), s32[]{:S(2)}) async-start(), calls=%async_computation.4 | async-start | bytes 4718592 | tf_op jit(solution)/shard_map/all_gather | solution.py:334
  156.2 135.7 %all-gather.8.cloned.1.call-start = ((), (), s32[]{:S(2)}) async-start(), calls=%async_computation.5 | async-start | bytes 2359296 | tf_op jit(solution)/shard_map/all_gather | solution.py:334
  164.0 46.9 %collective-permute-start.19 = (bf16[8,64,2048]{2,1,0:T(8,128)(2,1)}, bf16[8,64,2048]{2,1,0:T(8,128)(2,1)}, u32[]{:S(2)}, u32[]{:S(2)}) collective-permute-start(bf16[8,64,2048]{2,1,0:T(8,128)(2,1)} %bitcast.255), channel_id=1, source_target_pairs={{0,2},{1,3},{2,0},{3,1},{4,6},{5,7},{6,4},{7,5},{8,10},{9,11},{10,... | collective-permute-start | bytes 6291464 | tf_op jit(solution)/shard_map/ppermute | solution.py:36
  164.1 46.9 %collective-permute-start.18 = (bf16[8,64,2048]{2,1,0:T(8,128)(2,1)}, bf16[8,64,2048]{2,1,0:T(8,128)(2,1)}, u32[]{:S(2)}, u32[]{:S(2)}) collective-permute-start(bf16[8,64,2048]{2,1,0:T(8,128)(2,1)} %bitcast.256), channel_id=1, source_target_pairs={{0,1},{1,0},{2,3},{3,2},{4,5},{5,4},{6,7},{7,6},{8,9},{9,8},{10,11... | collective-permute-start | bytes 6291464 | tf_op jit(solution)/shard_map/ppermute | solution.py:36
  240.0 301.7 %reduce-scatter.4.cloned.1.call-start = ((), (), s32[]{:S(2)}) async-start(), calls=%async_computation.6 | async-start | bytes 4718592 | tf_op jit(solution)/shard_map/reduce_scatter | solution.py:338
  342.7 283.2 %reduce-scatter.6.cloned.1.call-start = ((), (), s32[]{:S(2)}) async-start(), calls=%async_computation.7 | async-start | bytes 2359296 | tf_op jit(solution)/shard_map/reduce_scatter | solution.py:338
  389.6 33.0 %collective-permute-start.34 = (bf16[512,512]{1,0:T(8,128)(2,1)}, bf16[512,512]{1,0:T(8,128)(2,1)}, u32[]{:S(2)}, u32[]{:S(2)}) collective-permute-start(bf16[512,512]{1,0:T(8,128)(2,1)} %get-tuple-element.307), channel_id=1, source_target_pairs={{0,1},{1,0},{2,3},{3,2},{4,5},{5,4},{6,7},{7,6},{8,9},{9,8},{10,11... | collective-permute-start | bytes 1572872 | tf_op jit(solution)/shard_map/ppermute | solution.py:36
  398.5 82.1 %collective-permute-start.36 = (bf16[8,2,64,2048]{3,2,0,1:T(8,128)(2,1)}, bf16[8,2,64,2048]{3,2,0,1:T(8,128)(2,1)}, u32[]{:S(2)}, u32[]{:S(2)}) collective-permute-start(bf16[8,2,64,2048]{3,2,0,1:T(8,128)(2,1)} %bitcast.234), channel_id=1, source_target_pairs={{0,1},{1,0},{2,3},{3,2},{4,5},{5,4},{6,7},{7,6},{8,9},{9,8},{10,11... | collective-permute-start | bytes 12582920 | tf_op jit(solution)/shard_map/ppermute | solution.py:36
  418.2 283.9 %reduce-scatter.8.cloned.1.call-start = ((), (), s32[]{:S(2)}) async-start(), calls=%async_computation.8 | async-start | bytes 2359296 | tf_op jit(solution)/shard_map/reduce_scatter | solution.py:338
  421.1 59.5 %collective-permute-start.35 = (bf16[2,128,2048]{2,1,0:T(8,128)(2,1)}, bf16[2,128,2048]{2,1,0:T(8,128)(2,1)}, u32[]{:S(2)}, u32[]{:S(2)}) collective-permute-start(bf16[2,128,2048]{2,1,0:T(8,128)(2,1)} %slice.614), channel_id=1, source_target_pairs={{0,2},{1,3},{2,0},{3,1},{4,6},{5,7},{6,4},{7,5},{8,10},{9,11},{10,... | collective-permute-start | bytes 3145736 | tf_op jit(solution)/shard_map/ppermute | solution.py:36
  491.8 33.7 %collective-permute-start.37 = (bf16[128,2048]{1,0:T(8,128)(2,1)S(1)}, bf16[128,2048]{1,0:T(8,128)(2,1)}, u32[]{:S(2)}, u32[]{:S(2)}) collective-permute-start(bf16[128,2048]{1,0:T(8,128)(2,1)S(1)} %fusion.74), channel_id=1, source_target_pairs={{0,1},{1,0},{2,3},{3,2},{4,5},{5,4},{6,7},{7,6},{8,9},{9,8},{10,11... | collective-permute-start | bytes 1572872 | tf_op jit(solution)/shard_map/ppermute | solution.py:36
  493.3 48.3 %collective-permute-start.40 = (bf16[8,64,2048]{2,1,0:T(8,128)(2,1)}, bf16[8,64,2048]{2,1,0:T(8,128)(2,1)}, u32[]{:S(2)}, u32[]{:S(2)}) collective-permute-start(bf16[8,64,2048]{2,1,0:T(8,128)(2,1)} %dynamic-slice_bitcast_fusion), channel_id=1, source_target_pairs={{0,2},{1,3},{2,0},{3,1},{4,6},{5,7},{6,4},{7,5},{8,10},{9,11},{10,... | collective-permute-start | bytes 6291464 | tf_op jit(solution)/shard_map/ppermute | solution.py:36
  541.7 39.8 %collective-permute-start.59 = (bf16[256,1024]{1,0:T(8,128)(2,1)}, bf16[256,1024]{1,0:T(8,128)(2,1)}, u32[]{:S(2)}, u32[]{:S(2)}) collective-permute-start(bf16[256,1024]{1,0:T(8,128)(2,1)} %reduce-scatter.4.cloned.1.call-done), channel_id=1, source_target_pairs={{0,1},{1,0},{2,3},{3,2},{4,5},{5,4},{6,7},{7,6},{8,9},{9,8},{10,11... | collective-permute-start | bytes 1572872 | tf_op jit(solution)/shard_map/ppermute | solution.py:36
  541.7 36.5 %collective-permute-start.57 = (bf16[256,1024]{1,0:T(8,128)(2,1)}, bf16[256,1024]{1,0:T(8,128)(2,1)}, u32[]{:S(2)}, u32[]{:S(2)}) collective-permute-start(bf16[256,1024]{1,0:T(8,128)(2,1)} %reduce-scatter.4.cloned.1.call-done), channel_id=1, source_target_pairs={{0,2},{1,3},{2,0},{3,1},{4,6},{5,7},{6,4},{7,5},{8,10},{9,11},{10,... | collective-permute-start | bytes 1572872 | tf_op jit(solution)/shard_map/ppermute | solution.py:36
  566.8 44.7 %collective-permute-start.45 = (bf16[2,512,2048]{2,1,0:T(8,128)(2,1)S(1)}, bf16[2,512,2048]{2,1,0:T(8,128)(2,1)S(1)}, u32[]{:S(2)}, u32[]{:S(2)}) collective-permute-start(bf16[2,512,2048]{2,1,0:T(8,128)(2,1)S(1)} %pad_maximum_fusion.3), channel_id=1, source_target_pairs={{0,1},{1,0},{2,3},{3,2},{4,5},{5,4},{6,7},{7,6},{8,9},{9,8},{10,11... | collective-permute-start | bytes 12582920 | tf_op jit(solution)/shard_map/ppermute | solution.py:36
  577.9 33.7 %collective-permute-start.44 = (bf16[256,1664]{1,0:T(8,128)(2,1)S(1)}, bf16[256,1664]{1,0:T(8,128)(2,1)S(1)}, u32[]{:S(2)}, u32[]{:S(2)}) collective-permute-start(bf16[256,1664]{1,0:T(8,128)(2,1)S(1)} %pad_maximum_fusion.16), channel_id=1, source_target_pairs={{8,0},{16,8},{24,16},{28,24},{20,28},{12,20},{4,12},{0,4},{9,1},{1... | collective-permute-start | bytes 2555912 | tf_op jit(solution)/shard_map/ppermute | solution.py:235
  579.6 32.0 %collective-permute-start.43 = (bf16[256,1664]{1,0:T(8,128)(2,1)S(1)}, bf16[256,1664]{1,0:T(8,128)(2,1)S(1)}, u32[]{:S(2)}, u32[]{:S(2)}) collective-permute-start(bf16[256,1664]{1,0:T(8,128)(2,1)S(1)} %fusion.69), channel_id=1, source_target_pairs={{0,8},{8,16},{16,24},{24,28},{28,20},{20,12},{12,4},{4,0},{1,9},{9... | collective-permute-start | bytes 2555912 | tf_op jit(solution)/shard_map/ppermute | solution.py:235
  642.5 44.0 %collective-permute-start.50 = (bf16[512,2048]{1,0:T(8,128)(2,1)}, bf16[512,2048]{1,0:T(8,128)(2,1)S(1)}, u32[]{:S(2)}, u32[]{:S(2)}) collective-permute-start(bf16[512,2048]{1,0:T(8,128)(2,1)} %convert_add_fusion.3), channel_id=1, source_target_pairs={{0,2},{1,3},{2,0},{3,1},{4,6},{5,7},{6,4},{7,5},{8,10},{9,11},{10,... | collective-permute-start | bytes 6291464 | tf_op jit(solution)/shard_map/ppermute | solution.py:36
  (150 other events, 2381.5 us)
Sparse Core Ops, SparseCore 0:
  100.7 51.5 all-gather.3
  156.3 75.4 all-gather.5
  240.1 51.7 all-gather.7
  342.9 89.5 reduce-scatter.3
  435.8 67.8 reduce-scatter.5
  564.8 79.9 reduce-scatter.7

commit v4 on v3

--- a/solution.py
+++ b/solution.py
@@ -304,12 +304,60 @@
     )(starts, *pieces)
 
 
-def ring_scatter(parts, n, shard, due):
+def normed_kernel(ids, hidden, scale, gain, out):
+    out[...] = (hidden[...].astype(F32) * scale[...] * gain[...]).astype(BF16)
+
+
+def normed_in_order(ids, hidden, scale, gain):
+    n = ids.shape[0]
+    rows, cols = hidden.shape
+    if cols // n % 128:
+        normed = (hidden.astype(F32) * scale * gain).astype(BF16)
+        return normed.reshape(rows, n, cols // n)[:, ids].reshape(rows, cols)
+    return pl.pallas_call(
+        normed_kernel,
+        grid_spec=pltpu.PrefetchScalarGridSpec(
+            num_scalar_prefetch=1,
+            grid=(n,),
+            in_specs=[
+                pl.BlockSpec((rows, cols // n), lambda i, ids: (0, ids[i])),
+                pl.BlockSpec((rows, 1), lambda i, ids: (0, 0)),
+                pl.BlockSpec((1, cols // n), lambda i, ids: (0, ids[i])),
+            ],
+            out_specs=pl.BlockSpec((rows, cols // n), lambda i, ids: (0, i)),
+        ),
+        out_shape=jax.ShapeDtypeStruct((rows, cols), BF16),
+        cost_estimate=cost(2 * rows * cols, 4 * rows * cols),
+        name="normed_in_order",
+    )(ids, hidden, scale, gain)
+
+
+def rows_kernel(ids, x, out):
+    out[...] = x[...].astype(out.dtype)
+
+
+def rows_in_order(ids, x):
+    n = ids.shape[0]
+    rows, cols = x.shape
+    return pl.pallas_call(
+        rows_kernel,
+        grid_spec=pltpu.PrefetchScalarGridSpec(
+            num_scalar_prefetch=1,
+            grid=(n,),
+            in_specs=[pl.BlockSpec((rows // n, cols), lambda i, ids: (ids[i], 0))],
+            out_specs=pl.BlockSpec((rows // n, cols), lambda i, ids: (i, 0)),
+        ),
+        out_shape=jax.ShapeDtypeStruct((rows, cols), BF16),
+        cost_estimate=cost(0, 4 * rows * cols),
+        name="rows_in_order",
+    )(ids, x)
+
+
+def ring_scatter(parts, n, due):
     rows = parts[0].shape[0] // n
     half = rows // 2
-    starts = of_shard(ring_ids(n) * rows, shard)
     chunk = lambda k, first=0, size=rows: jnp.concatenate(
-        [lax.dynamic_slice_in_dim(x, starts[k % n] + first, size, 0) for x in parts], 1
+        [x[k % n * rows + first : k % n * rows + first + size] for x in parts], 1
     )
     done = []
     ahead = ring_step(chunk(n // 2, 0, half), n)
@@ -411,20 +459,24 @@
     slots = slot_rows[0].reshape(experts * cap)
     select = (slots[:, None] == jnp.arange(length, dtype=jnp.int32)[None, :]).astype(BF16)
 
-    def to_experts(x):
+    def to_pair(x):
         own = lax.dynamic_index_in_dim(x, core, 0, keepdims=False)
         other = lax.dynamic_index_in_dim(x, 1 - core, 0, keepdims=False)
-        pair = jnp.stack([own, swap(other, 1)])
+        return jnp.stack([own, swap(other, 1)])
+
+    def to_experts(x):
+        pair = to_pair(x)
         return jnp.concatenate([pair, swap(pair, 2)], 0)
 
-    slot_upstream = to_experts(dot(select, out_grad).astype(BF16).reshape(experts, cap, width))
+    upstream_pair = to_pair(dot(select, out_grad).astype(BF16).reshape(experts, cap, width))
 
     pieces, arrays = ring_gather(
         jnp.concatenate([qkv_block, small_block], 1),
         n_shard,
-        (swap(hidden_in, 2), cosine, sine, slot_upstream, output_block, gate_up_block, down_block),
-    )
-    hidden_side, cosine, sine, slot_upstream, output_block, gate_up_block, down_block = arrays
+        (swap(hidden_in, 2), cosine, sine, upstream_pair, output_block, gate_up_block, down_block),
+    )
+    hidden_side, cosine, sine, upstream_pair, output_block, gate_up_block, down_block = arrays
+    slot_upstream = jnp.concatenate([upstream_pair, swap(upstream_pair, 2)], 0)
     hidden_all = jnp.concatenate(
         [hidden_in, swap(hidden_in, 1), hidden_side, swap(hidden_side, 1)], 0
     )
@@ -434,8 +486,9 @@
     pieces[-1] = (piece, k, first)
     ids = ring_ids(n_shard)
     starts = np.stack([ids[:, k] * my_rows + first for _, k, first in pieces], 1)
-    starts = of_shard(starts, shard)
+    starts, ring = of_shard(starts, shard), of_shard(ids, shard)
     w_qkv, small_w = place_rows([piece for piece, _, _ in pieces], starts, width, 3 * part)
+    w_qkv, slot_upstream = tie(w_qkv, slot_upstream)
     router_w = small_w[:, :routed]
     gains = small_w[:, routed : routed + 4].T.astype(F32)
     w_out_part = shard_gather(output_block).reshape(n_shard, quarter, width)
@@ -503,7 +556,10 @@
     window = probs_all[:, :experts] * named
     select_wide = select.reshape(experts, cap, length).astype(F32)
     slot_gates = to_experts(jnp.sum(select_wide * window.T[:, None, :], -1))
-    slot_inputs = to_experts(dot(select, inner).astype(BF16).reshape(experts, cap, width))
+    pair = to_pair(dot(select, inner).astype(BF16).reshape(experts, cap, width))
+    normed_ring = normed_in_order(ring, hidden_all, normed_scale, gain_one[None])
+    from_side, normed_ring = tie(swap(pair, 2), normed_ring)
+    slot_inputs = jnp.concatenate([pair, from_side], 0)
     slot_inputs = slot_inputs.reshape(4 * cap, width)
 
     gate_up = dot(slot_inputs, w_gu)
@@ -546,28 +602,30 @@
     from_side = swap(jnp.stack([piece(2), piece(3)]), 2)
     from_core, branch_grad = tie(swap(piece(1), 1), branch_grad)
     at = lambda x, i, axis: lax.dynamic_index_in_dim(x, i, axis, keepdims=False)
-    out_w_grad = dot(mixed, branch_grad, ((0,), (0,))).astype(BF16)
+    half = lambda which: at(mixed.reshape(length, n_shard, 2, 2, quarter), which, 3)
+    half_grad = lambda which: dot(
+        half(which).reshape(length, width // 2), branch_grad, ((0,), (0,))
+    ).astype(BF16)
+    out_there = swap(half_grad(1 - core), 1)
+    out_w_grad = (half_grad(core).astype(F32) + out_there).astype(BF16)
     from_side, out_w_grad, returned = tie(from_side, out_w_grad, returned)
     grads = jnp.concatenate([piece(0), from_core, from_side[0], swap(from_side[1], 1)], 0)
-    returned_there = send_side(returned, BF16)
-    out_w_grad = out_w_grad.reshape(n_shard, 2, 2, quarter, width)
-    out_there = swap(at(out_w_grad, 1 - core, 2), 1)
+    out_w_grad = out_w_grad.reshape(n_shard, 2, quarter, width)
+    out_there = swap(at(out_w_grad, 1 - side, 1), 2)
 
     query_grad, key_grad, value_grad = attend_back(
         queries, keys, values, grads, cosine, sine, doc_col, doc_row, heads, dim
     )
-    value_grad, returned_there, out_there = tie(value_grad, returned_there, out_there)
-    out_w_grad = (at(out_w_grad, core, 2).astype(F32) + out_there).astype(BF16)
-    own_gates = jnp.sum(select_wide * window.T[:, None, :], -1)
-    returned = from_experts(returned, returned_there, BF16)
-    output = (residual + add_slots(own_gates[:, :, None] * returned)).astype(BF16)
+    value_grad, out_there = tie(value_grad, out_there)
+    out_w_grad = (at(out_w_grad, side, 1).astype(F32) + out_there).astype(BF16)
+    out_owned = shard_scatter(out_w_grad.reshape(n_shard * quarter, width))
     weighted_q, weighted_k = query_grad * gain_query, key_grad * gain_key
     means = jnp.stack(
         [jnp.sum(weighted_q * query_raw, -1), jnp.sum(weighted_k * key_raw, -1)], -1
     )
     means = rep_sum(means.reshape(4, length, 2)).reshape(-1, 2) / width
-    means, out_w_grad = tie(means, out_w_grad)
-    out_there = swap(at(out_w_grad, 1 - side, 1), 2)
+    means, returned = tie(means, returned)
+    returned_there = send_side(returned, BF16)
     gain_query_grad = jnp.sum(query_grad * query_raw * query_scale, 0)
     gain_key_grad = jnp.sum(key_grad * key_raw * key_scale, 0)
     query_raw_grad = query_scale * weighted_q - query_raw * query_scale**3 * means[:, :1]
@@ -575,33 +633,39 @@
     qkv_grad = jnp.concatenate(
         [query_raw_grad.astype(BF16), key_raw_grad.astype(BF16), value_grad], 1
     )
-    qkv_w_grad = dot(normed, qkv_grad, ((0,), (0,))).astype(BF16)
-    qkv_grad, qkv_w_grad, out_there, gate_up_owned = tie(
-        qkv_grad, qkv_w_grad, out_there, gate_up_owned
-    )
-    out_w_grad = (at(out_w_grad, side, 1).astype(F32) + out_there).astype(BF16)
-    out_owned = shard_scatter(out_w_grad.reshape(n_shard * quarter, width))
+    qkv_w_grad = dot(normed_ring, qkv_grad, ((0,), (0,))).astype(BF16)
+    qkv_grad, qkv_w_grad, returned_there, gate_up_owned = tie(
+        qkv_grad, qkv_w_grad, returned_there, gate_up_owned
+    )
+    own_gates = jnp.sum(select_wide * window.T[:, None, :], -1)
+    returned = from_experts(returned, returned_there, BF16)
+    output = (residual + add_slots(own_gates[:, :, None] * returned)).astype(BF16)
     place = lambda g: lax.dynamic_update_slice_in_dim(
         jnp.zeros((width,), F32), g, rep * part, 0
     )
     small = jnp.stack([gain_two_grad, place(gain_query_grad), place(gain_key_grad)], 1)
     small = jnp.concatenate(
         [router_grad, small, jnp.zeros((width, 128 - 3 - routed), F32)], 1
-    ).astype(BF16)
-    slot_grads = qkv_grad.reshape(4, length, 3 * part)
-    back = lambda j: dot(slot_grads[j], w_qkv, ((1,), (1,)))
+    )
+    back = lambda slots, j: dot(
+        slots.reshape(4, length, 3 * part)[j], w_qkv, ((1,), (1,))
+    )
     due = (
-        lambda: (back(1), back(3)),
-        lambda one, three: (back(2), swap(jnp.stack([one, three]).astype(BF16), 1)),
-        lambda two, from_core: (
-            back(0) + from_core[0].astype(F32),
+        lambda: (qkv_grad, back(qkv_grad, 1), back(qkv_grad, 3)),
+        lambda slots, one, three: (
+            slots,
+            back(slots, 2),
+            swap(jnp.stack([one, three]).astype(BF16), 1),
+        ),
+        lambda slots, two, from_core: (
+            back(slots, 0) + from_core[0].astype(F32),
             two + from_core[1].astype(F32),
             down_owned,
         ),
         lambda zero, two, down: (zero, swap(two.astype(BF16), 2), down),
     )
     qkv_owned, (normed_grad, from_side, down_owned) = ring_scatter(
-        [qkv_w_grad, small], n_shard, shard, due
+        [qkv_w_grad, rows_in_order(ring, small)], n_shard, due
     )
     normed_grad = normed_grad + from_side.astype(F32)
     weighted = normed_grad * gain_one

time: 754 us -> 715 us (0.948)
  waiting for transfers between devices: 256 us -> 216 us
  local copies, waits for them, and re-layouts: 85.2 us -> 105 us
  between operations: 33.3 us -> 16.4 us
  Pallas kernels: 79.9 us -> 96.8 us
  matrix products: 131 us -> 123 us
    ppermute x47, waiting for transfers between devices: 166 us -> 128 us  [swap(): return lax.ppermute(x, 'rep', [(i, i ^ mask) for i in range(4)])]
    pallas_call x0 -> x2, Pallas kernels: none -> 17.1 us  [the longest x1 11.4 us: normed_in_order(): pl.pallas_call(normed_kernel, grid_spec=pltpu.PrefetchScalarGridSpec(num_...]
    unnamed x217 -> x222, local copies, waits for them, and re-layouts: 20.9 us -> 32.4 us
    dynamic_slice x17 -> x3, local copies, waits for them, and re-layouts: 10.7 us -> 0.17 us  [to_pair(): own = lax.dynamic_index_in_dim(x, core, 0, keepdims=False)]
    dot_general x34 -> x35, matrix products: 131 us -> 123 us  [dot(): return lax.dot_general(a, b, (dims, ((), ())), preferred_element_type=F32)]
  transfers between devices with their start and end apart: 69 -> 69, of which waited for: 35 -> 35; matrix products, arithmetic and copies ran while one was open for 37% -> 39% of each run, Pallas kernels for 11% -> 14%
where the time goes in v4:
time: 715 us; the launch traced here: 709 us
  waiting for transfers between devices  216 us (30%)
  matrix products  123 us (17%)
  other arithmetic  108 us (15%)
  local copies, waits for them, and re-layouts  105 us (15%)
  Pallas kernels  96.8 us (14%)
  starting transfers between devices  43.7 us (6%)
  between operations  16.4 us (2%)
    ppermute x47, waiting for transfers between devices, swap(): return lax.ppermute(x, 'rep', [(i, i ^ mask) for i in range(4)])  128 us
    dot_general x35, matrix products, dot(): return lax.dot_general(a, b, (dims, ((), ())), preferred_element_type=F32)  123 us
    ppermute x16, waiting for transfers between devices, ring_step(): lax.ppermute(x, 'shard', [(b, a) for a, b in pairs] if back else pairs)  88 us
    pallas_call x1, Pallas kernels, attend_back(): pl.pallas_call(functools.partial(attend_back_kernel, dim ** (-0.5)), grid...  38.2 us
    pallas_call x1, Pallas kernels, attend(): pl.pallas_call(functools.partial(attend_kernel, dim ** (-0.5)), grid=(tok...  35 us
    unnamed x222, local copies, waits for them, and re-layouts  32.4 us
    ppermute x47, starting transfers between devices, swap(): return lax.ppermute(x, 'rep', [(i, i ^ mask) for i in range(4)])  25.1 us
    ppermute x16, starting transfers between devices, ring_step(): lax.ppermute(x, 'shard', [(b, a) for a, b in pairs] if back else pairs)  17.5 us
  transfers between devices with their start and end apart: 69, of which 35 were waited for; matrix products, arithmetic and copies ran while one was open for 39% of the time, Pallas kernels for 14%

profile of v4, /device:TPU:0, one launch (start us, length us, event | category | flops | bytes accessed | tf_op | source)
XLA Modules:
  0.0 709.0 jit_solution(4036616038720731041)
XLA Ops:
  31.9 10.7 %collective-permute-done.1.refs_1_ = bf16[256,1664]{1,0:T(8,128)(2,1)} collective-permute-done((bf16[256,1664]{1,0:T(8,128)(2,1)}, bf16[256,1664]{1,0:T(8,128)(2,1)}, u32[]{:S(2)}, u32[]{:S(2)}) %collective-permute-start.1) | collective-permute-done | bytes 852000 | tf_op jit(solution)/shard_map/ppermute | solution.py:235
  49.3 14.7 %collective-permute-done.3.refs_3_ = bf16[256,1664]{1,0:T(8,128)(2,1)} collective-permute-done((bf16[256,1664]{1,0:T(8,128)(2,1)}, bf16[256,1664]{1,0:T(8,128)(2,1)}, u32[]{:S(2)}, u32[]{:S(2)}) %collective-permute-start.3) | collective-permute-done | bytes 852000 | tf_op jit(solution)/shard_map/ppermute | solution.py:235
  72.9 10.9 %collective-permute-done.5.refs_5_ = bf16[256,1664]{1,0:T(8,128)(2,1)S(1)} collective-permute-done((bf16[256,1664]{1,0:T(8,128)(2,1)}, bf16[256,1664]{1,0:T(8,128)(2,1)S(1)}, u32[]{:S(2)}, u32[]{:S(2)}) %collective-permute-start.5) | collective-permute-done | bytes 852000 | tf_op jit(solution)/shard_map/ppermute | solution.py:235
  100.7 10.2 %collective-permute-done.15 = bf16[2,128,2048]{2,1,0:T(8,128)(2,1)} collective-permute-done((bf16[2,128,2048]{2,1,0:T(8,128)(2,1)S(1)}, bf16[2,128,2048]{2,1,0:T(8,128)(2,1)}, u32[]{:S(2)}, u32[]{:S(2)}) %collective-permute-start.15) | collective-permute-done | bytes 1048608 | tf_op jit(solution)/shard_map/ppermute | solution.py:36
  129.6 17.5 %fusion.3.q_ref.k_ref.v_ref = f32[2048,1536]{1,0:T(8,128)S(1)} fusion(bf16[2048,1536]{1,0:T(8,128)(2,1)} %get-tuple-element.104, bf16[2048,2048]{1,0:T(8,128)(2,1)} %constant_dynamic-update-slice_fusion.hidden, f32[2048]{0:T(1024)S(1)} %bitcast.270, f32[2048]{0:T(1024)S(1)} %add_rsqrt_fusion), kind=kOutput, calls=%fused_computation.5 | convolution fusion | flops 12901679104 | bytes 27279360 | tf_op jit(solution)/shard_map/dot_general | solution.py:32
  168.2 35.0 %attend.1 = (bf16[2048,512]{1,0:T(8,128)(2,1)}, bf16[2048,512]{1,0:T(8,128)(2,1)}, bf16[2048,512]{1,0:T(8,128)(2,1)}, bf16[2048,512]{1,0:T(8,128)(2,1)}) custom-call(f32[2048,1536]{1,0:T(8,128)} %copy-done.2, f32[2048,1536]{1,0:T(8,128)} %copy-done.2, f32[2048,1536]{1,0:T(8,128)} %copy-done.2, f32[2048,1]{1,0:T(8,128)} %get-tuple-element.301.q_scale, ...), custom_call_target="tpu_custom_call" | custom-call | flops 2147483648 | bytes 20971520 | tf_op jit(solution)/shard_map/attend/pallas_call | solution.py:183
  203.2 6.8 collective-permute-done.19
  221.9 17.1 %collective-permute-done.20 = bf16[2,512,512]{2,1,0:T(8,128)(2,1)S(1)} collective-permute-done((bf16[2,512,512]{2,1,0:T(8,128)(2,1)S(1)}, bf16[2,512,512]{2,1,0:T(8,128)(2,1)S(1)}, u32[]{:S(2)}, u32[]{:S(2)}) %collective-permute-start.20) | collective-permute-done | bytes 1048608 | tf_op jit(solution)/shard_map/ppermute | solution.py:36
  243.9 7.9 %multiply_reduce_fusion.6 = (f32[512]{0:T(512)S(1)}, f32[512,2048]{1,0:T(8,128)S(1)}) fusion(bf16[2048,2048]{1,0:T(8,128)(2,1)} %bitcast.239, bf16[512,512]{1,0:T(8,128)(2,1)S(1)} %get-tuple-element.269, bf16[512,512]{1,0:T(8,128)(2,1)S(1)} %get-tuple-element.268, bf16[512,512]{1,0:T(8,128)(2,1)S(1)} %get-tuple-element.267, ...), kind=kOutput, calls=%fused_computation.43 | convolution fusion | flops 4307549696 | bytes 16779264 | tf_op jit(solution)/shard_map/dot_general | solution.py:32
  261.5 11.4 %normed_in_order.1 = bf16[2048,2048]{1,0:T(8,128)(2,1)} custom-call(s32[8]{0:T(128)} %fusion.126.ids, bf16[2048,2048]{1,0:T(8,128)(2,1)} %constant_dynamic-update-slice_fusion.hidden, f32[2048,1]{1,0:T(8,128)} %copy.134.scale, f32[1,2048]{1,0:T(1,128)} %copy-done.77), custom_call_target="tpu_custom_call" | custom-call | flops 8388608 | bytes 16777216 | tf_op jit(solution)/shard_map/normed_in_order/pallas_call | solution.py:317
  273.7 9.6 %collective-permute-done.27 = bf16[2,128,2048]{2,1,0:T(8,128)(2,1)} collective-permute-done((bf16[2,128,2048]{2,1,0:T(8,128)(2,1)}, bf16[2,128,2048]{2,1,0:T(8,128)(2,1)}, u32[]{:S(2)}, u32[]{:S(2)}) %collective-permute-start.27) | collective-permute-done | bytes 1048608 | tf_op jit(solution)/shard_map/ppermute | solution.py:36
  323.2 12.9 %collective-permute-done.28 = bf16[2,128,2048]{2,1,0:T(8,128)(2,1)} collective-permute-done((bf16[2,128,2048]{2,1,0:T(8,128)(2,1)}, bf16[2,128,2048]{2,1,0:T(8,128)(2,1)}, u32[]{:S(2)}, u32[]{:S(2)}) %collective-permute-start.28) | collective-permute-done | bytes 1048608 | tf_op jit(solution)/shard_map/ppermute | solution.py:36
  386.6 13.2 %collective-permute-done.33 = bf16[2,512,512]{2,1,0:T(8,128)(2,1)S(1)} collective-permute-done((bf16[2,512,512]{2,1,0:T(8,128)(2,1)S(1)}, bf16[2,512,512]{2,1,0:T(8,128)(2,1)S(1)}, u32[]{:S(2)}, u32[]{:S(2)}) %collective-permute-start.33) | collective-permute-done | bytes 1048608 | tf_op jit(solution)/shard_map/ppermute | solution.py:36
  408.9 38.2 %attend_back.1 = (f32[2048,512]{1,0:T(8,128)}, f32[2048,512]{1,0:T(8,128)}, bf16[2048,512]{1,0:T(8,128)(2,1)}) custom-call(bf16[2048,512]{1,0:T(8,128)(2,1)} %get-tuple-element.116.queries, bf16[2048,512]{1,0:T(8,128)(2,1)} %get-tuple-element.117.keys, bf16[2048,512]{1,0:T(8,128)(2,1)} %get-tuple-element.118.values, ...), custom_call_target="tpu_custom_call" | custom-call | flops 5368709120 | bytes 18874368 | tf_op jit(solution)/shard_map/attend_back/pallas_call | solution.py:206
  447.1 7.2 %multiply_reduce_fusion = (f32[512]{0:T(512)S(1)}, f32[2048]{0:T(1024)S(1)}, f32[2048]{0:T(1024)S(1)}, f32[512]{0:T(512)S(1)}) fusion(f32[2048,512]{1,0:T(8,128)} %get-tuple-element.128, f32[2048,1536]{1,0:T(8,128)} %copy-done.2, f32[2048]{0:T(1024)S(1)} %get-tuple-element.234, f32[512]{0:T(512)S(1)} %bitcast.289, f32[2048,512]{1,0:T(8,128)} %get-tuple-element.127, ...), kind=kLoop, calls=%fused_computation.31 | loop fusion | flops 12577792 | bytes 16818176 | tf_op jit(solution)/shard_map/reduce_sum | solution.py:630
  492.7 19.3 %convolution_convert_fusion = bf16[2048,1536]{1,0:T(8,128)(2,1)} fusion(bf16[2048,2048]{1,0:T(8,128)(2,1)} %normed_in_order.1, bf16[2048,512]{1,0:T(8,128)(2,1)} %get-tuple-element.134, bf16[2048,512]{1,0:T(8,128)(2,1)} %get-tuple-element.252, bf16[2048,512]{1,0:T(8,128)(2,1)S(1)} %get-tuple-element.251), kind=kOutput, calls=%fused_computation.10 | convolution fusion | flops 12906921984 | bytes 20971520 | tf_op jit(solution)/shard_map/dot_general | solution.py:32
  515.3 6.9 fusion.33
  535.3 8.9 %collective-permute-done.42 = bf16[128,1664]{1,0:T(8,128)(2,1)S(1)} collective-permute-done((bf16[128,1664]{1,0:T(8,128)(2,1)S(1)}, bf16[128,1664]{1,0:T(8,128)(2,1)S(1)}, u32[]{:S(2)}, u32[]{:S(2)}) %collective-permute-start.42) | collective-permute-done | bytes 426016 | tf_op jit(solution)/shard_map/ppermute | solution.py:235
  568.5 14.1 %collective-permute-done.44 = bf16[256,1664]{1,0:T(8,128)(2,1)S(1)} collective-permute-done((bf16[256,1664]{1,0:T(8,128)(2,1)S(1)}, bf16[256,1664]{1,0:T(8,128)(2,1)S(1)}, u32[]{:S(2)}, u32[]{:S(2)}) %collective-permute-start.44) | collective-permute-done | bytes 852000 | tf_op jit(solution)/shard_map/ppermute | solution.py:235
  589.1 7.7 %convert_add_fusion.3 = f32[512,2048]{1,0:T(8,128)} fusion(bf16[2048,1536]{1,0:T(8,128)(2,1)} %get-tuple-element.104, bf16[2,512,2048]{2,1,0:T(8,128)(2,1)S(1)} %collective-permute-done.45, bf16[2048,1536]{1,0:T(8,128)(2,1)S(1)} %copy-done.23), kind=kOutput, calls=%fused_computation.29 | convolution fusion | flops 3223322624 | bytes 14155776 | tf_op jit(solution)/shard_map/dot_general | solution.py:32
  596.8 7.6 %collective-permute-done.47 = bf16[256,1664]{1,0:T(8,128)(2,1)} collective-permute-done((bf16[256,1664]{1,0:T(8,128)(2,1)}, bf16[256,1664]{1,0:T(8,128)(2,1)}, u32[]{:S(2)}, u32[]{:S(2)}) %collective-permute-start.47) | collective-permute-done | bytes 852000 | tf_op jit(solution)/shard_map/ppermute | solution.py:235
  620.6 10.3 %collective-permute-done.49 = bf16[256,1664]{1,0:T(8,128)(2,1)S(1)} collective-permute-done((bf16[256,1664]{1,0:T(8,128)(2,1)S(1)}, bf16[256,1664]{1,0:T(8,128)(2,1)S(1)}, u32[]{:S(2)}, u32[]{:S(2)}) %collective-permute-start.49) | collective-permute-done | bytes 852000 | tf_op jit(solution)/shard_map/ppermute | solution.py:235
  633.0 20.3 %collective-permute-done.50 = bf16[512,2048]{1,0:T(8,128)(2,1)S(1)} collective-permute-done((bf16[512,2048]{1,0:T(8,128)(2,1)}, bf16[512,2048]{1,0:T(8,128)(2,1)S(1)}, u32[]{:S(2)}, u32[]{:S(2)}) %collective-permute-start.50) | collective-permute-done | bytes 2097184 | tf_op jit(solution)/shard_map/ppermute | solution.py:36
  666.4 11.6 %collective-permute-done.52 = bf16[256,1664]{1,0:T(8,128)(2,1)} collective-permute-done((bf16[256,1664]{1,0:T(8,128)(2,1)S(1)}, bf16[256,1664]{1,0:T(8,128)(2,1)}, u32[]{:S(2)}, u32[]{:S(2)}) %collective-permute-start.52) | collective-permute-done | bytes 852000 | tf_op jit(solution)/shard_map/ppermute | solution.py:36
  (555 shorter events, 362.3 us)
Async XLA Ops:
  7.2 154.4 %all-gather.4.cloned.1.call-start = ((), (), s32[]{:S(2)}) async-start(), calls=%async_computation.3 | async-start | bytes 2359296 | tf_op jit(solution)/shard_map/all_gather | solution.py:382
  25.3 59.8 %collective-permute-start.7 = (bf16[512,2048]{1,0:T(8,128)(2,1)}, bf16[512,2048]{1,0:T(8,128)(2,1)}, u32[]{:S(2)}, u32[]{:S(2)}) collective-permute-start(bf16[512,2048]{1,0:T(8,128)(2,1)} %param.19), channel_id=1, source_target_pairs={{0,2},{1,3},{2,0},{3,1},{4,6},{5,7},{6,4},{7,5},{8,10},{9,11},{10,... | collective-permute-start | bytes 6291464 | tf_op jit(solution)/shard_map/ppermute | solution.py:36
  47.2 43.0 %collective-permute-start = (bf16[512,2048]{1,0:T(8,128)(2,1)S(1)}, bf16[512,2048]{1,0:T(8,128)(2,1)}, u32[]{:S(2)}, u32[]{:S(2)}) collective-permute-start(bf16[512,2048]{1,0:T(8,128)(2,1)S(1)} %copy-done.14), channel_id=1, source_target_pairs={{0,1},{1,0},{2,3},{3,2},{4,5},{5,4},{6,7},{7,6},{8,9},{9,8},{10,11... | collective-permute-start | bytes 6291464 | tf_op jit(solution)/shard_map/ppermute | solution.py:36
  85.2 28.5 %collective-permute-start.12 = (bf16[512,2048]{1,0:T(8,128)(2,1)}, bf16[512,2048]{1,0:T(8,128)(2,1)}, u32[]{:S(2)}, u32[]{:S(2)}) collective-permute-start(bf16[512,2048]{1,0:T(8,128)(2,1)} %collective-permute-done.7), channel_id=1, source_target_pairs={{0,1},{1,0},{2,3},{3,2},{4,5},{5,4},{6,7},{7,6},{8,9},{9,8},{10,11... | collective-permute-start | bytes 6291464 | tf_op jit(solution)/shard_map/ppermute | solution.py:36
  94.3 27.6 %collective-permute-start.13 = (bf16[128,1664]{1,0:T(8,128)(2,1)}, bf16[128,1664]{1,0:T(8,128)(2,1)}, u32[]{:S(2)}, u32[]{:S(2)}) collective-permute-start(bf16[128,1664]{1,0:T(8,128)(2,1)} %slice.343), channel_id=1, source_target_pairs={{8,0},{16,8},{24,16},{28,24},{20,28},{12,20},{4,12},{0,4},{9,1},{1... | collective-permute-start | bytes 1277960 | tf_op jit(solution)/shard_map/ppermute | solution.py:235
  95.6 26.4 %collective-permute-start.14 = (bf16[128,1664]{1,0:T(8,128)(2,1)}, bf16[128,1664]{1,0:T(8,128)(2,1)}, u32[]{:S(2)}, u32[]{:S(2)}) collective-permute-start(bf16[128,1664]{1,0:T(8,128)(2,1)} %slice.344), channel_id=1, source_target_pairs={{0,8},{8,16},{16,24},{24,28},{28,20},{20,12},{12,4},{4,0},{1,9},{9... | collective-permute-start | bytes 1277960 | tf_op jit(solution)/shard_map/ppermute | solution.py:235
  97.2 141.9 %all-gather.6.cloned.1.call-start = ((), (), s32[]{:S(2)}) async-start(), calls=%async_computation.4 | async-start | bytes 4718592 | tf_op jit(solution)/shard_map/all_gather | solution.py:382
  152.5 136.4 %all-gather.8.cloned.1.call-start = ((), (), s32[]{:S(2)}) async-start(), calls=%async_computation.5 | async-start | bytes 2359296 | tf_op jit(solution)/shard_map/all_gather | solution.py:382
  161.6 41.6 %collective-permute-start.18 = (bf16[8,64,2048]{2,1,0:T(8,128)(2,1)}, bf16[8,64,2048]{2,1,0:T(8,128)(2,1)}, u32[]{:S(2)}, u32[]{:S(2)}) collective-permute-start(bf16[8,64,2048]{2,1,0:T(8,128)(2,1)} %bitcast.251), channel_id=1, source_target_pairs={{0,1},{1,0},{2,3},{3,2},{4,5},{5,4},{6,7},{7,6},{8,9},{9,8},{10,11... | collective-permute-start | bytes 6291464 | tf_op jit(solution)/shard_map/ppermute | solution.py:36
  161.7 48.3 %collective-permute-start.19 = (bf16[8,64,2048]{2,1,0:T(8,128)(2,1)}, bf16[8,64,2048]{2,1,0:T(8,128)(2,1)}, u32[]{:S(2)}, u32[]{:S(2)}) collective-permute-start(bf16[8,64,2048]{2,1,0:T(8,128)(2,1)} %bitcast.252), channel_id=1, source_target_pairs={{0,2},{1,3},{2,0},{3,1},{4,6},{5,7},{6,4},{7,5},{8,10},{9,11},{10,... | collective-permute-start | bytes 6291464 | tf_op jit(solution)/shard_map/ppermute | solution.py:36
  213.4 25.6 %collective-permute-start.20 = (bf16[2,512,512]{2,1,0:T(8,128)(2,1)S(1)}, bf16[2,512,512]{2,1,0:T(8,128)(2,1)S(1)}, u32[]{:S(2)}, u32[]{:S(2)}) collective-permute-start(bf16[2,512,512]{2,1,0:T(8,128)(2,1)S(1)} %bitcast.264), channel_id=1, source_target_pairs={{0,2},{1,3},{2,0},{3,1},{4,6},{5,7},{6,4},{7,5},{8,10},{9,11},{10,... | collective-permute-start | bytes 3145736 | tf_op jit(solution)/shard_map/ppermute | solution.py:36
  214.5 25.5 %collective-permute-start.23 = (bf16[512,512]{1,0:T(8,128)(2,1)}, bf16[512,512]{1,0:T(8,128)(2,1)}, u32[]{:S(2)}, u32[]{:S(2)}) collective-permute-start(bf16[512,512]{1,0:T(8,128)(2,1)} %slice.363), channel_id=1, source_target_pairs={{0,1},{1,0},{2,3},{3,2},{4,5},{5,4},{6,7},{7,6},{8,9},{9,8},{10,11... | collective-permute-start | bytes 1572872 | tf_op jit(solution)/shard_map/ppermute | solution.py:36
  239.9 275.4 %reduce-scatter.4.cloned.1.call-start = ((), (), s32[]{:S(2)}) async-start(), calls=%async_computation.6 | async-start | bytes 4718592 | tf_op jit(solution)/shard_map/reduce_scatter | solution.py:386
  257.9 25.5 %collective-permute-start.27 = (bf16[2,128,2048]{2,1,0:T(8,128)(2,1)}, bf16[2,128,2048]{2,1,0:T(8,128)(2,1)}, u32[]{:S(2)}, u32[]{:S(2)}) collective-permute-start(bf16[2,128,2048]{2,1,0:T(8,128)(2,1)} %pad_maximum_fusion.12), channel_id=1, source_target_pairs={{0,2},{1,3},{2,0},{3,1},{4,6},{5,7},{6,4},{7,5},{8,10},{9,11},{10,... | collective-permute-start | bytes 3145736 | tf_op jit(solution)/shard_map/ppermute | solution.py:36
  339.8 257.0 %reduce-scatter.6.cloned.1.call-start = ((), (), s32[]{:S(2)}) async-start(), calls=%async_computation.7 | async-start | bytes 2359296 | tf_op jit(solution)/shard_map/reduce_scatter | solution.py:386
  374.2 25.6 %collective-permute-start.33 = (bf16[2,512,512]{2,1,0:T(8,128)(2,1)S(1)}, bf16[2,512,512]{2,1,0:T(8,128)(2,1)S(1)}, u32[]{:S(2)}, u32[]{:S(2)}) collective-permute-start(bf16[2,512,512]{2,1,0:T(8,128)(2,1)S(1)} %pad_maximum_fusion.14), channel_id=1, source_target_pairs={{0,2},{1,3},{2,0},{3,1},{4,6},{5,7},{6,4},{7,5},{8,10},{9,11},{10,... | collective-permute-start | bytes 3145736 | tf_op jit(solution)/shard_map/ppermute | solution.py:36
  401.6 264.8 %reduce-scatter.8.cloned.1.call-start = ((), (), s32[]{:S(2)}) async-start(), calls=%async_computation.8 | async-start | bytes 2359296 | tf_op jit(solution)/shard_map/reduce_scatter | solution.py:386
  405.3 83.5 %collective-permute-start.38 = (bf16[8,64,2048]{2,1,0:T(8,128)(2,1)}, bf16[8,64,2048]{2,1,0:T(8,128)(2,1)}, u32[]{:S(2)}, u32[]{:S(2)}) collective-permute-start(bf16[8,64,2048]{2,1,0:T(8,128)(2,1)} %dynamic-slice_bitcast_fusion), channel_id=1, source_target_pairs={{0,2},{1,3},{2,0},{3,1},{4,6},{5,7},{6,4},{7,5},{8,10},{9,11},{10,... | collective-permute-start | bytes 6291464 | tf_op jit(solution)/shard_map/ppermute | solution.py:36
  480.0 35.3 %collective-permute-start.39 = (bf16[2,128,2048]{2,1,0:T(8,128)(2,1)}, bf16[2,128,2048]{2,1,0:T(8,128)(2,1)}, u32[]{:S(2)}, u32[]{:S(2)}) collective-permute-start(bf16[2,128,2048]{2,1,0:T(8,128)(2,1)} %slice.645), channel_id=1, source_target_pairs={{0,2},{1,3},{2,0},{3,1},{4,6},{5,7},{6,4},{7,5},{8,10},{9,11},{10,... | collective-permute-start | bytes 3145736 | tf_op jit(solution)/shard_map/ppermute | solution.py:36
  530.6 31.2 %collective-permute-start.59 = (bf16[256,1024]{1,0:T(8,128)(2,1)}, bf16[256,1024]{1,0:T(8,128)(2,1)}, u32[]{:S(2)}, u32[]{:S(2)}) collective-permute-start(bf16[256,1024]{1,0:T(8,128)(2,1)} %reduce-scatter.4.cloned.1.call-done), channel_id=1, source_target_pairs={{0,1},{1,0},{2,3},{3,2},{4,5},{5,4},{6,7},{7,6},{8,9},{9,8},{10,11... | collective-permute-start | bytes 1572872 | tf_op jit(solution)/shard_map/ppermute | solution.py:36
  546.9 35.6 %collective-permute-start.45 = (bf16[2,512,2048]{2,1,0:T(8,128)(2,1)S(1)}, bf16[2,512,2048]{2,1,0:T(8,128)(2,1)S(1)}, u32[]{:S(2)}, u32[]{:S(2)}) collective-permute-start(bf16[2,512,2048]{2,1,0:T(8,128)(2,1)S(1)} %pad_maximum_fusion.2), channel_id=1, source_target_pairs={{0,1},{1,0},{2,3},{3,2},{4,5},{5,4},{6,7},{7,6},{8,9},{9,8},{10,11... | collective-permute-start | bytes 12582920 | tf_op jit(solution)/shard_map/ppermute | solution.py:36
  552.7 29.8 %collective-permute-start.44 = (bf16[256,1664]{1,0:T(8,128)(2,1)S(1)}, bf16[256,1664]{1,0:T(8,128)(2,1)S(1)}, u32[]{:S(2)}, u32[]{:S(2)}) collective-permute-start(bf16[256,1664]{1,0:T(8,128)(2,1)S(1)} %pad_maximum_fusion.15), channel_id=1, source_target_pairs={{8,0},{16,8},{24,16},{28,24},{20,28},{12,20},{4,12},{0,4},{9,1},{1... | collective-permute-start | bytes 2555912 | tf_op jit(solution)/shard_map/ppermute | solution.py:235
  553.7 28.8 %collective-permute-start.43 = (bf16[256,1664]{1,0:T(8,128)(2,1)S(1)}, bf16[256,1664]{1,0:T(8,128)(2,1)S(1)}, u32[]{:S(2)}, u32[]{:S(2)}) collective-permute-start(bf16[256,1664]{1,0:T(8,128)(2,1)S(1)} %fusion.69), channel_id=1, source_target_pairs={{0,8},{8,16},{16,24},{24,28},{28,20},{20,12},{12,4},{4,0},{1,9},{9... | collective-permute-start | bytes 2555912 | tf_op jit(solution)/shard_map/ppermute | solution.py:235
  607.1 46.3 %collective-permute-start.50 = (bf16[512,2048]{1,0:T(8,128)(2,1)}, bf16[512,2048]{1,0:T(8,128)(2,1)S(1)}, u32[]{:S(2)}, u32[]{:S(2)}) collective-permute-start(bf16[512,2048]{1,0:T(8,128)(2,1)} %convert_add_fusion.2), channel_id=1, source_target_pairs={{0,2},{1,3},{2,0},{3,1},{4,6},{5,7},{6,4},{7,5},{8,10},{9,11},{10,... | collective-permute-start | bytes 6291464 | tf_op jit(solution)/shard_map/ppermute | solution.py:36
  (151 other events, 1897.5 us)
Sparse Core Ops, SparseCore 0:
  97.3 46.4 all-gather.3
  152.6 71.8 all-gather.5
  240.0 47.6 all-gather.7
  339.9 86.7 reduce-scatter.3
  430.6 68.4 reduce-scatter.5
  503.1 74.2 reduce-scatter.7

commit v5 on v4

--- a/solution.py
+++ b/solution.py
@@ -476,7 +476,6 @@
         (swap(hidden_in, 2), cosine, sine, upstream_pair, output_block, gate_up_block, down_block),
     )
     hidden_side, cosine, sine, upstream_pair, output_block, gate_up_block, down_block = arrays
-    slot_upstream = jnp.concatenate([upstream_pair, swap(upstream_pair, 2)], 0)
     hidden_all = jnp.concatenate(
         [hidden_in, swap(hidden_in, 1), hidden_side, swap(hidden_side, 1)], 0
     )
@@ -488,7 +487,6 @@
     starts = np.stack([ids[:, k] * my_rows + first for _, k, first in pieces], 1)
     starts, ring = of_shard(starts, shard), of_shard(ids, shard)
     w_qkv, small_w = place_rows([piece for piece, _, _ in pieces], starts, width, 3 * part)
-    w_qkv, slot_upstream = tie(w_qkv, slot_upstream)
     router_w = small_w[:, :routed]
     gains = small_w[:, routed : routed + 4].T.astype(F32)
     w_out_part = shard_gather(output_block).reshape(n_shard, quarter, width)
@@ -514,7 +512,9 @@
         return dot(select, high, ((0,), (0,))) + dot(select, low, ((0,), (0,)))
 
     normed = (hidden_all.astype(F32) * normed_scale * gain_one).astype(BF16)
-    qkv = dot(normed, w_qkv)
+    w_qkv, upstream_pair = tie(w_qkv, upstream_pair)
+    qkv, upstream_side = tie(dot(normed, w_qkv), swap(upstream_pair, 2))
+    slot_upstream = jnp.concatenate([upstream_pair, upstream_side], 0)
     query_raw, key_raw = qkv[:, :part], qkv[:, part : 2 * part]
     squares = jnp.stack([jnp.sum(query_raw * query_raw, -1), jnp.sum(key_raw * key_raw, -1)], -1)
     squares = rep_sum(squares.reshape(4, length, 2)).reshape(-1, 2)
@@ -558,7 +558,13 @@
     slot_gates = to_experts(jnp.sum(select_wide * window.T[:, None, :], -1))
     pair = to_pair(dot(select, inner).astype(BF16).reshape(experts, cap, width))
     normed_ring = normed_in_order(ring, hidden_all, normed_scale, gain_one[None])
-    from_side, normed_ring = tie(swap(pair, 2), normed_ring)
+    at = lambda x, i, axis: lax.dynamic_index_in_dim(x, i, axis, keepdims=False)
+    half = lambda which: at(mixed.reshape(length, n_shard, 2, 2, quarter), which, 3).reshape(
+        length, width // 2
+    )
+    from_side, normed_ring, mixed_own, mixed_other = tie(
+        swap(pair, 2), normed_ring, half(core), half(1 - core)
+    )
     slot_inputs = jnp.concatenate([pair, from_side], 0)
     slot_inputs = slot_inputs.reshape(4 * cap, width)
 
@@ -601,13 +607,9 @@
     piece = lambda j: lax.dynamic_slice_in_dim(mixed_grad, (rep ^ j) * part, part, 1)
     from_side = swap(jnp.stack([piece(2), piece(3)]), 2)
     from_core, branch_grad = tie(swap(piece(1), 1), branch_grad)
-    at = lambda x, i, axis: lax.dynamic_index_in_dim(x, i, axis, keepdims=False)
-    half = lambda which: at(mixed.reshape(length, n_shard, 2, 2, quarter), which, 3)
-    half_grad = lambda which: dot(
-        half(which).reshape(length, width // 2), branch_grad, ((0,), (0,))
-    ).astype(BF16)
-    out_there = swap(half_grad(1 - core), 1)
-    out_w_grad = (half_grad(core).astype(F32) + out_there).astype(BF16)
+    half_grad = lambda half: dot(half, branch_grad, ((0,), (0,))).astype(BF16)
+    out_there = swap(half_grad(mixed_other), 1)
+    out_w_grad = (half_grad(mixed_own).astype(F32) + out_there).astype(BF16)
     from_side, out_w_grad, returned = tie(from_side, out_w_grad, returned)
     grads = jnp.concatenate([piece(0), from_core, from_side[0], swap(from_side[1], 1)], 0)
     out_w_grad = out_w_grad.reshape(n_shard, 2, quarter, width)
@@ -659,22 +661,27 @@
         ),
         lambda slots, two, from_core: (
             back(slots, 0) + from_core[0].astype(F32),
-            two + from_core[1].astype(F32),
+            (two + from_core[1].astype(F32)).astype(BF16)[length // 2 :],
+            swap((two + from_core[1].astype(F32)).astype(BF16)[: length // 2], 2),
             down_owned,
         ),
-        lambda zero, two, down: (zero, swap(two.astype(BF16), 2), down),
-    )
-    qkv_owned, (normed_grad, from_side, down_owned) = ring_scatter(
+        lambda zero, rest, top, down: (zero, top, swap(rest, 2), down),
+    )
+    qkv_owned, (normed_grad, top, rest, down_owned) = ring_scatter(
         [qkv_w_grad, rows_in_order(ring, small)], n_shard, due
     )
-    normed_grad = normed_grad + from_side.astype(F32)
+    normed_grad = normed_grad + jnp.concatenate([top, rest], 0).astype(F32)
     weighted = normed_grad * gain_one
     scale_one = normed_scale[:length]
     inner_mean = jnp.mean(weighted * hidden, -1, keepdims=True)
     hidden_part = scale_one * weighted - hidden * scale_one * scale_one * scale_one * inner_mean
     input_grad = residual_grad + hidden_part
 
-    qkv_owned = qkv_owned.astype(BF16)
+    gain_part = jnp.sum(qkv_block.astype(F32) * qkv_owned[:, : 3 * part], 1, keepdims=True)
+    column = jnp.arange(128)[None, :] == routed + 3
+    qkv_owned = jnp.concatenate(
+        [qkv_owned[:, : 3 * part], jnp.where(column, gain_part, qkv_owned[:, 3 * part :])], 1
+    ).astype(BF16)
     qkv_core, qkv_side, out_owned = tie(swap(qkv_owned, 1), swap(qkv_owned, 2), out_owned)
     qkv_pieces = in_order([qkv_owned, qkv_core, qkv_side, swap(qkv_side, 1)], rep)
     spread = lambda i: jnp.concatenate(
@@ -682,9 +689,7 @@
     ).astype(F32)
     grads_qkv = [spread(i) for i in range(3)]
     small = sum(p[:, 3 * part :].astype(F32) for p in qkv_pieces)
-    gain_one_grad = sum(
-        jnp.sum(w.astype(F32) * g, 1) for w, g in zip((w_query, w_key, w_value), grads_qkv)
-    ) / attn_gain.astype(F32)
+    gain_one_grad = small[:, routed + 3] / attn_gain.astype(F32)
     out_full = jnp.concatenate(in_order(rep_gather(out_owned.astype(BF16)), rep), 0).astype(F32)
     gu_pieces = in_order(rep_gather(gate_up_owned.astype(BF16)), rep)
     dn_pieces = in_order(rep_gather(down_owned.astype(BF16)), rep)

time: 715 us -> 696 us (0.973)
  waiting for transfers between devices: 216 us -> 203 us
    ppermute x47 -> x48, waiting for transfers between devices: 128 us -> 107 us  [swap(): return lax.ppermute(x, 'rep', [(i, i ^ mask) for i in range(4)])]
    ppermute x16, waiting for transfers between devices: 88 us -> 96.5 us  [ring_step(): lax.ppermute(x, 'shard', [(b, a) for a, b in pairs] if back else pairs)]
    unnamed x222 -> x228, local copies, waits for them, and re-layouts: 32.4 us -> 30.3 us
    ppermute x47 -> x48, starting transfers between devices: 25.1 us -> 25.3 us  [swap(): return lax.ppermute(x, 'rep', [(i, i ^ mask) for i in range(4)])]
  transfers between devices with their start and end apart: 69 -> 70, of which waited for: 35 -> 35; matrix products, arithmetic and copies ran while one was open for 39% -> 41% of each run, Pallas kernels for 14% -> 14%
where the time goes in v5:
time: 696 us; the launch traced here: 690 us
  waiting for transfers between devices  203 us (29%)
  matrix products  122 us (18%)
  other arithmetic  108 us (16%)
  local copies, waits for them, and re-layouts  99.4 us (14%)
  Pallas kernels  96.8 us (14%)
  starting transfers between devices  44.1 us (6%)
  between operations  16.3 us (2%)
    dot_general x35, matrix products, dot(): return lax.dot_general(a, b, (dims, ((), ())), preferred_element_type=F32)  122 us
    ppermute x48, waiting for transfers between devices, swap(): return lax.ppermute(x, 'rep', [(i, i ^ mask) for i in range(4)])  107 us
    ppermute x16, waiting for transfers between devices, ring_step(): lax.ppermute(x, 'shard', [(b, a) for a, b in pairs] if back else pairs)  96.5 us
    pallas_call x1, Pallas kernels, attend_back(): pl.pallas_call(functools.partial(attend_back_kernel, dim ** (-0.5)), grid...  38.3 us
    pallas_call x1, Pallas kernels, attend(): pl.pallas_call(functools.partial(attend_kernel, dim ** (-0.5)), grid=(tok...  35 us
    unnamed x228, local copies, waits for them, and re-layouts  30.3 us
    ppermute x48, starting transfers between devices, swap(): return lax.ppermute(x, 'rep', [(i, i ^ mask) for i in range(4)])  25.3 us
    ppermute x16, starting transfers between devices, ring_step(): lax.ppermute(x, 'shard', [(b, a) for a, b in pairs] if back else pairs)  17.9 us
  transfers between devices with their start and end apart: 70, of which 35 were waited for; matrix products, arithmetic and copies ran while one was open for 41% of the time, Pallas kernels for 14%

profile of v5, /device:TPU:0, one launch (start us, length us, event | category | flops | bytes accessed | tf_op | source)
XLA Modules:
  0.0 689.5 jit_solution(9817926249552479040)
XLA Ops:
  29.0 8.9 %collective-permute-done.1.refs_1_ = bf16[256,1664]{1,0:T(8,128)(2,1)} collective-permute-done((bf16[256,1664]{1,0:T(8,128)(2,1)}, bf16[256,1664]{1,0:T(8,128)(2,1)}, u32[]{:S(2)}, u32[]{:S(2)}) %collective-permute-start.1) | collective-permute-done | bytes 852000 | tf_op jit(solution)/shard_map/ppermute | solution.py:235
  44.7 14.7 %collective-permute-done.3.refs_3_ = bf16[256,1664]{1,0:T(8,128)(2,1)} collective-permute-done((bf16[256,1664]{1,0:T(8,128)(2,1)}, bf16[256,1664]{1,0:T(8,128)(2,1)}, u32[]{:S(2)}, u32[]{:S(2)}) %collective-permute-start.3) | collective-permute-done | bytes 852000 | tf_op jit(solution)/shard_map/ppermute | solution.py:235
  68.3 11.1 %collective-permute-done.5.refs_5_ = bf16[256,1664]{1,0:T(8,128)(2,1)} collective-permute-done((bf16[256,1664]{1,0:T(8,128)(2,1)}, bf16[256,1664]{1,0:T(8,128)(2,1)}, u32[]{:S(2)}, u32[]{:S(2)}) %collective-permute-start.5) | collective-permute-done | bytes 852000 | tf_op jit(solution)/shard_map/ppermute | solution.py:235
  115.9 17.7 %fusion.3.q_ref.k_ref.v_ref = f32[2048,1536]{1,0:T(8,128)S(1)} fusion(bf16[2048,1536]{1,0:T(8,128)(2,1)} %get-tuple-element.110, bf16[2048,2048]{1,0:T(8,128)(2,1)} %constant_dynamic-update-slice_fusion.hidden, f32[2048]{0:T(1024)S(1)} %bitcast.274, f32[2048]{0:T(1024)S(1)} %add_rsqrt_fusion), kind=kOutput, calls=%fused_computation.5 | convolution fusion | flops 12901679104 | bytes 27279360 | tf_op jit(solution)/shard_map/dot_general | solution.py:32
  155.2 35.0 %attend.1 = (bf16[2048,512]{1,0:T(8,128)(2,1)}, bf16[2048,512]{1,0:T(8,128)(2,1)}, bf16[2048,512]{1,0:T(8,128)(2,1)}, bf16[2048,512]{1,0:T(8,128)(2,1)}) custom-call(f32[2048,1536]{1,0:T(8,128)} %copy-done.2, f32[2048,1536]{1,0:T(8,128)} %copy-done.2, f32[2048,1536]{1,0:T(8,128)} %copy-done.2, f32[2048,1]{1,0:T(8,128)} %get-tuple-element.310.q_scale, ...), custom_call_target="tpu_custom_call" | custom-call | flops 2147483648 | bytes 20971520 | tf_op jit(solution)/shard_map/attend/pallas_call | solution.py:183
  190.2 7.0 %collective-permute-done.19 = bf16[8,64,2048]{2,1,0:T(8,128)(2,1)} collective-permute-done((bf16[8,64,2048]{2,1,0:T(8,128)(2,1)}, bf16[8,64,2048]{2,1,0:T(8,128)(2,1)}, u32[]{:S(2)}, u32[]{:S(2)}) %collective-permute-start.19) | collective-permute-done | bytes 2097184 | tf_op jit(solution)/shard_map/ppermute | solution.py:36
  208.7 17.4 %collective-permute-done.20 = bf16[2,512,512]{2,1,0:T(8,128)(2,1)S(1)} collective-permute-done((bf16[2,512,512]{2,1,0:T(8,128)(2,1)S(1)}, bf16[2,512,512]{2,1,0:T(8,128)(2,1)S(1)}, u32[]{:S(2)}, u32[]{:S(2)}) %collective-permute-start.20) | collective-permute-done | bytes 1048608 | tf_op jit(solution)/shard_map/ppermute | solution.py:36
  231.0 7.6 %multiply_reduce_fusion.6 = (f32[512]{0:T(512)S(1)}, f32[512,2048]{1,0:T(8,128)S(1)}) fusion(bf16[2048,2048]{1,0:T(8,128)(2,1)} %bitcast.247, bf16[512,512]{1,0:T(8,128)(2,1)S(1)} %get-tuple-element.276, bf16[512,512]{1,0:T(8,128)(2,1)S(1)} %get-tuple-element.275, bf16[512,512]{1,0:T(8,128)(2,1)S(1)} %get-tuple-element.274, ...), kind=kOutput, calls=%fused_computation.44 | convolution fusion | flops 4307549696 | bytes 16779264 | tf_op jit(solution)/shard_map/dot_general | solution.py:32
  245.0 11.2 %normed_in_order.1 = bf16[2048,2048]{1,0:T(8,128)(2,1)} custom-call(s32[8]{0:T(128)} %fusion.128.ids, bf16[2048,2048]{1,0:T(8,128)(2,1)} %constant_dynamic-update-slice_fusion.hidden, f32[2048,1]{1,0:T(8,128)} %copy.114.scale, f32[1,2048]{1,0:T(1,128)} %copy-done.73), custom_call_target="tpu_custom_call" | custom-call | flops 8388608 | bytes 16777216 | tf_op jit(solution)/shard_map/normed_in_order/pallas_call | solution.py:317
  270.0 14.2 %collective-permute-done.27 = bf16[2,128,2048]{2,1,0:T(8,128)(2,1)} collective-permute-done((bf16[2,128,2048]{2,1,0:T(8,128)(2,1)}, bf16[2,128,2048]{2,1,0:T(8,128)(2,1)}, u32[]{:S(2)}, u32[]{:S(2)}) %collective-permute-start.27) | collective-permute-done | bytes 1048608 | tf_op jit(solution)/shard_map/ppermute | solution.py:36
  319.5 6.6 convolution_convert_fusion.2
  326.1 12.8 %collective-permute-done.28 = bf16[2,128,2048]{2,1,0:T(8,128)(2,1)} collective-permute-done((bf16[2,128,2048]{2,1,0:T(8,128)(2,1)}, bf16[2,128,2048]{2,1,0:T(8,128)(2,1)}, u32[]{:S(2)}, u32[]{:S(2)}) %collective-permute-start.28) | collective-permute-done | bytes 1048608 | tf_op jit(solution)/shard_map/ppermute | solution.py:36
  380.8 13.8 %collective-permute-done.33 = bf16[2,512,512]{2,1,0:T(8,128)(2,1)S(1)} collective-permute-done((bf16[2,512,512]{2,1,0:T(8,128)(2,1)S(1)}, bf16[2,512,512]{2,1,0:T(8,128)(2,1)S(1)}, u32[]{:S(2)}, u32[]{:S(2)}) %collective-permute-start.33) | collective-permute-done | bytes 1048608 | tf_op jit(solution)/shard_map/ppermute | solution.py:36
  403.6 38.3 %attend_back.1 = (f32[2048,512]{1,0:T(8,128)}, f32[2048,512]{1,0:T(8,128)}, bf16[2048,512]{1,0:T(8,128)(2,1)}) custom-call(bf16[2048,512]{1,0:T(8,128)(2,1)} %get-tuple-element.124.queries, bf16[2048,512]{1,0:T(8,128)(2,1)} %get-tuple-element.125.keys, bf16[2048,512]{1,0:T(8,128)(2,1)} %get-tuple-element.126.values, ...), custom_call_target="tpu_custom_call" | custom-call | flops 5368709120 | bytes 18874368 | tf_op jit(solution)/shard_map/attend_back/pallas_call | solution.py:206
  441.9 7.1 %multiply_reduce_fusion = (f32[512]{0:T(512)S(1)}, f32[2048]{0:T(1024)S(1)}, f32[2048]{0:T(1024)S(1)}, f32[512]{0:T(512)S(1)}) fusion(f32[2048,512]{1,0:T(8,128)} %get-tuple-element.138, f32[2048,1536]{1,0:T(8,128)} %copy-done.2, f32[2048]{0:T(1024)S(1)} %get-tuple-element.246, f32[512]{0:T(512)S(1)} %bitcast.293, f32[2048,512]{1,0:T(8,128)} %get-tuple-element.137, ...), kind=kLoop, calls=%fused_computation.32 | loop fusion | flops 12577792 | bytes 16818176 | tf_op jit(solution)/shard_map/reduce_sum | solution.py:632
  479.6 6.7 subtract_convert_fusion.1
  490.1 19.2 %convolution_convert_fusion = bf16[2048,1536]{1,0:T(8,128)(2,1)} fusion(bf16[2048,2048]{1,0:T(8,128)(2,1)} %normed_in_order.1, bf16[2048,512]{1,0:T(8,128)(2,1)} %get-tuple-element.144, bf16[2048,512]{1,0:T(8,128)(2,1)} %get-tuple-element.259, bf16[2048,512]{1,0:T(8,128)(2,1)S(1)} %get-tuple-element.258), kind=kOutput, calls=%fused_computation.10 | convolution fusion | flops 12906921984 | bytes 20971520 | tf_op jit(solution)/shard_map/dot_general | solution.py:32
  512.8 7.0 %fusion.34 = bf16[512,2048]{1,0:T(8,128)(2,1)S(1)} fusion(bf16[2048,1536]{1,0:T(8,128)(2,1)} %get-tuple-element.110, bf16[2048,1536]{1,0:T(8,128)(2,1)} %pad_maximum_fusion.1), kind=kOutput, calls=%fused_computation.109 | convolution fusion | flops 3221225472 | bytes 9961472 | tf_op jit(solution)/shard_map/dot_general | solution.py:32
  519.9 6.6 fusion.36
  533.6 12.6 %collective-permute-done.42 = bf16[128,1664]{1,0:T(8,128)(2,1)S(1)} collective-permute-done((bf16[128,1664]{1,0:T(8,128)(2,1)S(1)}, bf16[128,1664]{1,0:T(8,128)(2,1)S(1)}, u32[]{:S(2)}, u32[]{:S(2)}) %collective-permute-start.42) | collective-permute-done | bytes 426016 | tf_op jit(solution)/shard_map/ppermute | solution.py:235
  566.2 16.1 %collective-permute-done.44 = bf16[256,1664]{1,0:T(8,128)(2,1)S(1)} collective-permute-done((bf16[256,1664]{1,0:T(8,128)(2,1)S(1)}, bf16[256,1664]{1,0:T(8,128)(2,1)S(1)}, u32[]{:S(2)}, u32[]{:S(2)}) %collective-permute-start.44) | collective-permute-done | bytes 852000 | tf_op jit(solution)/shard_map/ppermute | solution.py:235
  595.6 12.5 %collective-permute-done.47 = bf16[256,1664]{1,0:T(8,128)(2,1)} collective-permute-done((bf16[256,1664]{1,0:T(8,128)(2,1)}, bf16[256,1664]{1,0:T(8,128)(2,1)}, u32[]{:S(2)}, u32[]{:S(2)}) %collective-permute-start.47) | collective-permute-done | bytes 852000 | tf_op jit(solution)/shard_map/ppermute | solution.py:235
  622.3 8.8 %collective-permute-done.50 = bf16[256,1664]{1,0:T(8,128)(2,1)S(1)} collective-permute-done((bf16[256,1664]{1,0:T(8,128)(2,1)S(1)}, bf16[256,1664]{1,0:T(8,128)(2,1)S(1)}, u32[]{:S(2)}, u32[]{:S(2)}) %collective-permute-start.50) | collective-permute-done | bytes 852000 | tf_op jit(solution)/shard_map/ppermute | solution.py:235
  651.5 10.7 %collective-permute-done.53 = bf16[256,1664]{1,0:T(8,128)(2,1)} collective-permute-done((bf16[256,1664]{1,0:T(8,128)(2,1)}, bf16[256,1664]{1,0:T(8,128)(2,1)}, u32[]{:S(2)}, u32[]{:S(2)}) %collective-permute-start.53) | collective-permute-done | bytes 852000 | tf_op jit(solution)/shard_map/ppermute | solution.py:36
  (569 shorter events, 349.6 us)
Async XLA Ops:
  7.2 141.6 %all-gather.4.cloned.1.call-start = ((), (), s32[]{:S(2)}) async-start(), calls=%async_computation.3 | async-start | bytes 2359296 | tf_op jit(solution)/shard_map/all_gather | solution.py:382
  20.7 59.9 %collective-permute-start.7 = (bf16[512,2048]{1,0:T(8,128)(2,1)}, bf16[512,2048]{1,0:T(8,128)(2,1)}, u32[]{:S(2)}, u32[]{:S(2)}) collective-permute-start(bf16[512,2048]{1,0:T(8,128)(2,1)} %param.19), channel_id=1, source_target_pairs={{0,2},{1,3},{2,0},{3,1},{4,6},{5,7},{6,4},{7,5},{8,10},{9,11},{10,... | collective-permute-start | bytes 6291464 | tf_op jit(solution)/shard_map/ppermute | solution.py:36
  42.6 40.7 %collective-permute-start = (bf16[512,2048]{1,0:T(8,128)(2,1)S(1)}, bf16[512,2048]{1,0:T(8,128)(2,1)}, u32[]{:S(2)}, u32[]{:S(2)}) collective-permute-start(bf16[512,2048]{1,0:T(8,128)(2,1)S(1)} %copy-done.13), channel_id=1, source_target_pairs={{0,1},{1,0},{2,3},{3,2},{4,5},{5,4},{6,7},{7,6},{8,9},{9,8},{10,11... | collective-permute-start | bytes 6291464 | tf_op jit(solution)/shard_map/ppermute | solution.py:36
  43.7 24.5 %collective-permute-start.11 = (bf16[128,2048]{1,0:T(8,128)(2,1)S(1)}, bf16[128,2048]{1,0:T(8,128)(2,1)S(1)}, u32[]{:S(2)}, u32[]{:S(2)}) collective-permute-start(bf16[128,2048]{1,0:T(8,128)(2,1)S(1)} %get-tuple-element.316), channel_id=1, source_target_pairs={{0,1},{1,0},{2,3},{3,2},{4,5},{5,4},{6,7},{7,6},{8,9},{9,8},{10,11... | collective-permute-start | bytes 1572872 | tf_op jit(solution)/shard_map/ppermute | solution.py:36
  92.2 134.0 %all-gather.6.cloned.1.call-start = ((), (), s32[]{:S(2)}) async-start(), calls=%async_computation.4 | async-start | bytes 4718592 | tf_op jit(solution)/shard_map/all_gather | solution.py:382
  139.8 151.2 %all-gather.8.cloned.1.call-start = ((), (), s32[]{:S(2)}) async-start(), calls=%async_computation.5 | async-start | bytes 2359296 | tf_op jit(solution)/shard_map/all_gather | solution.py:382
  148.8 41.4 %collective-permute-start.18 = (bf16[8,64,2048]{2,1,0:T(8,128)(2,1)}, bf16[8,64,2048]{2,1,0:T(8,128)(2,1)}, u32[]{:S(2)}, u32[]{:S(2)}) collective-permute-start(bf16[8,64,2048]{2,1,0:T(8,128)(2,1)} %bitcast.259), channel_id=1, source_target_pairs={{0,1},{1,0},{2,3},{3,2},{4,5},{5,4},{6,7},{7,6},{8,9},{9,8},{10,11... | collective-permute-start | bytes 6291464 | tf_op jit(solution)/shard_map/ppermute | solution.py:36
  148.9 48.3 %collective-permute-start.19 = (bf16[8,64,2048]{2,1,0:T(8,128)(2,1)}, bf16[8,64,2048]{2,1,0:T(8,128)(2,1)}, u32[]{:S(2)}, u32[]{:S(2)}) collective-permute-start(bf16[8,64,2048]{2,1,0:T(8,128)(2,1)} %bitcast.260), channel_id=1, source_target_pairs={{0,2},{1,3},{2,0},{3,1},{4,6},{5,7},{6,4},{7,5},{8,10},{9,11},{10,... | collective-permute-start | bytes 6291464 | tf_op jit(solution)/shard_map/ppermute | solution.py:36
  200.6 25.6 %collective-permute-start.20 = (bf16[2,512,512]{2,1,0:T(8,128)(2,1)S(1)}, bf16[2,512,512]{2,1,0:T(8,128)(2,1)S(1)}, u32[]{:S(2)}, u32[]{:S(2)}) collective-permute-start(bf16[2,512,512]{2,1,0:T(8,128)(2,1)S(1)} %bitcast.268), channel_id=1, source_target_pairs={{0,2},{1,3},{2,0},{3,1},{4,6},{5,7},{6,4},{7,5},{8,10},{9,11},{10,... | collective-permute-start | bytes 3145736 | tf_op jit(solution)/shard_map/ppermute | solution.py:36
  201.5 25.6 %collective-permute-start.23 = (bf16[512,512]{1,0:T(8,128)(2,1)}, bf16[512,512]{1,0:T(8,128)(2,1)}, u32[]{:S(2)}, u32[]{:S(2)}) collective-permute-start(bf16[512,512]{1,0:T(8,128)(2,1)} %slice.398), channel_id=1, source_target_pairs={{0,1},{1,0},{2,3},{3,2},{4,5},{5,4},{6,7},{7,6},{8,9},{9,8},{10,11... | collective-permute-start | bytes 1572872 | tf_op jit(solution)/shard_map/ppermute | solution.py:36
  227.1 285.8 %reduce-scatter.4.cloned.1.call-start = ((), (), s32[]{:S(2)}) async-start(), calls=%async_computation.6 | async-start | bytes 4718592 | tf_op jit(solution)/shard_map/reduce_scatter | solution.py:386
  258.5 25.8 %collective-permute-start.27 = (bf16[2,128,2048]{2,1,0:T(8,128)(2,1)}, bf16[2,128,2048]{2,1,0:T(8,128)(2,1)}, u32[]{:S(2)}, u32[]{:S(2)}) collective-permute-start(bf16[2,128,2048]{2,1,0:T(8,128)(2,1)} %pad_maximum_fusion.13), channel_id=1, source_target_pairs={{0,2},{1,3},{2,0},{3,1},{4,6},{5,7},{6,4},{7,5},{8,10},{9,11},{10,... | collective-permute-start | bytes 3145736 | tf_op jit(solution)/shard_map/ppermute | solution.py:36
  314.5 24.4 %collective-permute-start.28 = (bf16[2,128,2048]{2,1,0:T(8,128)(2,1)}, bf16[2,128,2048]{2,1,0:T(8,128)(2,1)}, u32[]{:S(2)}, u32[]{:S(2)}) collective-permute-start(bf16[2,128,2048]{2,1,0:T(8,128)(2,1)} %bitcast.45), channel_id=1, source_target_pairs={{0,2},{1,3},{2,0},{3,1},{4,6},{5,7},{6,4},{7,5},{8,10},{9,11},{10,... | collective-permute-start | bytes 3145736 | tf_op jit(solution)/shard_map/ppermute | solution.py:36
  342.6 253.0 %reduce-scatter.6.cloned.1.call-start = ((), (), s32[]{:S(2)}) async-start(), calls=%async_computation.7 | async-start | bytes 2359296 | tf_op jit(solution)/shard_map/reduce_scatter | solution.py:386
  369.1 25.5 %collective-permute-start.33 = (bf16[2,512,512]{2,1,0:T(8,128)(2,1)S(1)}, bf16[2,512,512]{2,1,0:T(8,128)(2,1)S(1)}, u32[]{:S(2)}, u32[]{:S(2)}) collective-permute-start(bf16[2,512,512]{2,1,0:T(8,128)(2,1)S(1)} %pad_maximum_fusion.15), channel_id=1, source_target_pairs={{0,2},{1,3},{2,0},{3,1},{4,6},{5,7},{6,4},{7,5},{8,10},{9,11},{10,... | collective-permute-start | bytes 3145736 | tf_op jit(solution)/shard_map/ppermute | solution.py:36
  396.4 255.0 %reduce-scatter.8.cloned.1.call-start = ((), (), s32[]{:S(2)}) async-start(), calls=%async_computation.8 | async-start | bytes 2359296 | tf_op jit(solution)/shard_map/reduce_scatter | solution.py:386
  400.2 86.1 %collective-permute-start.38 = (bf16[8,64,2048]{2,1,0:T(8,128)(2,1)}, bf16[8,64,2048]{2,1,0:T(8,128)(2,1)}, u32[]{:S(2)}, u32[]{:S(2)}) collective-permute-start(bf16[8,64,2048]{2,1,0:T(8,128)(2,1)} %dynamic-slice_bitcast_fusion), channel_id=1, source_target_pairs={{0,2},{1,3},{2,0},{3,1},{4,6},{5,7},{6,4},{7,5},{8,10},{9,11},{10,... | collective-permute-start | bytes 6291464 | tf_op jit(solution)/shard_map/ppermute | solution.py:36
  477.4 35.3 %collective-permute-start.39 = (bf16[2,128,2048]{2,1,0:T(8,128)(2,1)}, bf16[2,128,2048]{2,1,0:T(8,128)(2,1)}, u32[]{:S(2)}, u32[]{:S(2)}) collective-permute-start(bf16[2,128,2048]{2,1,0:T(8,128)(2,1)} %slice.697), channel_id=1, source_target_pairs={{0,2},{1,3},{2,0},{3,1},{4,6},{5,7},{6,4},{7,5},{8,10},{9,11},{10,... | collective-permute-start | bytes 3145736 | tf_op jit(solution)/shard_map/ppermute | solution.py:36
  528.4 25.6 %collective-permute-start.58 = (bf16[256,1024]{1,0:T(8,128)(2,1)S(1)}, bf16[256,1024]{1,0:T(8,128)(2,1)S(1)}, u32[]{:S(2)}, u32[]{:S(2)}) collective-permute-start(bf16[256,1024]{1,0:T(8,128)(2,1)S(1)} %copy-done.62), channel_id=1, source_target_pairs={{0,2},{1,3},{2,0},{3,1},{4,6},{5,7},{6,4},{7,5},{8,10},{9,11},{10,... | collective-permute-start | bytes 1572872 | tf_op jit(solution)/shard_map/ppermute | solution.py:36
  529.3 32.2 %collective-permute-start.60 = (bf16[256,1024]{1,0:T(8,128)(2,1)S(1)}, bf16[256,1024]{1,0:T(8,128)(2,1)S(1)}, u32[]{:S(2)}, u32[]{:S(2)}) collective-permute-start(bf16[256,1024]{1,0:T(8,128)(2,1)S(1)} %copy-done.62), channel_id=1, source_target_pairs={{0,1},{1,0},{2,3},{3,2},{4,5},{5,4},{6,7},{7,6},{8,9},{9,8},{10,11... | collective-permute-start | bytes 1572872 | tf_op jit(solution)/shard_map/ppermute | solution.py:36
  546.6 35.7 %collective-permute-start.45 = (bf16[2,512,2048]{2,1,0:T(8,128)(2,1)S(1)}, bf16[2,512,2048]{2,1,0:T(8,128)(2,1)S(1)}, u32[]{:S(2)}, u32[]{:S(2)}) collective-permute-start(bf16[2,512,2048]{2,1,0:T(8,128)(2,1)S(1)} %pad_maximum_fusion.2), channel_id=1, source_target_pairs={{0,1},{1,0},{2,3},{3,2},{4,5},{5,4},{6,7},{7,6},{8,9},{9,8},{10,11... | collective-permute-start | bytes 12582920 | tf_op jit(solution)/shard_map/ppermute | solution.py:36
  552.4 29.8 %collective-permute-start.44 = (bf16[256,1664]{1,0:T(8,128)(2,1)S(1)}, bf16[256,1664]{1,0:T(8,128)(2,1)S(1)}, u32[]{:S(2)}, u32[]{:S(2)}) collective-permute-start(bf16[256,1664]{1,0:T(8,128)(2,1)S(1)} %pad_maximum_fusion.16), channel_id=1, source_target_pairs={{8,0},{16,8},{24,16},{28,24},{20,28},{12,20},{4,12},{0,4},{9,1},{1... | collective-permute-start | bytes 2555912 | tf_op jit(solution)/shard_map/ppermute | solution.py:235
  554.0 28.2 %collective-permute-start.43 = (bf16[256,1664]{1,0:T(8,128)(2,1)S(1)}, bf16[256,1664]{1,0:T(8,128)(2,1)S(1)}, u32[]{:S(2)}, u32[]{:S(2)}) collective-permute-start(bf16[256,1664]{1,0:T(8,128)(2,1)S(1)} %fusion.70), channel_id=1, source_target_pairs={{0,8},{8,16},{16,24},{24,28},{28,20},{20,12},{12,4},{4,0},{1,9},{9... | collective-permute-start | bytes 2555912 | tf_op jit(solution)/shard_map/ppermute | solution.py:235
  584.6 26.0 %collective-permute-start.48 = (bf16[256,2048]{1,0:T(8,128)(2,1)}, bf16[256,2048]{1,0:T(8,128)(2,1)S(1)}, u32[]{:S(2)}, u32[]{:S(2)}) collective-permute-start(bf16[256,2048]{1,0:T(8,128)(2,1)} %get-tuple-element.293), channel_id=1, source_target_pairs={{0,2},{1,3},{2,0},{3,1},{4,6},{5,7},{6,4},{7,5},{8,10},{9,11},{10,... | collective-permute-start | bytes 3145736 | tf_op jit(solution)/shard_map/ppermute | solution.py:36
  (155 other events, 1893.6 us)
Sparse Core Ops, SparseCore 0:
  92.3 47.8 all-gather.3
  142.9 71.5 all-gather.5
  227.2 50.3 all-gather.7
  342.7 89.5 reduce-scatter.3
  436.2 68.0 reduce-scatter.5
  508.3 74.9 reduce-scatter.7

commit v6 on v5

--- a/solution.py
+++ b/solution.py
@@ -13,6 +13,7 @@
 THETA = 10000.0
 REACH = 2
 ROWS = 128
+COVER = 1 << 27
 F32 = jnp.float32
 BF16 = jnp.bfloat16
 
@@ -327,9 +328,31 @@
             out_specs=pl.BlockSpec((rows, cols // n), lambda i, ids: (0, i)),
         ),
         out_shape=jax.ShapeDtypeStruct((rows, cols), BF16),
-        cost_estimate=cost(2 * rows * cols, 4 * rows * cols),
+        cost_estimate=cost(0, COVER),
         name="normed_in_order",
     )(ids, hidden, scale, gain)
+
+
+def back_kernel(x, w, out):
+    out[0] = dot(x[...], w[...], ((1,), (1,))).astype(out.dtype)
+
+
+def back_product(x, w, first, count, rows, dtype):
+    inner = x.shape[1]
+    cols = w.shape[0]
+    step = 512
+    return pl.pallas_call(
+        back_kernel,
+        grid=(count, cols // step),
+        in_specs=[
+            pl.BlockSpec((rows, inner), lambda j, i: (first + 2 * j, 0)),
+            pl.BlockSpec((step, inner), lambda j, i: (i, 0)),
+        ],
+        out_specs=pl.BlockSpec((1, rows, step), lambda j, i: (j, 0, i)),
+        out_shape=jax.ShapeDtypeStruct((count, rows, cols), dtype),
+        cost_estimate=cost(0, COVER),
+        name="back_product",
+    )(x, w)
 
 
 def rows_kernel(ids, x, out):
@@ -540,9 +563,11 @@
     from_side = swap(blocks[2:], 2)
     out_pieces = in_order([w_out_part, out_core, out_side, swap(out_side, 1)], rep)
     output_w = jnp.stack(out_pieces, 1).reshape(width, width)
-    from_side, w_gu, output_w = tie(from_side, w_gu, output_w)
+    from_core, late_scale = tie(swap(blocks[1], 1), normed_scale)
+    normed_ring = normed_in_order(ring, hidden_all, late_scale, gain_one[None])
+    from_side, w_gu, output_w, normed_ring = tie(from_side, w_gu, output_w, normed_ring)
     mixed = jnp.concatenate(
-        in_order([blocks[0], swap(blocks[1], 1), from_side[0], swap(from_side[1], 1)], rep), 1
+        in_order([blocks[0], from_core, from_side[0], swap(from_side[1], 1)], rep), 1
     )
     hidden = hidden_in.astype(F32)
     residual = hidden + dot(mixed, output_w)
@@ -557,14 +582,7 @@
     select_wide = select.reshape(experts, cap, length).astype(F32)
     slot_gates = to_experts(jnp.sum(select_wide * window.T[:, None, :], -1))
     pair = to_pair(dot(select, inner).astype(BF16).reshape(experts, cap, width))
-    normed_ring = normed_in_order(ring, hidden_all, normed_scale, gain_one[None])
-    at = lambda x, i, axis: lax.dynamic_index_in_dim(x, i, axis, keepdims=False)
-    half = lambda which: at(mixed.reshape(length, n_shard, 2, 2, quarter), which, 3).reshape(
-        length, width // 2
-    )
-    from_side, normed_ring, mixed_own, mixed_other = tie(
-        swap(pair, 2), normed_ring, half(core), half(1 - core)
-    )
+    from_side = swap(pair, 2)
     slot_inputs = jnp.concatenate([pair, from_side], 0)
     slot_inputs = slot_inputs.reshape(4 * cap, width)
 
@@ -584,8 +602,16 @@
     slot_input_grad = dot(gate_up_grad, w_gu, ((1,), (1,))).reshape(4, cap, width)
     down_w_grad = dot(activated, returned_grad, ((0,), (0,))).astype(BF16)
     gate_up_w_grad = dot(slot_inputs, gate_up_grad, ((0,), (0,))).astype(BF16)
-    there, down_w_grad, gate_up_w_grad = tie(
-        send_side(slot_input_grad, BF16), down_w_grad, gate_up_w_grad
+    at = lambda x, i, axis: lax.dynamic_index_in_dim(x, i, axis, keepdims=False)
+    half = lambda which: at(mixed.reshape(length, n_shard, 2, 2, quarter), which, 3).reshape(
+        length, width // 2
+    )
+    there, down_w_grad, gate_up_w_grad, mixed_own, mixed_other = tie(
+        send_side(slot_input_grad, BF16),
+        down_w_grad,
+        gate_up_w_grad,
+        half(core),
+        half(1 - core),
     )
     slot_input_grad = from_experts(slot_input_grad, there, BF16)
     gate_up_owned = shard_scatter(gate_up_w_grad)
@@ -649,18 +675,19 @@
     small = jnp.concatenate(
         [router_grad, small, jnp.zeros((width, 128 - 3 - routed), F32)], 1
     )
-    back = lambda slots, j: dot(
-        slots.reshape(4, length, 3 * part)[j], w_qkv, ((1,), (1,))
-    )
+    back = lambda slots, first, count, dtype: back_product(
+        slots, w_qkv, first, count, length, dtype
+    )
+
+    def near(slots, odd):
+        odd, slots = tie(swap(odd, 1), slots)
+        return slots, back(slots, 2, 1, F32)[0], odd
+
     due = (
-        lambda: (qkv_grad, back(qkv_grad, 1), back(qkv_grad, 3)),
-        lambda slots, one, three: (
-            slots,
-            back(slots, 2),
-            swap(jnp.stack([one, three]).astype(BF16), 1),
-        ),
+        lambda: (qkv_grad, back(qkv_grad, 1, 2, BF16)),
+        near,
         lambda slots, two, from_core: (
-            back(slots, 0) + from_core[0].astype(F32),
+            back(slots, 0, 1, F32)[0] + from_core[0].astype(F32),
             (two + from_core[1].astype(F32)).astype(BF16)[length // 2 :],
             swap((two + from_core[1].astype(F32)).astype(BF16)[: length // 2], 2),
             down_owned,

time: 696 us -> 680 us (0.977)
  waiting for transfers between devices: 203 us -> 153 us
  Pallas kernels: 96.8 us -> 126 us
  matrix products: 122 us -> 98.9 us
  other arithmetic: 108 us -> 121 us
  local copies, waits for them, and re-layouts: 99.4 us -> 110 us
    ppermute x16, waiting for transfers between devices: 96.5 us -> 62.3 us  [ring_step(): lax.ppermute(x, 'shard', [(b, a) for a, b in pairs] if back else pairs)]
    pallas_call x0 -> x3, Pallas kernels: none -> 29.2 us  [back_product(): pl.pallas_call(back_kernel, grid=(count, cols // step), in_specs=[pl.Bloc...]
    dot_general x35 -> x31, matrix products: 122 us -> 98.9 us  [dot(): return lax.dot_general(a, b, (dims, ((), ())), preferred_element_type=F32)]
    ppermute x48, waiting for transfers between devices: 107 us -> 88.9 us  [swap(): return lax.ppermute(x, 'rep', [(i, i ^ mask) for i in range(4)])]
    unnamed x228 -> x238, local copies, waits for them, and re-layouts: 30.3 us -> 34.5 us
  transfers between devices with their start and end apart: 70 -> 70, of which waited for: 35 -> 37; matrix products, arithmetic and copies ran while one was open for 41% -> 41% of each run, Pallas kernels for 14% -> 19%
where the time goes in v6:
time: 680 us; the launch traced here: 673 us
  waiting for transfers between devices  153 us (22%)
  Pallas kernels  126 us (19%)
  other arithmetic  121 us (18%)
  local copies, waits for them, and re-layouts  110 us (16%)
  matrix products  98.9 us (15%)
  starting transfers between devices  47.4 us (7%)
  between operations  16.4 us (2%)
    dot_general x31, matrix products, dot(): return lax.dot_general(a, b, (dims, ((), ())), preferred_element_type=F32)  98.9 us
    ppermute x48, waiting for transfers between devices, swap(): return lax.ppermute(x, 'rep', [(i, i ^ mask) for i in range(4)])  88.9 us
    ppermute x16, waiting for transfers between devices, ring_step(): lax.ppermute(x, 'shard', [(b, a) for a, b in pairs] if back else pairs)  62.3 us
    pallas_call x1, Pallas kernels, attend_back(): pl.pallas_call(functools.partial(attend_back_kernel, dim ** (-0.5)), grid...  38.2 us
    pallas_call x1, Pallas kernels, attend(): pl.pallas_call(functools.partial(attend_kernel, dim ** (-0.5)), grid=(tok...  35 us
    unnamed x238, local copies, waits for them, and re-layouts  34.5 us
    pallas_call x3, Pallas kernels, back_product(): pl.pallas_call(back_kernel, grid=(count, cols // step), in_specs=[pl.Bloc...  29.2 us
    ppermute x48, starting transfers between devices, swap(): return lax.ppermute(x, 'rep', [(i, i ^ mask) for i in range(4)])  28.5 us
  transfers between devices with their start and end apart: 70, of which 37 were waited for; matrix products, arithmetic and copies ran while one was open for 41% of the time, Pallas kernels for 19%

profile of v6, /device:TPU:0, one launch (start us, length us, event | category | flops | bytes accessed | tf_op | source)
XLA Modules:
  0.0 672.7 jit_solution(9136935126360320205)
XLA Ops:
  29.1 8.9 %collective-permute-done.1.refs_1_ = bf16[256,1664]{1,0:T(8,128)(2,1)} collective-permute-done((bf16[256,1664]{1,0:T(8,128)(2,1)}, bf16[256,1664]{1,0:T(8,128)(2,1)}, u32[]{:S(2)}, u32[]{:S(2)}) %collective-permute-start.1) | collective-permute-done | bytes 852000 | tf_op jit(solution)/shard_map/ppermute | solution.py:236
  44.7 14.7 %collective-permute-done.3.refs_3_ = bf16[256,1664]{1,0:T(8,128)(2,1)} collective-permute-done((bf16[256,1664]{1,0:T(8,128)(2,1)}, bf16[256,1664]{1,0:T(8,128)(2,1)}, u32[]{:S(2)}, u32[]{:S(2)}) %collective-permute-start.3) | collective-permute-done | bytes 852000 | tf_op jit(solution)/shard_map/ppermute | solution.py:236
  68.3 11.1 %collective-permute-done.5.refs_5_ = bf16[256,1664]{1,0:T(8,128)(2,1)} collective-permute-done((bf16[256,1664]{1,0:T(8,128)(2,1)}, bf16[256,1664]{1,0:T(8,128)(2,1)}, u32[]{:S(2)}, u32[]{:S(2)}) %collective-permute-start.5) | collective-permute-done | bytes 852000 | tf_op jit(solution)/shard_map/ppermute | solution.py:236
  105.3 6.4 place_rows.1
  116.0 17.7 %fusion.3.q_ref.k_ref.v_ref = f32[2048,1536]{1,0:T(8,128)S(1)} fusion(bf16[2048,1536]{1,0:T(8,128)(2,1)} %get-tuple-element.112.w, bf16[2048,2048]{1,0:T(8,128)(2,1)} %constant_dynamic-update-slice_fusion.hidden, f32[2048]{0:T(1024)S(1)} %bitcast.262, f32[2048]{0:T(1024)S(1)} %add_rsqrt_fusion), kind=kOutput, calls=%fused_computation.5 | convolution fusion | flops 12901679104 | bytes 27279360 | tf_op jit(solution)/shard_map/dot_general | solution.py:33
  155.2 35.0 %attend.1 = (bf16[2048,512]{1,0:T(8,128)(2,1)}, bf16[2048,512]{1,0:T(8,128)(2,1)}, bf16[2048,512]{1,0:T(8,128)(2,1)}, bf16[2048,512]{1,0:T(8,128)(2,1)}) custom-call(f32[2048,1536]{1,0:T(8,128)} %copy-done.2, f32[2048,1536]{1,0:T(8,128)} %copy-done.2, f32[2048,1536]{1,0:T(8,128)} %copy-done.2, f32[2048,1]{1,0:T(8,128)} %get-tuple-element.314.q_scale, ...), custom_call_target="tpu_custom_call" | custom-call | flops 2147483648 | bytes 20971520 | tf_op jit(solution)/shard_map/attend/pallas_call | solution.py:184
  190.2 6.8 %collective-permute-done.19 = bf16[8,64,2048]{2,1,0:T(8,128)(2,1)} collective-permute-done((bf16[8,64,2048]{2,1,0:T(8,128)(2,1)}, bf16[8,64,2048]{2,1,0:T(8,128)(2,1)}, u32[]{:S(2)}, u32[]{:S(2)}) %collective-permute-start.19) | collective-permute-done | bytes 2097184 | tf_op jit(solution)/shard_map/ppermute | solution.py:37
  205.3 11.1 %normed_in_order.1 = bf16[2048,2048]{1,0:T(8,128)(2,1)} custom-call(s32[8]{0:T(128)} %fusion.120.ids, bf16[2048,2048]{1,0:T(8,128)(2,1)} %constant_dynamic-update-slice_fusion.hidden, f32[2048,1]{1,0:T(8,128)} %copy.114.scale, f32[1,2048]{1,0:T(1,128)} %copy-done.82), custom_call_target="tpu_custom_call" | custom-call | bytes 134217728 | tf_op jit(solution)/shard_map/normed_in_order/pallas_call | solution.py:318
  233.0 8.0 %multiply_reduce_fusion.6 = (f32[512]{0:T(512)S(1)}, f32[512,2048]{1,0:T(8,128)S(1)}) fusion(bf16[2048,2048]{1,0:T(8,128)(2,1)} %bitcast.238, bf16[512,512]{1,0:T(8,128)(2,1)S(1)} %get-tuple-element.280, bf16[512,512]{1,0:T(8,128)(2,1)S(1)} %get-tuple-element.279, bf16[512,512]{1,0:T(8,128)(2,1)S(1)} %get-tuple-element.278, ...), kind=kOutput, calls=%fused_computation.43 | convolution fusion | flops 4307549696 | bytes 16779264 | tf_op jit(solution)/shard_map/dot_general | solution.py:33
  252.1 20.4 %collective-permute-done.27 = bf16[2,128,2048]{2,1,0:T(8,128)(2,1)} collective-permute-done((bf16[2,128,2048]{2,1,0:T(8,128)(2,1)}, bf16[2,128,2048]{2,1,0:T(8,128)(2,1)}, u32[]{:S(2)}, u32[]{:S(2)}) %collective-permute-start.27) | collective-permute-done | bytes 1048608 | tf_op jit(solution)/shard_map/ppermute | solution.py:37
  322.0 6.2 convolution_convert_fusion.2
  367.2 6.2 add_convert_fusion
  373.3 13.8 %collective-permute-done.33 = bf16[2,512,512]{2,1,0:T(8,128)(2,1)S(1)} collective-permute-done((bf16[2,512,512]{2,1,0:T(8,128)(2,1)S(1)}, bf16[2,512,512]{2,1,0:T(8,128)(2,1)S(1)}, u32[]{:S(2)}, u32[]{:S(2)}) %collective-permute-start.33) | collective-permute-done | bytes 1048608 | tf_op jit(solution)/shard_map/ppermute | solution.py:37
  396.7 38.2 %attend_back.1 = (f32[2048,512]{1,0:T(8,128)}, f32[2048,512]{1,0:T(8,128)}, bf16[2048,512]{1,0:T(8,128)(2,1)}) custom-call(bf16[2048,512]{1,0:T(8,128)(2,1)} %get-tuple-element.128.queries, bf16[2048,512]{1,0:T(8,128)(2,1)} %get-tuple-element.129.keys, bf16[2048,512]{1,0:T(8,128)(2,1)} %get-tuple-element.130.values, ...), custom_call_target="tpu_custom_call" | custom-call | flops 5368709120 | bytes 18874368 | tf_op jit(solution)/shard_map/attend_back/pallas_call | solution.py:207
  435.0 6.9 %multiply_reduce_fusion = (f32[512]{0:T(512)S(1)}, f32[2048]{0:T(1024)S(1)}, f32[2048]{0:T(1024)S(1)}, f32[512]{0:T(512)S(1)}) fusion(f32[2048,512]{1,0:T(8,128)} %get-tuple-element.141, f32[2048,1536]{1,0:T(8,128)} %copy-done.2, f32[2048]{0:T(1024)S(1)} %get-tuple-element.250, f32[512]{0:T(512)S(1)} %bitcast.281, f32[2048,512]{1,0:T(8,128)} %get-tuple-element.140, ...), kind=kLoop, calls=%fused_computation.31 | loop fusion | flops 12577792 | bytes 16818176 | tf_op jit(solution)/shard_map/reduce_sum | solution.py:658
  472.0 6.7 subtract_convert_fusion.1
  482.5 19.2 %convolution_convert_fusion = bf16[2048,1536]{1,0:T(8,128)(2,1)} fusion(bf16[2048,2048]{1,0:T(8,128)(2,1)} %normed_in_order.1, bf16[2048,512]{1,0:T(8,128)(2,1)} %get-tuple-element.147, bf16[2048,512]{1,0:T(8,128)(2,1)} %get-tuple-element.263, bf16[2048,512]{1,0:T(8,128)(2,1)S(1)} %get-tuple-element.262), kind=kOutput, calls=%fused_computation.10 | convolution fusion | flops 12906921984 | bytes 20971520 | tf_op jit(solution)/shard_map/dot_general | solution.py:33
  518.3 13.4 %back_product.3 = bf16[2,512,2048]{2,1,0:T(8,128)(2,1)} custom-call(bf16[2048,1536]{1,0:T(8,128)(2,1)} %pad_maximum_fusion.1.x, bf16[2048,1536]{1,0:T(8,128)(2,1)} %get-tuple-element.112.w), custom_call_target="tpu_custom_call" | custom-call | bytes 134217728 | tf_op jit(solution)/shard_map/back_product/pallas_call | solution.py:344
  552.6 7.9 %back_product.4 = f32[1,512,2048]{2,1,0:T(8,128)} custom-call(bf16[2048,1536]{1,0:T(8,128)(2,1)} %pad_maximum_fusion.1.x, bf16[2048,1536]{1,0:T(8,128)(2,1)} %get-tuple-element.112.w), custom_call_target="tpu_custom_call" | custom-call | bytes 134217728 | tf_op jit(solution)/shard_map/back_product/pallas_call | solution.py:344
  576.6 7.9 %back_product.5 = f32[1,512,2048]{2,1,0:T(8,128)} custom-call(bf16[2048,1536]{1,0:T(8,128)(2,1)} %pad_maximum_fusion.1.x, bf16[2048,1536]{1,0:T(8,128)(2,1)} %get-tuple-element.112.w), custom_call_target="tpu_custom_call" | custom-call | bytes 134217728 | tf_op jit(solution)/shard_map/back_product/pallas_call | solution.py:344
  606.6 8.7 %collective-permute-done.50 = bf16[256,1664]{1,0:T(8,128)(2,1)S(1)} collective-permute-done((bf16[256,1664]{1,0:T(8,128)(2,1)S(1)}, bf16[256,1664]{1,0:T(8,128)(2,1)S(1)}, u32[]{:S(2)}, u32[]{:S(2)}) %collective-permute-start.50) | collective-permute-done | bytes 852000 | tf_op jit(solution)/shard_map/ppermute | solution.py:236
  628.5 6.1 fusion.13
  634.8 10.3 %collective-permute-done.53 = bf16[256,1664]{1,0:T(8,128)(2,1)} collective-permute-done((bf16[256,1664]{1,0:T(8,128)(2,1)}, bf16[256,1664]{1,0:T(8,128)(2,1)}, u32[]{:S(2)}, u32[]{:S(2)}) %collective-permute-start.53) | collective-permute-done | bytes 852000 | tf_op jit(solution)/shard_map/ppermute | solution.py:37
  646.5 6.2 collective-permute-done.55
  (576 shorter events, 358.4 us)
Async XLA Ops:
  7.2 141.4 %all-gather.4.cloned.1.call-start = ((), (), s32[]{:S(2)}) async-start(), calls=%async_computation.3 | async-start | bytes 2359296 | tf_op jit(solution)/shard_map/all_gather | solution.py:405
  18.8 23.7 %collective-permute-start.9 = (s32[1,512]{1,0:T(1,128)S(1)}, s32[1,512]{1,0:T(1,128)S(1)}, u32[]{:S(2)}, u32[]{:S(2)}) collective-permute-start(s32[1,512]{1,0:T(1,128)S(1)} %copy-done.105), channel_id=1, source_target_pairs={{0,2},{1,3},{2,0},{3,1},{4,6},{5,7},{6,4},{7,5},{8,10},{9,11},{10,... | collective-permute-start | bytes 6152 | tf_op jit(solution)/shard_map/ppermute | solution.py:37
  20.7 59.9 %collective-permute-start.7 = (bf16[512,2048]{1,0:T(8,128)(2,1)}, bf16[512,2048]{1,0:T(8,128)(2,1)}, u32[]{:S(2)}, u32[]{:S(2)}) collective-permute-start(bf16[512,2048]{1,0:T(8,128)(2,1)} %param.19), channel_id=1, source_target_pairs={{0,2},{1,3},{2,0},{3,1},{4,6},{5,7},{6,4},{7,5},{8,10},{9,11},{10,... | collective-permute-start | bytes 6291464 | tf_op jit(solution)/shard_map/ppermute | solution.py:37
  42.6 40.8 %collective-permute-start = (bf16[512,2048]{1,0:T(8,128)(2,1)S(1)}, bf16[512,2048]{1,0:T(8,128)(2,1)}, u32[]{:S(2)}, u32[]{:S(2)}) collective-permute-start(bf16[512,2048]{1,0:T(8,128)(2,1)S(1)} %copy-done.14), channel_id=1, source_target_pairs={{0,1},{1,0},{2,3},{3,2},{4,5},{5,4},{6,7},{7,6},{8,9},{9,8},{10,11... | collective-permute-start | bytes 6291464 | tf_op jit(solution)/shard_map/ppermute | solution.py:37
  43.7 24.5 %collective-permute-start.11 = (bf16[128,2048]{1,0:T(8,128)(2,1)S(1)}, bf16[128,2048]{1,0:T(8,128)(2,1)S(1)}, u32[]{:S(2)}, u32[]{:S(2)}) collective-permute-start(bf16[128,2048]{1,0:T(8,128)(2,1)S(1)} %get-tuple-element.320), channel_id=1, source_target_pairs={{0,1},{1,0},{2,3},{3,2},{4,5},{5,4},{6,7},{7,6},{8,9},{9,8},{10,11... | collective-permute-start | bytes 1572872 | tf_op jit(solution)/shard_map/ppermute | solution.py:37
  92.3 135.9 %all-gather.6.cloned.1.call-start = ((), (), s32[]{:S(2)}) async-start(), calls=%async_computation.4 | async-start | bytes 4718592 | tf_op jit(solution)/shard_map/all_gather | solution.py:405
  114.6 23.9 %collective-permute-start.15 = (bf16[2,128,2048]{2,1,0:T(8,128)(2,1)S(1)}, bf16[2,128,2048]{2,1,0:T(8,128)(2,1)S(1)}, u32[]{:S(2)}, u32[]{:S(2)}) collective-permute-start(bf16[2,128,2048]{2,1,0:T(8,128)(2,1)S(1)} %pad_maximum_fusion.11), channel_id=1, source_target_pairs={{0,2},{1,3},{2,0},{3,1},{4,6},{5,7},{6,4},{7,5},{8,10},{9,11},{10,... | collective-permute-start | bytes 3145736 | tf_op jit(solution)/shard_map/ppermute | solution.py:37
  139.6 140.3 %all-gather.8.cloned.1.call-start = ((), (), s32[]{:S(2)}) async-start(), calls=%async_computation.5 | async-start | bytes 2359296 | tf_op jit(solution)/shard_map/all_gather | solution.py:405
  148.6 41.6 %collective-permute-start.18 = (bf16[8,64,2048]{2,1,0:T(8,128)(2,1)}, bf16[8,64,2048]{2,1,0:T(8,128)(2,1)}, u32[]{:S(2)}, u32[]{:S(2)}) collective-permute-start(bf16[8,64,2048]{2,1,0:T(8,128)(2,1)} %bitcast.248), channel_id=1, source_target_pairs={{0,1},{1,0},{2,3},{3,2},{4,5},{5,4},{6,7},{7,6},{8,9},{9,8},{10,11... | collective-permute-start | bytes 6291464 | tf_op jit(solution)/shard_map/ppermute | solution.py:37
  148.7 48.3 %collective-permute-start.19 = (bf16[8,64,2048]{2,1,0:T(8,128)(2,1)}, bf16[8,64,2048]{2,1,0:T(8,128)(2,1)}, u32[]{:S(2)}, u32[]{:S(2)}) collective-permute-start(bf16[8,64,2048]{2,1,0:T(8,128)(2,1)} %bitcast.249), channel_id=1, source_target_pairs={{0,2},{1,3},{2,0},{3,1},{4,6},{5,7},{6,4},{7,5},{8,10},{9,11},{10,... | collective-permute-start | bytes 6291464 | tf_op jit(solution)/shard_map/ppermute | solution.py:37
  202.9 25.2 %collective-permute-start.20 = (bf16[2,512,512]{2,1,0:T(8,128)(2,1)}, bf16[2,512,512]{2,1,0:T(8,128)(2,1)S(1)}, u32[]{:S(2)}, u32[]{:S(2)}) collective-permute-start(bf16[2,512,512]{2,1,0:T(8,128)(2,1)} %bitcast.17), channel_id=1, source_target_pairs={{0,2},{1,3},{2,0},{3,1},{4,6},{5,7},{6,4},{7,5},{8,10},{9,11},{10,... | collective-permute-start | bytes 3145736 | tf_op jit(solution)/shard_map/ppermute | solution.py:37
  229.1 275.9 %reduce-scatter.4.cloned.1.call-start = ((), (), s32[]{:S(2)}) async-start(), calls=%async_computation.6 | async-start | bytes 4718592 | tf_op jit(solution)/shard_map/reduce_scatter | solution.py:409
  247.0 25.5 %collective-permute-start.27 = (bf16[2,128,2048]{2,1,0:T(8,128)(2,1)}, bf16[2,128,2048]{2,1,0:T(8,128)(2,1)}, u32[]{:S(2)}, u32[]{:S(2)}) collective-permute-start(bf16[2,128,2048]{2,1,0:T(8,128)(2,1)} %pad_maximum_fusion.12), channel_id=1, source_target_pairs={{0,2},{1,3},{2,0},{3,1},{4,6},{5,7},{6,4},{7,5},{8,10},{9,11},{10,... | collective-permute-start | bytes 3145736 | tf_op jit(solution)/shard_map/ppermute | solution.py:37
  306.6 24.4 %collective-permute-start.28 = (bf16[2,128,2048]{2,1,0:T(8,128)(2,1)}, bf16[2,128,2048]{2,1,0:T(8,128)(2,1)}, u32[]{:S(2)}, u32[]{:S(2)}) collective-permute-start(bf16[2,128,2048]{2,1,0:T(8,128)(2,1)} %bitcast.42), channel_id=1, source_target_pairs={{0,2},{1,3},{2,0},{3,1},{4,6},{5,7},{6,4},{7,5},{8,10},{9,11},{10,... | collective-permute-start | bytes 3145736 | tf_op jit(solution)/shard_map/ppermute | solution.py:37
  334.7 255.5 %reduce-scatter.6.cloned.1.call-start = ((), (), s32[]{:S(2)}) async-start(), calls=%async_computation.7 | async-start | bytes 2359296 | tf_op jit(solution)/shard_map/reduce_scatter | solution.py:409
  361.6 25.5 %collective-permute-start.33 = (bf16[2,512,512]{2,1,0:T(8,128)(2,1)S(1)}, bf16[2,512,512]{2,1,0:T(8,128)(2,1)S(1)}, u32[]{:S(2)}, u32[]{:S(2)}) collective-permute-start(bf16[2,512,512]{2,1,0:T(8,128)(2,1)S(1)} %pad_maximum_fusion.14), channel_id=1, source_target_pairs={{0,2},{1,3},{2,0},{3,1},{4,6},{5,7},{6,4},{7,5},{8,10},{9,11},{10,... | collective-permute-start | bytes 3145736 | tf_op jit(solution)/shard_map/ppermute | solution.py:37
  389.0 245.8 %reduce-scatter.8.cloned.1.call-start = ((), (), s32[]{:S(2)}) async-start(), calls=%async_computation.8 | async-start | bytes 2359296 | tf_op jit(solution)/shard_map/reduce_scatter | solution.py:409
  392.7 86.0 %collective-permute-start.38 = (bf16[8,64,2048]{2,1,0:T(8,128)(2,1)}, bf16[8,64,2048]{2,1,0:T(8,128)(2,1)}, u32[]{:S(2)}, u32[]{:S(2)}) collective-permute-start(bf16[8,64,2048]{2,1,0:T(8,128)(2,1)} %dynamic-slice_bitcast_fusion), channel_id=1, source_target_pairs={{0,2},{1,3},{2,0},{3,1},{4,6},{5,7},{6,4},{7,5},{8,10},{9,11},{10,... | collective-permute-start | bytes 6291464 | tf_op jit(solution)/shard_map/ppermute | solution.py:37
  470.4 34.6 %collective-permute-start.39 = (bf16[2,128,2048]{2,1,0:T(8,128)(2,1)}, bf16[2,128,2048]{2,1,0:T(8,128)(2,1)}, u32[]{:S(2)}, u32[]{:S(2)}) collective-permute-start(bf16[2,128,2048]{2,1,0:T(8,128)(2,1)} %slice.669), channel_id=1, source_target_pairs={{0,2},{1,3},{2,0},{3,1},{4,6},{5,7},{6,4},{7,5},{8,10},{9,11},{10,... | collective-permute-start | bytes 3145736 | tf_op jit(solution)/shard_map/ppermute | solution.py:37
  510.9 28.1 %collective-permute-start.58 = (bf16[256,1024]{1,0:T(8,128)(2,1)}, bf16[256,1024]{1,0:T(8,128)(2,1)}, u32[]{:S(2)}, u32[]{:S(2)}) collective-permute-start(bf16[256,1024]{1,0:T(8,128)(2,1)} %reduce-scatter.4.cloned.1.call-done), channel_id=1, source_target_pairs={{0,2},{1,3},{2,0},{3,1},{4,6},{5,7},{6,4},{7,5},{8,10},{9,11},{10,... | collective-permute-start | bytes 1572872 | tf_op jit(solution)/shard_map/ppermute | solution.py:37
  512.4 33.5 %collective-permute-start.60 = (bf16[256,1024]{1,0:T(8,128)(2,1)}, bf16[256,1024]{1,0:T(8,128)(2,1)}, u32[]{:S(2)}, u32[]{:S(2)}) collective-permute-start(bf16[256,1024]{1,0:T(8,128)(2,1)} %reduce-scatter.4.cloned.1.call-done), channel_id=1, source_target_pairs={{0,1},{1,0},{2,3},{3,2},{4,5},{5,4},{6,7},{7,6},{8,9},{9,8},{10,11... | collective-permute-start | bytes 1572872 | tf_op jit(solution)/shard_map/ppermute | solution.py:37
  536.0 24.4 %collective-permute-start.44 = (bf16[256,1664]{1,0:T(8,128)(2,1)}, bf16[256,1664]{1,0:T(8,128)(2,1)S(1)}, u32[]{:S(2)}, u32[]{:S(2)}) collective-permute-start(bf16[256,1664]{1,0:T(8,128)(2,1)} %pad_maximum_fusion.15), channel_id=1, source_target_pairs={{8,0},{16,8},{24,16},{28,24},{20,28},{12,20},{4,12},{0,4},{9,1},{1... | collective-permute-start | bytes 2555912 | tf_op jit(solution)/shard_map/ppermute | solution.py:236
  539.0 25.4 %collective-permute-start.43 = (bf16[256,1664]{1,0:T(8,128)(2,1)}, bf16[256,1664]{1,0:T(8,128)(2,1)S(1)}, u32[]{:S(2)}, u32[]{:S(2)}) collective-permute-start(bf16[256,1664]{1,0:T(8,128)(2,1)} %fusion.63), channel_id=1, source_target_pairs={{0,8},{8,16},{16,24},{24,28},{28,20},{20,12},{12,4},{4,0},{1,9},{9... | collective-permute-start | bytes 2555912 | tf_op jit(solution)/shard_map/ppermute | solution.py:236
  569.8 24.5 %collective-permute-start.48 = (bf16[256,2048]{1,0:T(8,128)(2,1)}, bf16[256,2048]{1,0:T(8,128)(2,1)S(1)}, u32[]{:S(2)}, u32[]{:S(2)}) collective-permute-start(bf16[256,2048]{1,0:T(8,128)(2,1)} %get-tuple-element.297), channel_id=1, source_target_pairs={{0,2},{1,3},{2,0},{3,1},{4,6},{5,7},{6,4},{7,5},{8,10},{9,11},{10,... | collective-permute-start | bytes 3145736 | tf_op jit(solution)/shard_map/ppermute | solution.py:37
  (160 other events, 1829.0 us)
Sparse Core Ops, SparseCore 0:
  92.4 47.8 all-gather.3
  143.0 71.2 all-gather.5
  229.2 50.7 all-gather.7
  334.8 88.1 reduce-scatter.3
  427.0 67.9 reduce-scatter.5
  498.9 74.8 reduce-scatter.7

commit v7 on v6

--- a/solution.py
+++ b/solution.py
@@ -124,8 +124,9 @@
         scores = dot(queries_ref[start:end], keys_ref[low:end], ((1,), (1,))) * factor
         scores = scores + bias[start:end, low:end]
         weights = jnp.exp(scores - jnp.max(scores, -1, keepdims=True))
-        probs = (weights * (1.0 / jnp.sum(weights, -1, keepdims=True))).astype(BF16)
-        mixed_ref[start:end] = dot(probs, values_ref[low:end]).astype(BF16)
+        inverse = 1.0 / jnp.sum(weights, -1, keepdims=True)
+        mixed = dot(weights.astype(BF16), values_ref[low:end]) * inverse
+        mixed_ref[start:end] = mixed.astype(BF16)
 
 
 def attend_back_kernel(
@@ -355,25 +356,32 @@
     )(x, w)
 
 
-def rows_kernel(ids, x, out):
-    out[...] = x[...].astype(out.dtype)
-
-
-def rows_in_order(ids, x):
+def small_kernel(n, first, ids, x, columns, out):
+    rows = x.shape[0] // n
+    for i in range(n):
+        here = pl.ds(pl.multiple_of(ids[i] * rows, 16), rows)
+        block = x[here, :]
+        lanes = lax.broadcasted_iota(jnp.int32, block.shape, 1)
+        for c in range(columns.shape[1]):
+            block = jnp.where(lanes == first + c, columns[here, c : c + 1], block)
+        out[i * rows : (i + 1) * rows] = block.astype(BF16)
+
+
+def small_in_order(ids, x, columns, first):
     n = ids.shape[0]
-    rows, cols = x.shape
+    whole = lambda shape: pl.BlockSpec(shape, lambda i, ids: (0, 0))
     return pl.pallas_call(
-        rows_kernel,
+        functools.partial(small_kernel, n, first),
         grid_spec=pltpu.PrefetchScalarGridSpec(
             num_scalar_prefetch=1,
-            grid=(n,),
-            in_specs=[pl.BlockSpec((rows // n, cols), lambda i, ids: (ids[i], 0))],
-            out_specs=pl.BlockSpec((rows // n, cols), lambda i, ids: (i, 0)),
+            grid=(1,),
+            in_specs=[whole(x.shape), whole(columns.shape)],
+            out_specs=whole(x.shape),
         ),
-        out_shape=jax.ShapeDtypeStruct((rows, cols), BF16),
-        cost_estimate=cost(0, 4 * rows * cols),
-        name="rows_in_order",
-    )(ids, x)
+        out_shape=jax.ShapeDtypeStruct(x.shape, BF16),
+        cost_estimate=cost(0, 8 * x.size),
+        name="small_in_order",
+    )(ids, x, columns)
 
 
 def ring_scatter(parts, n, due):
@@ -624,7 +632,7 @@
     logits_grad = (
         probs_all * (chosen_grad - jnp.sum(probs_all * chosen_grad, -1, keepdims=True))
     ).astype(BF16)
-    router_grad = dot(inner, logits_grad, ((0,), (0,)))
+    router_grad = dot(inner, jnp.pad(logits_grad, ((0, 0), (0, 128 - routed))), ((0,), (0,)))
     inner_grad = add_slots(slot_input_grad) + dot(logits_grad, router_w, ((1,), (1,)))
     residual_part, gain_two_grad = norm_back(residual, scale_two, gain_two, inner_grad)
     residual_grad = upstream + residual_part
@@ -672,9 +680,7 @@
         jnp.zeros((width,), F32), g, rep * part, 0
     )
     small = jnp.stack([gain_two_grad, place(gain_query_grad), place(gain_key_grad)], 1)
-    small = jnp.concatenate(
-        [router_grad, small, jnp.zeros((width, 128 - 3 - routed), F32)], 1
-    )
+    small = small_in_order(ring, router_grad, small, routed)
     back = lambda slots, first, count, dtype: back_product(
         slots, w_qkv, first, count, length, dtype
     )
@@ -695,7 +701,7 @@
         lambda zero, rest, top, down: (zero, top, swap(rest, 2), down),
     )
     qkv_owned, (normed_grad, top, rest, down_owned) = ring_scatter(
-        [qkv_w_grad, rows_in_order(ring, small)], n_shard, due
+        [qkv_w_grad, small], n_shard, due
     )
     normed_grad = normed_grad + jnp.concatenate([top, rest], 0).astype(F32)
     weighted = normed_grad * gain_one

time: 680 us -> 685 us (level)
  waiting for transfers between devices: 153 us -> 177 us
  local copies, waits for them, and re-layouts: 110 us -> 98.4 us
  Pallas kernels: 126 us -> 115 us
    ppermute x16, waiting for transfers between devices: 62.3 us -> 77.5 us  [ring_step(): lax.ppermute(x, 'shard', [(b, a) for a, b in pairs] if back else pairs)]
    ppermute x48, waiting for transfers between devices: 88.9 us -> 99.5 us  [swap(): return lax.ppermute(x, 'rep', [(i, i ^ mask) for i in range(4)])]
    pallas_call x1, Pallas kernels: 35 us -> 27 us  [attend(): pl.pallas_call(functools.partial(attend_kernel, dim ** (-0.5)), grid=(tok...]
    unnamed x238 -> x220, local copies, waits for them, and re-layouts: 34.5 us -> 30.1 us
  transfers between devices with their start and end apart: 70 -> 70, of which waited for: 37 -> 38; matrix products, arithmetic and copies ran while one was open for 41% -> 41% of each run, Pallas kernels for 19% -> 17%
where the time goes in v7:
time: 685 us; the launch traced here: 678 us
  waiting for transfers between devices  177 us (26%)
  other arithmetic  126 us (18%)
  Pallas kernels  115 us (17%)
  matrix products  99.6 us (15%)
  local copies, waits for them, and re-layouts  98.4 us (14%)
  starting transfers between devices  46.2 us (7%)
  between operations  16.2 us (2%)
    dot_general x31, matrix products, dot(): return lax.dot_general(a, b, (dims, ((), ())), preferred_element_type=F32)  99.6 us
    ppermute x48, waiting for transfers between devices, swap(): return lax.ppermute(x, 'rep', [(i, i ^ mask) for i in range(4)])  99.5 us
    ppermute x16, waiting for transfers between devices, ring_step(): lax.ppermute(x, 'shard', [(b, a) for a, b in pairs] if back else pairs)  77.5 us
    pallas_call x1, Pallas kernels, attend_back(): pl.pallas_call(functools.partial(attend_back_kernel, dim ** (-0.5)), grid...  38.2 us
    unnamed x220, local copies, waits for them, and re-layouts  30.1 us
    pallas_call x3, Pallas kernels, back_product(): pl.pallas_call(back_kernel, grid=(count, cols // step), in_specs=[pl.Bloc...  29 us
    ppermute x48, starting transfers between devices, swap(): return lax.ppermute(x, 'rep', [(i, i ^ mask) for i in range(4)])  28.1 us
    pallas_call x1, Pallas kernels, attend(): pl.pallas_call(functools.partial(attend_kernel, dim ** (-0.5)), grid=(tok...  27 us
  transfers between devices with their start and end apart: 70, of which 38 were waited for; matrix products, arithmetic and copies ran while one was open for 41% of the time, Pallas kernels for 17%

profile of v7, /device:TPU:0, one launch (start us, length us, event | category | flops | bytes accessed | tf_op | source)
XLA Modules:
  0.0 678.4 jit_solution(584502299314536311)
XLA Ops:
  30.8 10.9 %collective-permute-done.2.refs_2_ = bf16[256,1664]{1,0:T(8,128)(2,1)} collective-permute-done((bf16[256,1664]{1,0:T(8,128)(2,1)}, bf16[256,1664]{1,0:T(8,128)(2,1)}, u32[]{:S(2)}, u32[]{:S(2)}) %collective-permute-start.2) | collective-permute-done | bytes 852000 | tf_op jit(solution)/shard_map/ppermute | solution.py:237
  48.1 15.0 %collective-permute-done.3.refs_3_ = bf16[256,1664]{1,0:T(8,128)(2,1)} collective-permute-done((bf16[256,1664]{1,0:T(8,128)(2,1)}, bf16[256,1664]{1,0:T(8,128)(2,1)}, u32[]{:S(2)}, u32[]{:S(2)}) %collective-permute-start.3) | collective-permute-done | bytes 852000 | tf_op jit(solution)/shard_map/ppermute | solution.py:237
  71.2 11.4 %collective-permute-done.5.refs_5_ = bf16[256,1664]{1,0:T(8,128)(2,1)} collective-permute-done((bf16[256,1664]{1,0:T(8,128)(2,1)}, bf16[256,1664]{1,0:T(8,128)(2,1)}, u32[]{:S(2)}, u32[]{:S(2)}) %collective-permute-start.5) | collective-permute-done | bytes 852000 | tf_op jit(solution)/shard_map/ppermute | solution.py:237
  105.8 6.9 %collective-permute-done.13.refs_8_ = bf16[128,1664]{1,0:T(8,128)(2,1)S(1)} collective-permute-done((bf16[128,1664]{1,0:T(8,128)(2,1)S(1)}, bf16[128,1664]{1,0:T(8,128)(2,1)S(1)}, u32[]{:S(2)}, u32[]{:S(2)}) %collective-permute-start.13) | collective-permute-done | bytes 426016 | tf_op jit(solution)/shard_map/ppermute | solution.py:237
  113.4 6.4 place_rows.1
  122.8 17.5 %fusion.3.q_ref.k_ref.v_ref = f32[2048,1536]{1,0:T(8,128)S(1)} fusion(bf16[2048,1536]{1,0:T(8,128)(2,1)} %get-tuple-element.112.w, bf16[2048,2048]{1,0:T(8,128)(2,1)} %constant_dynamic-update-slice_fusion.hidden, f32[2048]{0:T(1024)S(1)} %bitcast.263, f32[2048]{0:T(1024)S(1)} %add_rsqrt_fusion), kind=kOutput, calls=%fused_computation.5 | convolution fusion | flops 12901679104 | bytes 27279360 | tf_op jit(solution)/shard_map/dot_general | solution.py:33
  140.3 6.2 collective-permute-done.15
  162.6 27.0 %attend.1 = (bf16[2048,512]{1,0:T(8,128)(2,1)}, bf16[2048,512]{1,0:T(8,128)(2,1)}, bf16[2048,512]{1,0:T(8,128)(2,1)}, bf16[2048,512]{1,0:T(8,128)(2,1)}) custom-call(f32[2048,1536]{1,0:T(8,128)} %copy-done.2, f32[2048,1536]{1,0:T(8,128)} %copy-done.2, f32[2048,1536]{1,0:T(8,128)} %copy-done.2, f32[2048,1]{1,0:T(8,128)} %get-tuple-element.314.q_scale, ...), custom_call_target="tpu_custom_call" | custom-call | flops 2147483648 | bytes 20971520 | tf_op jit(solution)/shard_map/attend/pallas_call | solution.py:185
  189.6 13.7 %collective-permute-done.19 = bf16[8,64,2048]{2,1,0:T(8,128)(2,1)} collective-permute-done((bf16[8,64,2048]{2,1,0:T(8,128)(2,1)}, bf16[8,64,2048]{2,1,0:T(8,128)(2,1)}, u32[]{:S(2)}, u32[]{:S(2)}) %collective-permute-start.19) | collective-permute-done | bytes 2097184 | tf_op jit(solution)/shard_map/ppermute | solution.py:37
  212.1 11.1 %normed_in_order.1 = bf16[2048,2048]{1,0:T(8,128)(2,1)} custom-call(s32[8]{0:T(128)} %fusion.119.ids, bf16[2048,2048]{1,0:T(8,128)(2,1)} %constant_dynamic-update-slice_fusion.hidden, f32[2048,1]{1,0:T(8,128)} %copy.109.scale, f32[1,2048]{1,0:T(1,128)} %copy-done.81), custom_call_target="tpu_custom_call" | custom-call | bytes 134217728 | tf_op jit(solution)/shard_map/normed_in_order/pallas_call | solution.py:319
  239.3 8.0 %multiply_reduce_fusion.6 = (f32[512]{0:T(512)S(1)}, f32[512,2048]{1,0:T(8,128)S(1)}) fusion(bf16[2048,2048]{1,0:T(8,128)(2,1)} %bitcast.239, bf16[512,512]{1,0:T(8,128)(2,1)S(1)} %get-tuple-element.280, bf16[512,512]{1,0:T(8,128)(2,1)S(1)} %get-tuple-element.279, bf16[512,512]{1,0:T(8,128)(2,1)S(1)} %get-tuple-element.278, ...), kind=kOutput, calls=%fused_computation.43 | convolution fusion | flops 4307549696 | bytes 16779264 | tf_op jit(solution)/shard_map/dot_general | solution.py:33
  258.9 20.0 %collective-permute-done.27 = bf16[2,128,2048]{2,1,0:T(8,128)(2,1)} collective-permute-done((bf16[2,128,2048]{2,1,0:T(8,128)(2,1)}, bf16[2,128,2048]{2,1,0:T(8,128)(2,1)}, u32[]{:S(2)}, u32[]{:S(2)}) %collective-permute-start.27) | collective-permute-done | bytes 1048608 | tf_op jit(solution)/shard_map/ppermute | solution.py:37
  326.9 6.2 convolution_convert_fusion.2
  378.2 13.8 %collective-permute-done.33 = bf16[2,512,512]{2,1,0:T(8,128)(2,1)S(1)} collective-permute-done((bf16[2,512,512]{2,1,0:T(8,128)(2,1)S(1)}, bf16[2,512,512]{2,1,0:T(8,128)(2,1)S(1)}, u32[]{:S(2)}, u32[]{:S(2)}) %collective-permute-start.33) | collective-permute-done | bytes 1048608 | tf_op jit(solution)/shard_map/ppermute | solution.py:37
  402.0 38.2 %attend_back.1 = (f32[2048,512]{1,0:T(8,128)}, f32[2048,512]{1,0:T(8,128)}, bf16[2048,512]{1,0:T(8,128)(2,1)}) custom-call(bf16[2048,512]{1,0:T(8,128)(2,1)} %get-tuple-element.128.queries, bf16[2048,512]{1,0:T(8,128)(2,1)} %get-tuple-element.129.keys, bf16[2048,512]{1,0:T(8,128)(2,1)} %get-tuple-element.130.values, ...), custom_call_target="tpu_custom_call" | custom-call | flops 5368709120 | bytes 18874368 | tf_op jit(solution)/shard_map/attend_back/pallas_call | solution.py:208
  440.2 7.0 %multiply_reduce_fusion.1 = (f32[512]{0:T(512)S(1)}, f32[2048]{0:T(1024)S(1)}, f32[2048]{0:T(1024)S(1)}, f32[512]{0:T(512)S(1)}) fusion(f32[2048,512]{1,0:T(8,128)} %get-tuple-element.140, f32[2048,1536]{1,0:T(8,128)} %copy-done.2, f32[2048]{0:T(1024)S(1)} %get-tuple-element.248, f32[512]{0:T(512)S(1)} %bitcast.284, f32[2048,512]{1,0:T(8,128)} %get-tuple-element.141, ...), kind=kLoop, calls=%fused_computation.32 | loop fusion | flops 12577792 | bytes 16818176 | tf_op jit(solution)/shard_map/reduce_sum | solution.py:665
  466.2 6.5 subtract_convert_fusion.1
  476.6 19.3 %convolution_convert_fusion = bf16[2048,1536]{1,0:T(8,128)(2,1)} fusion(bf16[2048,2048]{1,0:T(8,128)(2,1)} %normed_in_order.1, bf16[2048,512]{1,0:T(8,128)(2,1)} %get-tuple-element.147, bf16[2048,512]{1,0:T(8,128)(2,1)} %get-tuple-element.263, bf16[2048,512]{1,0:T(8,128)(2,1)S(1)} %get-tuple-element.262), kind=kOutput, calls=%fused_computation.10 | convolution fusion | flops 12906921984 | bytes 20971520 | tf_op jit(solution)/shard_map/dot_general | solution.py:33
  511.8 13.3 %back_product.3 = bf16[2,512,2048]{2,1,0:T(8,128)(2,1)} custom-call(bf16[2048,1536]{1,0:T(8,128)(2,1)} %pad_maximum_fusion.1.x, bf16[2048,1536]{1,0:T(8,128)(2,1)} %get-tuple-element.112.w), custom_call_target="tpu_custom_call" | custom-call | bytes 134217728 | tf_op jit(solution)/shard_map/back_product/pallas_call | solution.py:345
  550.6 7.9 %back_product.4 = f32[1,512,2048]{2,1,0:T(8,128)} custom-call(bf16[2048,1536]{1,0:T(8,128)(2,1)} %pad_maximum_fusion.1.x, bf16[2048,1536]{1,0:T(8,128)(2,1)} %get-tuple-element.112.w), custom_call_target="tpu_custom_call" | custom-call | bytes 134217728 | tf_op jit(solution)/shard_map/back_product/pallas_call | solution.py:345
  575.1 7.9 %back_product.5 = f32[1,512,2048]{2,1,0:T(8,128)} custom-call(bf16[2048,1536]{1,0:T(8,128)(2,1)} %pad_maximum_fusion.1.x, bf16[2048,1536]{1,0:T(8,128)(2,1)} %get-tuple-element.112.w), custom_call_target="tpu_custom_call" | custom-call | bytes 134217728 | tf_op jit(solution)/shard_map/back_product/pallas_call | solution.py:345
  607.7 9.5 %collective-permute-done.50 = bf16[256,1664]{1,0:T(8,128)(2,1)S(1)} collective-permute-done((bf16[256,1664]{1,0:T(8,128)(2,1)S(1)}, bf16[256,1664]{1,0:T(8,128)(2,1)S(1)}, u32[]{:S(2)}, u32[]{:S(2)}) %collective-permute-start.50) | collective-permute-done | bytes 852000 | tf_op jit(solution)/shard_map/ppermute | solution.py:237
  632.5 6.2 fusion.13
  638.9 11.5 %collective-permute-done.53 = bf16[256,1664]{1,0:T(8,128)(2,1)} collective-permute-done((bf16[256,1664]{1,0:T(8,128)(2,1)}, bf16[256,1664]{1,0:T(8,128)(2,1)}, u32[]{:S(2)}, u32[]{:S(2)}) %collective-permute-start.53) | collective-permute-done | bytes 852000 | tf_op jit(solution)/shard_map/ppermute | solution.py:37
  (556 shorter events, 361.1 us)
Async XLA Ops:
  7.2 149.1 %all-gather.4.cloned.1.call-start = ((), (), s32[]{:S(2)}) async-start(), calls=%async_computation.3 | async-start | bytes 2359296 | tf_op jit(solution)/shard_map/all_gather | solution.py:413
  7.2 38.8 %collective-permute-start.8 = (s32[1,512]{1,0:T(1,128)}, s32[1,512]{1,0:T(1,128)S(1)}, u32[]{:S(2)}, u32[]{:S(2)}) collective-permute-start(s32[1,512]{1,0:T(1,128)} %param.20), channel_id=1, source_target_pairs={{0,1},{1,0},{2,3},{3,2},{4,5},{5,4},{6,7},{7,6},{8,9},{9,8},{10,11... | collective-permute-start | bytes 6152 | tf_op jit(solution)/shard_map/ppermute | solution.py:37
  7.8 38.1 %collective-permute-start.9 = (s32[1,512]{1,0:T(1,128)}, s32[1,512]{1,0:T(1,128)S(1)}, u32[]{:S(2)}, u32[]{:S(2)}) collective-permute-start(s32[1,512]{1,0:T(1,128)} %param.20), channel_id=1, source_target_pairs={{0,2},{1,3},{2,0},{3,1},{4,6},{5,7},{6,4},{7,5},{8,10},{9,11},{10,... | collective-permute-start | bytes 6152 | tf_op jit(solution)/shard_map/ppermute | solution.py:37
  22.4 61.5 %collective-permute-start.7 = (bf16[512,2048]{1,0:T(8,128)(2,1)}, bf16[512,2048]{1,0:T(8,128)(2,1)}, u32[]{:S(2)}, u32[]{:S(2)}) collective-permute-start(bf16[512,2048]{1,0:T(8,128)(2,1)} %param.19), channel_id=1, source_target_pairs={{0,2},{1,3},{2,0},{3,1},{4,6},{5,7},{6,4},{7,5},{8,10},{9,11},{10,... | collective-permute-start | bytes 6291464 | tf_op jit(solution)/shard_map/ppermute | solution.py:37
  46.1 40.5 %collective-permute-start = (bf16[512,2048]{1,0:T(8,128)(2,1)S(1)}, bf16[512,2048]{1,0:T(8,128)(2,1)}, u32[]{:S(2)}, u32[]{:S(2)}) collective-permute-start(bf16[512,2048]{1,0:T(8,128)(2,1)S(1)} %copy-done.13), channel_id=1, source_target_pairs={{0,1},{1,0},{2,3},{3,2},{4,5},{5,4},{6,7},{7,6},{8,9},{9,8},{10,11... | collective-permute-start | bytes 6291464 | tf_op jit(solution)/shard_map/ppermute | solution.py:37
  89.8 144.6 %all-gather.6.cloned.1.call-start = ((), (), s32[]{:S(2)}) async-start(), calls=%async_computation.4 | async-start | bytes 4718592 | tf_op jit(solution)/shard_map/all_gather | solution.py:413
  147.6 136.8 %all-gather.8.cloned.1.call-start = ((), (), s32[]{:S(2)}) async-start(), calls=%async_computation.5 | async-start | bytes 2359296 | tf_op jit(solution)/shard_map/all_gather | solution.py:413
  156.3 47.1 %collective-permute-start.19 = (bf16[8,64,2048]{2,1,0:T(8,128)(2,1)}, bf16[8,64,2048]{2,1,0:T(8,128)(2,1)}, u32[]{:S(2)}, u32[]{:S(2)}) collective-permute-start(bf16[8,64,2048]{2,1,0:T(8,128)(2,1)} %bitcast.249), channel_id=1, source_target_pairs={{0,2},{1,3},{2,0},{3,1},{4,6},{5,7},{6,4},{7,5},{8,10},{9,11},{10,... | collective-permute-start | bytes 6291464 | tf_op jit(solution)/shard_map/ppermute | solution.py:37
  157.3 46.1 %collective-permute-start.18 = (bf16[8,64,2048]{2,1,0:T(8,128)(2,1)}, bf16[8,64,2048]{2,1,0:T(8,128)(2,1)}, u32[]{:S(2)}, u32[]{:S(2)}) collective-permute-start(bf16[8,64,2048]{2,1,0:T(8,128)(2,1)} %bitcast.250), channel_id=1, source_target_pairs={{0,1},{1,0},{2,3},{3,2},{4,5},{5,4},{6,7},{7,6},{8,9},{9,8},{10,11... | collective-permute-start | bytes 6291464 | tf_op jit(solution)/shard_map/ppermute | solution.py:37
  209.2 25.3 %collective-permute-start.20 = (bf16[2,512,512]{2,1,0:T(8,128)(2,1)}, bf16[2,512,512]{2,1,0:T(8,128)(2,1)S(1)}, u32[]{:S(2)}, u32[]{:S(2)}) collective-permute-start(bf16[2,512,512]{2,1,0:T(8,128)(2,1)} %bitcast.17), channel_id=1, source_target_pairs={{0,2},{1,3},{2,0},{3,1},{4,6},{5,7},{6,4},{7,5},{8,10},{9,11},{10,... | collective-permute-start | bytes 3145736 | tf_op jit(solution)/shard_map/ppermute | solution.py:37
  235.4 263.7 %reduce-scatter.4.cloned.1.call-start = ((), (), s32[]{:S(2)}) async-start(), calls=%async_computation.6 | async-start | bytes 4718592 | tf_op jit(solution)/shard_map/reduce_scatter | solution.py:417
  253.4 25.5 %collective-permute-start.27 = (bf16[2,128,2048]{2,1,0:T(8,128)(2,1)}, bf16[2,128,2048]{2,1,0:T(8,128)(2,1)}, u32[]{:S(2)}, u32[]{:S(2)}) collective-permute-start(bf16[2,128,2048]{2,1,0:T(8,128)(2,1)} %pad_maximum_fusion.12), channel_id=1, source_target_pairs={{0,2},{1,3},{2,0},{3,1},{4,6},{5,7},{6,4},{7,5},{8,10},{9,11},{10,... | collective-permute-start | bytes 3145736 | tf_op jit(solution)/shard_map/ppermute | solution.py:37
  311.4 24.4 %collective-permute-start.28 = (bf16[2,128,2048]{2,1,0:T(8,128)(2,1)}, bf16[2,128,2048]{2,1,0:T(8,128)(2,1)}, u32[]{:S(2)}, u32[]{:S(2)}) collective-permute-start(bf16[2,128,2048]{2,1,0:T(8,128)(2,1)} %bitcast.42), channel_id=1, source_target_pairs={{0,2},{1,3},{2,0},{3,1},{4,6},{5,7},{6,4},{7,5},{8,10},{9,11},{10,... | collective-permute-start | bytes 3145736 | tf_op jit(solution)/shard_map/ppermute | solution.py:37
  339.6 249.1 %reduce-scatter.6.cloned.1.call-start = ((), (), s32[]{:S(2)}) async-start(), calls=%async_computation.7 | async-start | bytes 2359296 | tf_op jit(solution)/shard_map/reduce_scatter | solution.py:417
  366.5 25.5 %collective-permute-start.33 = (bf16[2,512,512]{2,1,0:T(8,128)(2,1)S(1)}, bf16[2,512,512]{2,1,0:T(8,128)(2,1)S(1)}, u32[]{:S(2)}, u32[]{:S(2)}) collective-permute-start(bf16[2,512,512]{2,1,0:T(8,128)(2,1)S(1)} %pad_maximum_fusion.14), channel_id=1, source_target_pairs={{0,2},{1,3},{2,0},{3,1},{4,6},{5,7},{6,4},{7,5},{8,10},{9,11},{10,... | collective-permute-start | bytes 3145736 | tf_op jit(solution)/shard_map/ppermute | solution.py:37
  394.6 244.2 %reduce-scatter.8.cloned.1.call-start = ((), (), s32[]{:S(2)}) async-start(), calls=%async_computation.8 | async-start | bytes 2359296 | tf_op jit(solution)/shard_map/reduce_scatter | solution.py:417
  398.0 74.7 %collective-permute-start.38 = (bf16[8,64,2048]{2,1,0:T(8,128)(2,1)}, bf16[8,64,2048]{2,1,0:T(8,128)(2,1)}, u32[]{:S(2)}, u32[]{:S(2)}) collective-permute-start(bf16[8,64,2048]{2,1,0:T(8,128)(2,1)} %dynamic-slice_bitcast_fusion), channel_id=1, source_target_pairs={{0,2},{1,3},{2,0},{3,1},{4,6},{5,7},{6,4},{7,5},{8,10},{9,11},{10,... | collective-permute-start | bytes 6291464 | tf_op jit(solution)/shard_map/ppermute | solution.py:37
  464.7 34.3 %collective-permute-start.39 = (bf16[2,128,2048]{2,1,0:T(8,128)(2,1)}, bf16[2,128,2048]{2,1,0:T(8,128)(2,1)}, u32[]{:S(2)}, u32[]{:S(2)}) collective-permute-start(bf16[2,128,2048]{2,1,0:T(8,128)(2,1)} %slice.669), channel_id=1, source_target_pairs={{0,2},{1,3},{2,0},{3,1},{4,6},{5,7},{6,4},{7,5},{8,10},{9,11},{10,... | collective-permute-start | bytes 3145736 | tf_op jit(solution)/shard_map/ppermute | solution.py:37
  499.1 45.0 %collective-permute-start.60 = (bf16[256,1024]{1,0:T(8,128)(2,1)}, bf16[256,1024]{1,0:T(8,128)(2,1)}, u32[]{:S(2)}, u32[]{:S(2)}) collective-permute-start(bf16[256,1024]{1,0:T(8,128)(2,1)} %reduce-scatter.4.cloned.1.call-done), channel_id=1, source_target_pairs={{0,1},{1,0},{2,3},{3,2},{4,5},{5,4},{6,7},{7,6},{8,9},{9,8},{10,11... | collective-permute-start | bytes 1572872 | tf_op jit(solution)/shard_map/ppermute | solution.py:37
  499.2 38.0 %collective-permute-start.58 = (bf16[256,1024]{1,0:T(8,128)(2,1)}, bf16[256,1024]{1,0:T(8,128)(2,1)}, u32[]{:S(2)}, u32[]{:S(2)}) collective-permute-start(bf16[256,1024]{1,0:T(8,128)(2,1)} %reduce-scatter.4.cloned.1.call-done), channel_id=1, source_target_pairs={{0,2},{1,3},{2,0},{3,1},{4,6},{5,7},{6,4},{7,5},{8,10},{9,11},{10,... | collective-permute-start | bytes 1572872 | tf_op jit(solution)/shard_map/ppermute | solution.py:37
  533.1 25.4 %collective-permute-start.44 = (bf16[256,1664]{1,0:T(8,128)(2,1)}, bf16[256,1664]{1,0:T(8,128)(2,1)S(1)}, u32[]{:S(2)}, u32[]{:S(2)}) collective-permute-start(bf16[256,1664]{1,0:T(8,128)(2,1)} %pad_maximum_fusion.15), channel_id=1, source_target_pairs={{8,0},{16,8},{24,16},{28,24},{20,28},{12,20},{4,12},{0,4},{9,1},{1... | collective-permute-start | bytes 2555912 | tf_op jit(solution)/shard_map/ppermute | solution.py:237
  535.4 27.0 %collective-permute-start.43 = (bf16[256,1664]{1,0:T(8,128)(2,1)}, bf16[256,1664]{1,0:T(8,128)(2,1)}, u32[]{:S(2)}, u32[]{:S(2)}) collective-permute-start(bf16[256,1664]{1,0:T(8,128)(2,1)} %fusion.63), channel_id=1, source_target_pairs={{0,8},{8,16},{16,24},{24,28},{28,20},{20,12},{12,4},{4,0},{1,9},{9... | collective-permute-start | bytes 2555912 | tf_op jit(solution)/shard_map/ppermute | solution.py:237
  563.5 29.6 %collective-permute-start.47 = (bf16[256,1664]{1,0:T(8,128)(2,1)}, bf16[256,1664]{1,0:T(8,128)(2,1)}, u32[]{:S(2)}, u32[]{:S(2)}) collective-permute-start(bf16[256,1664]{1,0:T(8,128)(2,1)} %add_convert_fusion.4), channel_id=1, source_target_pairs={{8,0},{16,8},{24,16},{28,24},{20,28},{12,20},{4,12},{0,4},{9,1},{1... | collective-permute-start | bytes 2555912 | tf_op jit(solution)/shard_map/ppermute | solution.py:237
  568.8 26.2 %collective-permute-start.48 = (bf16[256,2048]{1,0:T(8,128)(2,1)}, bf16[256,2048]{1,0:T(8,128)(2,1)S(1)}, u32[]{:S(2)}, u32[]{:S(2)}) collective-permute-start(bf16[256,2048]{1,0:T(8,128)(2,1)} %get-tuple-element.297), channel_id=1, source_target_pairs={{0,2},{1,3},{2,0},{3,1},{4,6},{5,7},{6,4},{7,5},{8,10},{9,11},{10,... | collective-permute-start | bytes 3145736 | tf_op jit(solution)/shard_map/ppermute | solution.py:37
  (151 other events, 1316.3 us)
Sparse Core Ops, SparseCore 0:
  90.0 51.4 all-gather.3
  147.7 72.3 all-gather.5
  235.5 48.6 all-gather.7
  339.7 87.8 reduce-scatter.3
  431.5 67.9 reduce-scatter.5
  503.5 81.2 reduce-scatter.7

commit v8 on v7

--- a/solution.py
+++ b/solution.py
@@ -632,7 +632,8 @@
     logits_grad = (
         probs_all * (chosen_grad - jnp.sum(probs_all * chosen_grad, -1, keepdims=True))
     ).astype(BF16)
-    router_grad = dot(inner, jnp.pad(logits_grad, ((0, 0), (0, 128 - routed))), ((0,), (0,)))
+    router_grad = dot(inner, logits_grad, ((0,), (0,)))
+    router_grad = jnp.pad(router_grad, ((0, 0), (0, 128 - routed)))
     inner_grad = add_slots(slot_input_grad) + dot(logits_grad, router_w, ((1,), (1,)))
     residual_part, gain_two_grad = norm_back(residual, scale_two, gain_two, inner_grad)
     residual_grad = upstream + residual_part

time: 685 us -> 685 us (level)
    unnamed x220 -> x224, local copies, waits for them, and re-layouts: 30.1 us -> 30.8 us
where the time goes in v8:
time: 685 us; the launch traced here: 678 us
  waiting for transfers between devices  177 us (26%)
  other arithmetic  124 us (18%)
  Pallas kernels  115 us (17%)
  local copies, waits for them, and re-layouts  100 us (15%)
  matrix products  98.7 us (14%)
  starting transfers between devices  45.8 us (7%)
  between operations  16.3 us (2%)
    ppermute x48, waiting for transfers between devices, swap(): return lax.ppermute(x, 'rep', [(i, i ^ mask) for i in range(4)])  100 us
    dot_general x31, matrix products, dot(): return lax.dot_general(a, b, (dims, ((), ())), preferred_element_type=F32)  98.7 us
    ppermute x16, waiting for transfers between devices, ring_step(): lax.ppermute(x, 'shard', [(b, a) for a, b in pairs] if back else pairs)  76.7 us
    pallas_call x1, Pallas kernels, attend_back(): pl.pallas_call(functools.partial(attend_back_kernel, dim ** (-0.5)), grid...  38.2 us
    unnamed x224, local copies, waits for them, and re-layouts  30.8 us
    pallas_call x3, Pallas kernels, back_product(): pl.pallas_call(back_kernel, grid=(count, cols // step), in_specs=[pl.Bloc...  29.2 us
    ppermute x48, starting transfers between devices, swap(): return lax.ppermute(x, 'rep', [(i, i ^ mask) for i in range(4)])  27.4 us
    pallas_call x1, Pallas kernels, attend(): pl.pallas_call(functools.partial(attend_kernel, dim ** (-0.5)), grid=(tok...  27 us
  transfers between devices with their start and end apart: 70, of which 38 were waited for; matrix products, arithmetic and copies ran while one was open for 41% of the time, Pallas kernels for 17%

profile of v8, /device:TPU:0, one launch (start us, length us, event | category | flops | bytes accessed | tf_op | source)
XLA Modules:
  0.0 678.0 jit_solution(10165236640475740578)
XLA Ops:
  30.8 10.9 %collective-permute-done.2.refs_2_ = bf16[256,1664]{1,0:T(8,128)(2,1)} collective-permute-done((bf16[256,1664]{1,0:T(8,128)(2,1)}, bf16[256,1664]{1,0:T(8,128)(2,1)}, u32[]{:S(2)}, u32[]{:S(2)}) %collective-permute-start.2) | collective-permute-done | bytes 852000 | tf_op jit(solution)/shard_map/ppermute | solution.py:237
  48.1 15.0 %collective-permute-done.3.refs_3_ = bf16[256,1664]{1,0:T(8,128)(2,1)} collective-permute-done((bf16[256,1664]{1,0:T(8,128)(2,1)}, bf16[256,1664]{1,0:T(8,128)(2,1)}, u32[]{:S(2)}, u32[]{:S(2)}) %collective-permute-start.3) | collective-permute-done | bytes 852000 | tf_op jit(solution)/shard_map/ppermute | solution.py:237
  71.2 11.4 %collective-permute-done.5.refs_5_ = bf16[256,1664]{1,0:T(8,128)(2,1)} collective-permute-done((bf16[256,1664]{1,0:T(8,128)(2,1)}, bf16[256,1664]{1,0:T(8,128)(2,1)}, u32[]{:S(2)}, u32[]{:S(2)}) %collective-permute-start.5) | collective-permute-done | bytes 852000 | tf_op jit(solution)/shard_map/ppermute | solution.py:237
  105.8 6.8 %collective-permute-done.13.refs_8_ = bf16[128,1664]{1,0:T(8,128)(2,1)S(1)} collective-permute-done((bf16[128,1664]{1,0:T(8,128)(2,1)S(1)}, bf16[128,1664]{1,0:T(8,128)(2,1)S(1)}, u32[]{:S(2)}, u32[]{:S(2)}) %collective-permute-start.13) | collective-permute-done | bytes 426016 | tf_op jit(solution)/shard_map/ppermute | solution.py:237
  113.4 6.4 place_rows.1
  122.8 17.5 %fusion.3.q_ref.k_ref.v_ref = f32[2048,1536]{1,0:T(8,128)S(1)} fusion(bf16[2048,1536]{1,0:T(8,128)(2,1)} %get-tuple-element.112.w, bf16[2048,2048]{1,0:T(8,128)(2,1)} %constant_dynamic-update-slice_fusion.hidden, f32[2048]{0:T(1024)S(1)} %bitcast.262, f32[2048]{0:T(1024)S(1)} %add_rsqrt_fusion), kind=kOutput, calls=%fused_computation.5 | convolution fusion | flops 12901679104 | bytes 27279360 | tf_op jit(solution)/shard_map/dot_general | solution.py:33
  162.7 27.0 %attend.1 = (bf16[2048,512]{1,0:T(8,128)(2,1)}, bf16[2048,512]{1,0:T(8,128)(2,1)}, bf16[2048,512]{1,0:T(8,128)(2,1)}, bf16[2048,512]{1,0:T(8,128)(2,1)}) custom-call(f32[2048,1536]{1,0:T(8,128)} %copy-done.2, f32[2048,1536]{1,0:T(8,128)} %copy-done.2, f32[2048,1536]{1,0:T(8,128)} %copy-done.2, f32[2048,1]{1,0:T(8,128)} %get-tuple-element.314.q_scale, ...), custom_call_target="tpu_custom_call" | custom-call | flops 2147483648 | bytes 20971520 | tf_op jit(solution)/shard_map/attend/pallas_call | solution.py:185
  189.7 13.7 %collective-permute-done.19 = bf16[8,64,2048]{2,1,0:T(8,128)(2,1)} collective-permute-done((bf16[8,64,2048]{2,1,0:T(8,128)(2,1)}, bf16[8,64,2048]{2,1,0:T(8,128)(2,1)}, u32[]{:S(2)}, u32[]{:S(2)}) %collective-permute-start.19) | collective-permute-done | bytes 2097184 | tf_op jit(solution)/shard_map/ppermute | solution.py:37
  212.2 11.1 %normed_in_order.1 = bf16[2048,2048]{1,0:T(8,128)(2,1)} custom-call(s32[8]{0:T(128)} %fusion.120.ids, bf16[2048,2048]{1,0:T(8,128)(2,1)} %constant_dynamic-update-slice_fusion.hidden, f32[2048,1]{1,0:T(8,128)} %copy.112.scale, f32[1,2048]{1,0:T(1,128)} %copy-done.83), custom_call_target="tpu_custom_call" | custom-call | bytes 134217728 | tf_op jit(solution)/shard_map/normed_in_order/pallas_call | solution.py:319
  239.4 8.0 %multiply_reduce_fusion.6 = (f32[512]{0:T(512)S(1)}, f32[512,2048]{1,0:T(8,128)S(1)}) fusion(bf16[2048,2048]{1,0:T(8,128)(2,1)} %bitcast.238, bf16[512,512]{1,0:T(8,128)(2,1)S(1)} %get-tuple-element.280, bf16[512,512]{1,0:T(8,128)(2,1)S(1)} %get-tuple-element.279, bf16[512,512]{1,0:T(8,128)(2,1)S(1)} %get-tuple-element.278, ...), kind=kOutput, calls=%fused_computation.43 | convolution fusion | flops 4307549696 | bytes 16779264 | tf_op jit(solution)/shard_map/dot_general | solution.py:33
  259.0 20.0 %collective-permute-done.27 = bf16[2,128,2048]{2,1,0:T(8,128)(2,1)} collective-permute-done((bf16[2,128,2048]{2,1,0:T(8,128)(2,1)}, bf16[2,128,2048]{2,1,0:T(8,128)(2,1)}, u32[]{:S(2)}, u32[]{:S(2)}) %collective-permute-start.27) | collective-permute-done | bytes 1048608 | tf_op jit(solution)/shard_map/ppermute | solution.py:37
  326.6 6.2 convolution_convert_fusion.2
  377.9 13.8 %collective-permute-done.33 = bf16[2,512,512]{2,1,0:T(8,128)(2,1)S(1)} collective-permute-done((bf16[2,512,512]{2,1,0:T(8,128)(2,1)S(1)}, bf16[2,512,512]{2,1,0:T(8,128)(2,1)S(1)}, u32[]{:S(2)}, u32[]{:S(2)}) %collective-permute-start.33) | collective-permute-done | bytes 1048608 | tf_op jit(solution)/shard_map/ppermute | solution.py:37
  401.9 38.2 %attend_back.1 = (f32[2048,512]{1,0:T(8,128)}, f32[2048,512]{1,0:T(8,128)}, bf16[2048,512]{1,0:T(8,128)(2,1)}) custom-call(bf16[2048,512]{1,0:T(8,128)(2,1)} %get-tuple-element.128.queries, bf16[2048,512]{1,0:T(8,128)(2,1)} %get-tuple-element.129.keys, bf16[2048,512]{1,0:T(8,128)(2,1)} %get-tuple-element.130.values, ...), custom_call_target="tpu_custom_call" | custom-call | flops 5368709120 | bytes 18874368 | tf_op jit(solution)/shard_map/attend_back/pallas_call | solution.py:208
  440.1 7.0 %multiply_reduce_fusion.1 = (f32[512]{0:T(512)S(1)}, f32[2048]{0:T(1024)S(1)}, f32[2048]{0:T(1024)S(1)}, f32[512]{0:T(512)S(1)}) fusion(f32[2048,512]{1,0:T(8,128)} %get-tuple-element.140, f32[2048,1536]{1,0:T(8,128)} %copy-done.2, f32[2048]{0:T(1024)S(1)} %get-tuple-element.248, f32[512]{0:T(512)S(1)} %bitcast.283, f32[2048,512]{1,0:T(8,128)} %get-tuple-element.141, ...), kind=kLoop, calls=%fused_computation.32 | loop fusion | flops 12577792 | bytes 16818176 | tf_op jit(solution)/shard_map/reduce_sum | solution.py:666
  466.1 6.5 subtract_convert_fusion.1
  476.5 19.2 %convolution_convert_fusion = bf16[2048,1536]{1,0:T(8,128)(2,1)} fusion(bf16[2048,2048]{1,0:T(8,128)(2,1)} %normed_in_order.1, bf16[2048,512]{1,0:T(8,128)(2,1)} %get-tuple-element.147, bf16[2048,512]{1,0:T(8,128)(2,1)} %get-tuple-element.263, bf16[2048,512]{1,0:T(8,128)(2,1)S(1)} %get-tuple-element.262), kind=kOutput, calls=%fused_computation.10 | convolution fusion | flops 12906921984 | bytes 20971520 | tf_op jit(solution)/shard_map/dot_general | solution.py:33
  511.8 13.3 %back_product.3 = bf16[2,512,2048]{2,1,0:T(8,128)(2,1)} custom-call(bf16[2048,1536]{1,0:T(8,128)(2,1)} %pad_maximum_fusion.1.x, bf16[2048,1536]{1,0:T(8,128)(2,1)} %get-tuple-element.112.w), custom_call_target="tpu_custom_call" | custom-call | bytes 134217728 | tf_op jit(solution)/shard_map/back_product/pallas_call | solution.py:345
  550.7 8.0 %back_product.4 = f32[1,512,2048]{2,1,0:T(8,128)} custom-call(bf16[2048,1536]{1,0:T(8,128)(2,1)} %pad_maximum_fusion.1.x, bf16[2048,1536]{1,0:T(8,128)(2,1)} %get-tuple-element.112.w), custom_call_target="tpu_custom_call" | custom-call | bytes 134217728 | tf_op jit(solution)/shard_map/back_product/pallas_call | solution.py:345
  574.7 8.0 %back_product.5 = f32[1,512,2048]{2,1,0:T(8,128)} custom-call(bf16[2048,1536]{1,0:T(8,128)(2,1)} %pad_maximum_fusion.1.x, bf16[2048,1536]{1,0:T(8,128)(2,1)} %get-tuple-element.112.w), custom_call_target="tpu_custom_call" | custom-call | bytes 134217728 | tf_op jit(solution)/shard_map/back_product/pallas_call | solution.py:345
  606.8 9.6 %collective-permute-done.50 = bf16[256,1664]{1,0:T(8,128)(2,1)S(1)} collective-permute-done((bf16[256,1664]{1,0:T(8,128)(2,1)S(1)}, bf16[256,1664]{1,0:T(8,128)(2,1)S(1)}, u32[]{:S(2)}, u32[]{:S(2)}) %collective-permute-start.50) | collective-permute-done | bytes 852000 | tf_op jit(solution)/shard_map/ppermute | solution.py:237
  632.1 6.2 fusion.13
  638.4 11.5 %collective-permute-done.53 = bf16[256,1664]{1,0:T(8,128)(2,1)} collective-permute-done((bf16[256,1664]{1,0:T(8,128)(2,1)}, bf16[256,1664]{1,0:T(8,128)(2,1)}, u32[]{:S(2)}, u32[]{:S(2)}) %collective-permute-start.53) | collective-permute-done | bytes 852000 | tf_op jit(solution)/shard_map/ppermute | solution.py:37
  651.7 6.3 collective-permute-done.55
  (560 shorter events, 360.2 us)
Async XLA Ops:
  7.2 149.1 %all-gather.4.cloned.1.call-start = ((), (), s32[]{:S(2)}) async-start(), calls=%async_computation.3 | async-start | bytes 2359296 | tf_op jit(solution)/shard_map/all_gather | solution.py:413
  7.2 38.8 %collective-permute-start.8 = (s32[1,512]{1,0:T(1,128)}, s32[1,512]{1,0:T(1,128)S(1)}, u32[]{:S(2)}, u32[]{:S(2)}) collective-permute-start(s32[1,512]{1,0:T(1,128)} %param.20), channel_id=1, source_target_pairs={{0,1},{1,0},{2,3},{3,2},{4,5},{5,4},{6,7},{7,6},{8,9},{9,8},{10,11... | collective-permute-start | bytes 6152 | tf_op jit(solution)/shard_map/ppermute | solution.py:37
  7.8 38.1 %collective-permute-start.9 = (s32[1,512]{1,0:T(1,128)}, s32[1,512]{1,0:T(1,128)S(1)}, u32[]{:S(2)}, u32[]{:S(2)}) collective-permute-start(s32[1,512]{1,0:T(1,128)} %param.20), channel_id=1, source_target_pairs={{0,2},{1,3},{2,0},{3,1},{4,6},{5,7},{6,4},{7,5},{8,10},{9,11},{10,... | collective-permute-start | bytes 6152 | tf_op jit(solution)/shard_map/ppermute | solution.py:37
  22.4 61.5 %collective-permute-start.7 = (bf16[512,2048]{1,0:T(8,128)(2,1)}, bf16[512,2048]{1,0:T(8,128)(2,1)}, u32[]{:S(2)}, u32[]{:S(2)}) collective-permute-start(bf16[512,2048]{1,0:T(8,128)(2,1)} %param.19), channel_id=1, source_target_pairs={{0,2},{1,3},{2,0},{3,1},{4,6},{5,7},{6,4},{7,5},{8,10},{9,11},{10,... | collective-permute-start | bytes 6291464 | tf_op jit(solution)/shard_map/ppermute | solution.py:37
  46.1 40.6 %collective-permute-start = (bf16[512,2048]{1,0:T(8,128)(2,1)S(1)}, bf16[512,2048]{1,0:T(8,128)(2,1)}, u32[]{:S(2)}, u32[]{:S(2)}) collective-permute-start(bf16[512,2048]{1,0:T(8,128)(2,1)S(1)} %copy-done.14), channel_id=1, source_target_pairs={{0,1},{1,0},{2,3},{3,2},{4,5},{5,4},{6,7},{7,6},{8,9},{9,8},{10,11... | collective-permute-start | bytes 6291464 | tf_op jit(solution)/shard_map/ppermute | solution.py:37
  89.8 144.7 %all-gather.6.cloned.1.call-start = ((), (), s32[]{:S(2)}) async-start(), calls=%async_computation.4 | async-start | bytes 4718592 | tf_op jit(solution)/shard_map/all_gather | solution.py:413
  147.6 136.9 %all-gather.8.cloned.1.call-start = ((), (), s32[]{:S(2)}) async-start(), calls=%async_computation.5 | async-start | bytes 2359296 | tf_op jit(solution)/shard_map/all_gather | solution.py:413
  156.3 47.1 %collective-permute-start.19 = (bf16[8,64,2048]{2,1,0:T(8,128)(2,1)}, bf16[8,64,2048]{2,1,0:T(8,128)(2,1)}, u32[]{:S(2)}, u32[]{:S(2)}) collective-permute-start(bf16[8,64,2048]{2,1,0:T(8,128)(2,1)} %bitcast.248), channel_id=1, source_target_pairs={{0,2},{1,3},{2,0},{3,1},{4,6},{5,7},{6,4},{7,5},{8,10},{9,11},{10,... | collective-permute-start | bytes 6291464 | tf_op jit(solution)/shard_map/ppermute | solution.py:37
  157.3 46.1 %collective-permute-start.18 = (bf16[8,64,2048]{2,1,0:T(8,128)(2,1)}, bf16[8,64,2048]{2,1,0:T(8,128)(2,1)}, u32[]{:S(2)}, u32[]{:S(2)}) collective-permute-start(bf16[8,64,2048]{2,1,0:T(8,128)(2,1)} %bitcast.249), channel_id=1, source_target_pairs={{0,1},{1,0},{2,3},{3,2},{4,5},{5,4},{6,7},{7,6},{8,9},{9,8},{10,11... | collective-permute-start | bytes 6291464 | tf_op jit(solution)/shard_map/ppermute | solution.py:37
  209.3 25.3 %collective-permute-start.20 = (bf16[2,512,512]{2,1,0:T(8,128)(2,1)}, bf16[2,512,512]{2,1,0:T(8,128)(2,1)S(1)}, u32[]{:S(2)}, u32[]{:S(2)}) collective-permute-start(bf16[2,512,512]{2,1,0:T(8,128)(2,1)} %bitcast.17), channel_id=1, source_target_pairs={{0,2},{1,3},{2,0},{3,1},{4,6},{5,7},{6,4},{7,5},{8,10},{9,11},{10,... | collective-permute-start | bytes 3145736 | tf_op jit(solution)/shard_map/ppermute | solution.py:37
  235.4 263.5 %reduce-scatter.4.cloned.1.call-start = ((), (), s32[]{:S(2)}) async-start(), calls=%async_computation.6 | async-start | bytes 4718592 | tf_op jit(solution)/shard_map/reduce_scatter | solution.py:417
  253.4 25.5 %collective-permute-start.27 = (bf16[2,128,2048]{2,1,0:T(8,128)(2,1)}, bf16[2,128,2048]{2,1,0:T(8,128)(2,1)}, u32[]{:S(2)}, u32[]{:S(2)}) collective-permute-start(bf16[2,128,2048]{2,1,0:T(8,128)(2,1)} %pad_maximum_fusion.12), channel_id=1, source_target_pairs={{0,2},{1,3},{2,0},{3,1},{4,6},{5,7},{6,4},{7,5},{8,10},{9,11},{10,... | collective-permute-start | bytes 3145736 | tf_op jit(solution)/shard_map/ppermute | solution.py:37
  311.1 24.4 %collective-permute-start.28 = (bf16[2,128,2048]{2,1,0:T(8,128)(2,1)}, bf16[2,128,2048]{2,1,0:T(8,128)(2,1)}, u32[]{:S(2)}, u32[]{:S(2)}) collective-permute-start(bf16[2,128,2048]{2,1,0:T(8,128)(2,1)} %bitcast.42), channel_id=1, source_target_pairs={{0,2},{1,3},{2,0},{3,1},{4,6},{5,7},{6,4},{7,5},{8,10},{9,11},{10,... | collective-permute-start | bytes 3145736 | tf_op jit(solution)/shard_map/ppermute | solution.py:37
  339.2 249.2 %reduce-scatter.6.cloned.1.call-start = ((), (), s32[]{:S(2)}) async-start(), calls=%async_computation.7 | async-start | bytes 2359296 | tf_op jit(solution)/shard_map/reduce_scatter | solution.py:417
  366.1 25.5 %collective-permute-start.33 = (bf16[2,512,512]{2,1,0:T(8,128)(2,1)S(1)}, bf16[2,512,512]{2,1,0:T(8,128)(2,1)S(1)}, u32[]{:S(2)}, u32[]{:S(2)}) collective-permute-start(bf16[2,512,512]{2,1,0:T(8,128)(2,1)S(1)} %pad_maximum_fusion.14), channel_id=1, source_target_pairs={{0,2},{1,3},{2,0},{3,1},{4,6},{5,7},{6,4},{7,5},{8,10},{9,11},{10,... | collective-permute-start | bytes 3145736 | tf_op jit(solution)/shard_map/ppermute | solution.py:37
  394.5 243.9 %reduce-scatter.8.cloned.1.call-start = ((), (), s32[]{:S(2)}) async-start(), calls=%async_computation.8 | async-start | bytes 2359296 | tf_op jit(solution)/shard_map/reduce_scatter | solution.py:417
  397.9 74.7 %collective-permute-start.38 = (bf16[8,64,2048]{2,1,0:T(8,128)(2,1)}, bf16[8,64,2048]{2,1,0:T(8,128)(2,1)}, u32[]{:S(2)}, u32[]{:S(2)}) collective-permute-start(bf16[8,64,2048]{2,1,0:T(8,128)(2,1)} %dynamic-slice_bitcast_fusion), channel_id=1, source_target_pairs={{0,2},{1,3},{2,0},{3,1},{4,6},{5,7},{6,4},{7,5},{8,10},{9,11},{10,... | collective-permute-start | bytes 6291464 | tf_op jit(solution)/shard_map/ppermute | solution.py:37
  464.7 34.2 %collective-permute-start.39 = (bf16[2,128,2048]{2,1,0:T(8,128)(2,1)}, bf16[2,128,2048]{2,1,0:T(8,128)(2,1)}, u32[]{:S(2)}, u32[]{:S(2)}) collective-permute-start(bf16[2,128,2048]{2,1,0:T(8,128)(2,1)} %slice.669), channel_id=1, source_target_pairs={{0,2},{1,3},{2,0},{3,1},{4,6},{5,7},{6,4},{7,5},{8,10},{9,11},{10,... | collective-permute-start | bytes 3145736 | tf_op jit(solution)/shard_map/ppermute | solution.py:37
  499.0 45.2 %collective-permute-start.60 = (bf16[256,1024]{1,0:T(8,128)(2,1)}, bf16[256,1024]{1,0:T(8,128)(2,1)}, u32[]{:S(2)}, u32[]{:S(2)}) collective-permute-start(bf16[256,1024]{1,0:T(8,128)(2,1)} %reduce-scatter.4.cloned.1.call-done), channel_id=1, source_target_pairs={{0,1},{1,0},{2,3},{3,2},{4,5},{5,4},{6,7},{7,6},{8,9},{9,8},{10,11... | collective-permute-start | bytes 1572872 | tf_op jit(solution)/shard_map/ppermute | solution.py:37
  499.1 38.2 %collective-permute-start.58 = (bf16[256,1024]{1,0:T(8,128)(2,1)}, bf16[256,1024]{1,0:T(8,128)(2,1)}, u32[]{:S(2)}, u32[]{:S(2)}) collective-permute-start(bf16[256,1024]{1,0:T(8,128)(2,1)} %reduce-scatter.4.cloned.1.call-done), channel_id=1, source_target_pairs={{0,2},{1,3},{2,0},{3,1},{4,6},{5,7},{6,4},{7,5},{8,10},{9,11},{10,... | collective-permute-start | bytes 1572872 | tf_op jit(solution)/shard_map/ppermute | solution.py:37
  533.1 25.5 %collective-permute-start.44 = (bf16[256,1664]{1,0:T(8,128)(2,1)}, bf16[256,1664]{1,0:T(8,128)(2,1)S(1)}, u32[]{:S(2)}, u32[]{:S(2)}) collective-permute-start(bf16[256,1664]{1,0:T(8,128)(2,1)} %pad_maximum_fusion.15), channel_id=1, source_target_pairs={{8,0},{16,8},{24,16},{28,24},{20,28},{12,20},{4,12},{0,4},{9,1},{1... | collective-permute-start | bytes 2555912 | tf_op jit(solution)/shard_map/ppermute | solution.py:237
  535.4 26.5 %collective-permute-start.43 = (bf16[256,1664]{1,0:T(8,128)(2,1)}, bf16[256,1664]{1,0:T(8,128)(2,1)}, u32[]{:S(2)}, u32[]{:S(2)}) collective-permute-start(bf16[256,1664]{1,0:T(8,128)(2,1)} %fusion.63), channel_id=1, source_target_pairs={{0,8},{8,16},{16,24},{24,28},{28,20},{20,12},{12,4},{4,0},{1,9},{9... | collective-permute-start | bytes 2555912 | tf_op jit(solution)/shard_map/ppermute | solution.py:237
  563.0 29.2 %collective-permute-start.47 = (bf16[256,1664]{1,0:T(8,128)(2,1)}, bf16[256,1664]{1,0:T(8,128)(2,1)}, u32[]{:S(2)}, u32[]{:S(2)}) collective-permute-start(bf16[256,1664]{1,0:T(8,128)(2,1)} %add_convert_fusion.4), channel_id=1, source_target_pairs={{8,0},{16,8},{24,16},{28,24},{20,28},{12,20},{4,12},{0,4},{9,1},{1... | collective-permute-start | bytes 2555912 | tf_op jit(solution)/shard_map/ppermute | solution.py:237
  568.3 25.9 %collective-permute-start.48 = (bf16[256,2048]{1,0:T(8,128)(2,1)}, bf16[256,2048]{1,0:T(8,128)(2,1)S(1)}, u32[]{:S(2)}, u32[]{:S(2)}) collective-permute-start(bf16[256,2048]{1,0:T(8,128)(2,1)} %get-tuple-element.297), channel_id=1, source_target_pairs={{0,2},{1,3},{2,0},{3,1},{4,6},{5,7},{6,4},{7,5},{8,10},{9,11},{10,... | collective-permute-start | bytes 3145736 | tf_op jit(solution)/shard_map/ppermute | solution.py:37
  (153 other events, 1336.2 us)
Sparse Core Ops, SparseCore 0:
  90.0 51.4 all-gather.3
  147.8 72.2 all-gather.5
  235.6 48.5 all-gather.7
  339.3 87.6 reduce-scatter.3
  431.0 67.9 reduce-scatter.5
  503.0 80.8 reduce-scatter.7
